TPU v7x, 32 devices: a whole 2x2x4 slice. The times are simulated.
32 devices in a mesh: dp: 8 (over y, x, core), tensor: 4 (over z).
Axes of the slice: x: 2, y: 2, z: 4, core: 2. Of those that a mesh axis runs over, the one named last changes fastest.
Arguments:
- tokens: bfloat16 [16, 256, 768], P('dp', 'tensor'), may hold values from -6 to 6
- cotangent: bfloat16 [16, 256, 768], P('dp', 'tensor'), may hold values from -6 to 6
- labels: int32 [16], replicated, may hold values from 0 to 999
- timesteps: int32 [16], replicated, may hold values from 0 to 999
- class_table: bfloat16 [1000, 768], replicated, may hold values from -5 to 5
- modulation_weight: bfloat16 [768, 4608], P('dp', 'tensor'), may hold values from -0.21875 to 0.21875
- modulation_bias: float32 [4608], P('tensor'), may hold values from -3 to 3
- attend_weight: bfloat16 [768, 3, 768], P('dp', None, 'tensor'), may hold values from -0.21875 to 0.21875
- attend_bias: float32 [2, 768], P(None, 'tensor'), may hold values from -3 to 3
- output_weight: bfloat16 [768, 768], P('dp', 'tensor'), may hold values from -0.875 to 0.875
- output_bias: float32 [768], replicated, may hold values from -3 to 3
- expand_weight: bfloat16 [768, 3072], P('dp', 'tensor'), may hold values from -0.21875 to 0.21875
- expand_bias: float32 [3072], P('tensor'), may hold values from -3 to 3
- reduce_weight: bfloat16 [768, 3072], P('dp', 'tensor'), may hold values from -0.109375 to 0.109375
- reduce_bias: float32 [768], replicated, may hold values from -3 to 3
Outputs:
- block_output: bfloat16 [16, 256, 768], P('dp', 'tensor')
- tokens_grad: float32 [16, 256, 768], P('dp', 'tensor')
- table_grad: float32 [1000, 768], P(None, 'dp')
- modulation_weight_grad: float32 [768, 4608], P('dp', 'tensor')
- modulation_bias_grad: float32 [4608], P('tensor')
- attend_weight_grad: float32 [768, 3, 768], P('dp', None, 'tensor')
- attend_bias_grad: float32 [2, 768], P(None, 'tensor')
- output_weight_grad: float32 [768, 768], P('dp', 'tensor')
- output_bias_grad: float32 [768], replicated
- expand_weight_grad: float32 [768, 3072], P('dp', 'tensor')
- expand_bias_grad: float32 [3072], P('tensor')
- reduce_weight_grad: float32 [768, 3072], P('dp', 'tensor')
- reduce_bias_grad: float32 [768], replicated
All inputs are finite; a program needn't handle non-finite values.
Results may differ from a plain program's by a relative error of at most 0.02.
The roundings to bfloat16 on the way count: a program that leaves them out, or rounds other values in their place, can miss the bound.
Values may be sent and summed in bfloat16 or wider, within the bound.
No kernel may reach another device: no remote copies, remote signals or barrier semaphores. Data moves between devices by JAX's collectives and lax.ppermute only.
A program may use at most 128 MiB of HBM per device.

v0:
```python
import math

import jax
import jax.numpy as jnp
from jax import lax
from jax.sharding import PartitionSpec as P

HD = 64


norm_eps = 1e-06


def timestep_features(steps_in, model_width):
    halfway = model_width // 2
    frequency = jnp.exp(-math.log(10000.0) * jnp.arange(halfway, dtype=jnp.float32) / halfway)
    angles = steps_in.astype(jnp.float32)[:, None] * frequency[None, :]
    return jnp.concatenate([jnp.cos(angles), jnp.sin(angles)], axis=1)


def condition(label_ids, steps_in, class_table):
    looked = jnp.take(class_table, label_ids, axis=0).astype(jnp.float32)
    return looked + timestep_features(steps_in, class_table.shape[1])


def silu_back(inputs, upstream):
    sigmoid = jax.nn.sigmoid(inputs)
    return upstream * sigmoid * (1.0 + inputs * (1.0 - sigmoid))


def gelu_back(inputs, upstream):
    outputs, pullback = jax.vjp(lambda inner: jax.nn.gelu(inner, approximate=True), inputs)
    return pullback(upstream)[0]


def normalize(inputs):
    centered = inputs - jnp.mean(inputs, axis=-1, keepdims=True)
    inverse = lax.rsqrt(jnp.mean(centered * centered, axis=-1, keepdims=True) + norm_eps)
    return (centered * inverse, inverse)


def norm_back(upstream, normed, inverse):
    return inverse * (
        upstream
        - jnp.mean(upstream, axis=-1, keepdims=True)
        - normed * jnp.mean(upstream * normed, axis=-1, keepdims=True)
    )


def collect(local_rows):
    return lax.all_gather(local_rows, "tensor", axis=1, tiled=True)


def spread(partial_rows):
    return lax.psum_scatter(partial_rows, "tensor", scatter_dimension=1, tiled=True)


def on_device(
    tokens,
    cotangent,
    labels,
    timesteps,
    class_table,
    modulation_weight,
    modulation_bias,
    attend_weight,
    attend_bias,
    output_weight,
    output_bias,
    expand_weight,
    expand_bias,
    reduce_weight,
    reduce_bias,
):
    tensor_count = lax.axis_size("tensor")
    data_index = lax.axis_index("dp")
    tensor_index = lax.axis_index("tensor")
    latent_count = tokens.shape[0]
    model_width = tokens.shape[2]
    row_share = modulation_weight.shape[0]
    head_width = attend_weight.shape[2]
    head_count = head_width // HD
    classes_total = class_table.shape[0]
    score_scale = 1.0 / math.sqrt(HD)
    row_start = data_index * row_share
    zero_index = jnp.zeros((), jnp.int32)
    modulation_full, attend_full, output_full, expand_full, reduce_full = (
        lax.all_gather(modulation_weight, "dp", axis=0, tiled=True),
        lax.all_gather(attend_weight, "dp", axis=0, tiled=True),
        lax.all_gather(output_weight, "dp", axis=0, tiled=True),
        lax.all_gather(expand_weight, "dp", axis=0, tiled=True),
        lax.all_gather(reduce_weight, "dp", axis=0, tiled=True),
    )
    own_labels = lax.dynamic_slice_in_dim(labels, data_index * latent_count, latent_count)
    own_steps = lax.dynamic_slice_in_dim(timesteps, data_index * latent_count, latent_count)
    cond_own = condition(own_labels, own_steps, class_table)
    silu_own = jax.nn.silu(cond_own).astype(jnp.bfloat16)
    modulation_share = jnp.dot(silu_own, modulation_full, preferred_element_type=jnp.float32)
    modulation = lax.all_gather(modulation_share + modulation_bias, "tensor", axis=1, tiled=True)
    pieces = modulation.reshape(latent_count, 6, 1, model_width)
    shift_attend, scale_attend, gate_attend = (pieces[:, 0], pieces[:, 1], pieces[:, 2])
    shift_hidden, scale_hidden, gate_hidden = (pieces[:, 3], pieces[:, 4], pieces[:, 5])
    tokens_wide = tokens.astype(jnp.float32)
    normed_first, inverse_first = normalize(tokens_wide)
    attend_in = (normed_first * (1.0 + scale_attend) + shift_attend).astype(jnp.bfloat16)
    attend_rows = collect(attend_in)
    seq_len = attend_rows.shape[1]
    bias_rows = jnp.stack([attend_bias[0], jnp.zeros_like(attend_bias[0]), attend_bias[1]])
    projected = (
        jnp.einsum("bsd,dje->jbse", attend_rows, attend_full, preferred_element_type=jnp.float32)
        + bias_rows[:, None, None, :]
    ).astype(jnp.bfloat16)
    split_heads = projected.reshape(3, latent_count, seq_len, head_count, HD)
    query_heads, key_heads, value_heads = (split_heads[0], split_heads[1], split_heads[2])
    scores = (
        jnp.einsum("bqhe,bkhe->bhqk", query_heads, key_heads, preferred_element_type=jnp.float32)
        * score_scale
    )
    log_total = jax.nn.logsumexp(scores, axis=-1)
    probs = jnp.exp(scores - log_total[..., None]).astype(jnp.bfloat16)
    mixed = jnp.einsum(
        "bhqk,bkhe->bqhe", probs, value_heads, preferred_element_type=jnp.float32
    ).astype(jnp.bfloat16)
    mixed_rows = mixed.reshape(latent_count, seq_len, head_width)
    attend_out = (
        spread(
            jnp.einsum("bsi,oi->bso", mixed_rows, output_full, preferred_element_type=jnp.float32)
        )
        + output_bias
    )
    residual = tokens_wide + gate_attend * attend_out
    normed_second, inverse_second = normalize(residual)
    hidden_in = (normed_second * (1.0 + scale_hidden) + shift_hidden).astype(jnp.bfloat16)
    hidden_rows = collect(hidden_in)
    pre_act = (
        jnp.einsum("bsd,df->bsf", hidden_rows, expand_full, preferred_element_type=jnp.float32)
        + expand_bias
    )
    activated = jax.nn.gelu(pre_act, approximate=True).astype(jnp.bfloat16)
    hidden_out = (
        spread(
            jnp.einsum("bsf,of->bso", activated, reduce_full, preferred_element_type=jnp.float32)
        )
        + reduce_bias
    )
    block_output = (residual + gate_hidden * hidden_out).astype(jnp.bfloat16)
    upstream = cotangent.astype(jnp.float32)
    grad_gate_hidden = jnp.sum(upstream * hidden_out, axis=1)
    reduce_term = upstream * gate_hidden
    grad_reduce_bias = jnp.sum(reduce_term, axis=(0, 1))
    reduce_rows = collect(reduce_term.astype(jnp.bfloat16))
    grad_act = jnp.einsum(
        "bso,of->bsf", reduce_rows, reduce_full, preferred_element_type=jnp.float32
    )
    grad_reduce = jnp.einsum(
        "bso,bsf->of", reduce_rows, activated, preferred_element_type=jnp.float32
    )
    grad_pre = gelu_back(pre_act, grad_act)
    grad_expand_bias = jnp.sum(grad_pre, axis=(0, 1))
    grad_pre_low = grad_pre.astype(jnp.bfloat16)
    grad_expand = jnp.einsum(
        "bsd,bsf->df", hidden_rows, grad_pre_low, preferred_element_type=jnp.float32
    )
    grad_hidden_in = spread(
        jnp.einsum("bsf,df->bsd", grad_pre_low, expand_full, preferred_element_type=jnp.float32)
    )
    grad_shift_hidden = jnp.sum(grad_hidden_in, axis=1)
    grad_scale_hidden = jnp.sum(grad_hidden_in * normed_second, axis=1)
    grad_residual = upstream + norm_back(
        grad_hidden_in * (1.0 + scale_hidden), normed_second, inverse_second
    )
    grad_gate_attend = jnp.sum(grad_residual * attend_out, axis=1)
    output_term = grad_residual * gate_attend
    grad_output_bias = jnp.sum(output_term, axis=(0, 1))
    output_rows = collect(output_term.astype(jnp.bfloat16))
    grad_output = jnp.einsum(
        "bso,bsi->oi", output_rows, mixed_rows, preferred_element_type=jnp.float32
    )
    grad_mixed = jnp.einsum(
        "bso,oi->bsi", output_rows, output_full, preferred_element_type=jnp.float32
    ).astype(jnp.bfloat16)
    grad_mixed_heads = grad_mixed.reshape(latent_count, seq_len, head_count, HD)
    recomputed = jnp.exp(
        jnp.einsum("bqhe,bkhe->bhqk", query_heads, key_heads, preferred_element_type=jnp.float32)
        * score_scale
        - log_total[..., None]
    )
    row_dot = jnp.einsum(
        "bqhe,bqhe->bhq", grad_mixed_heads, mixed, preferred_element_type=jnp.float32
    )
    grad_probs = jnp.einsum(
        "bqhe,bkhe->bhqk", grad_mixed_heads, value_heads, preferred_element_type=jnp.float32
    )
    grad_logit = (recomputed * (grad_probs - row_dot[..., None])).astype(jnp.bfloat16)
    grad_query = (
        jnp.einsum("bhqk,bkhe->bqhe", grad_logit, key_heads, preferred_element_type=jnp.float32)
        * score_scale
    )
    grad_key = (
        jnp.einsum("bhqk,bqhe->bkhe", grad_logit, query_heads, preferred_element_type=jnp.float32)
        * score_scale
    )
    grad_value = jnp.einsum(
        "bhqk,bqhe->bkhe", probs, grad_mixed_heads, preferred_element_type=jnp.float32
    )
    grad_projected = jnp.stack([grad_query, grad_key, grad_value]).reshape(
        3, latent_count, seq_len, head_width
    )
    grad_attend_bias = jnp.stack(
        [jnp.sum(grad_projected[0], axis=(0, 1)), jnp.sum(grad_projected[2], axis=(0, 1))]
    )
    grad_projected_low = grad_projected.astype(jnp.bfloat16)
    grad_attend = jnp.einsum(
        "bsd,jbse->dje", attend_rows, grad_projected_low, preferred_element_type=jnp.float32
    )
    grad_attend_in = spread(
        jnp.einsum(
            "jbse,dje->bsd", grad_projected_low, attend_full, preferred_element_type=jnp.float32
        )
    )
    grad_shift_attend = jnp.sum(grad_attend_in, axis=1)
    grad_scale_attend = jnp.sum(grad_attend_in * normed_first, axis=1)
    tokens_grad = grad_residual + norm_back(
        grad_attend_in * (1.0 + scale_attend), normed_first, inverse_first
    )
    grad_modulation_rows = jnp.concatenate(
        [
            grad_shift_attend,
            grad_scale_attend,
            grad_gate_attend,
            grad_shift_hidden,
            grad_scale_hidden,
            grad_gate_hidden,
        ],
        axis=1,
    )
    grad_modulation = lax.psum_scatter(
        grad_modulation_rows, "tensor", scatter_dimension=1, tiled=True
    )
    grad_modulation_bias = jnp.sum(grad_modulation, axis=0)
    grad_modulation_low = grad_modulation.astype(jnp.bfloat16)
    grad_modulation_weight = jnp.einsum(
        "ld,lc->dc", silu_own, grad_modulation_low, preferred_element_type=jnp.float32
    )
    grad_modulation_weight, grad_attend, grad_output, grad_expand, grad_reduce = (
        lax.psum_scatter(grad_modulation_weight, "dp", scatter_dimension=0, tiled=True),
        lax.psum_scatter(grad_attend, "dp", scatter_dimension=0, tiled=True),
        lax.psum_scatter(grad_output, "dp", scatter_dimension=0, tiled=True),
        lax.psum_scatter(grad_expand, "dp", scatter_dimension=0, tiled=True),
        lax.psum_scatter(grad_reduce, "dp", scatter_dimension=0, tiled=True),
    )
    grad_silu = jnp.einsum(
        "lc,dc->ld", grad_modulation_low, modulation_full, preferred_element_type=jnp.float32
    )
    grad_cond = silu_back(cond_own, grad_silu)
    shard_rows = lax.all_gather(grad_cond, ("dp", "tensor"), axis=0, tiled=True)
    row_count = shard_rows.shape[0]
    positions = jnp.arange(row_count, dtype=jnp.int32)
    latent_ids = positions // latent_count // tensor_count * latent_count + positions % latent_count
    picked = jnp.take(labels, latent_ids)
    onehot = (picked[:, None] == jnp.arange(classes_total, dtype=jnp.int32)[None, :]).astype(
        jnp.float32
    )
    columns = lax.dynamic_slice_in_dim(shard_rows, row_start, row_share, 1)
    table_grad = jnp.einsum(
        "rc,rd->cd",
        onehot,
        columns,
        precision=lax.Precision.HIGHEST,
        preferred_element_type=jnp.float32,
    )
    expand_share = grad_expand_bias.shape[0]
    modulation_cols = grad_modulation_bias.shape[0]
    padded_attend = lax.dynamic_update_slice(
        jnp.zeros((2, head_width * tensor_count), jnp.float32),
        grad_attend_bias,
        (zero_index, tensor_index * head_width),
    )
    padded_expand = lax.dynamic_update_slice(
        jnp.zeros((expand_share * tensor_count,), jnp.float32),
        grad_expand_bias,
        (tensor_index * expand_share,),
    )
    padded_modulation = lax.dynamic_update_slice(
        jnp.zeros((modulation_cols * tensor_count,), jnp.float32),
        grad_modulation_bias,
        (tensor_index * modulation_cols,),
    )
    summed_attend, summed_expand, summed_modulation, summed_output, summed_reduce = lax.psum(
        (padded_attend, padded_expand, padded_modulation, grad_output_bias, grad_reduce_bias),
        ("dp", "tensor"),
    )
    attend_bias_grad = lax.dynamic_slice_in_dim(
        summed_attend, tensor_index * head_width, head_width, 1
    )
    expand_bias_grad = lax.dynamic_slice_in_dim(
        summed_expand, tensor_index * expand_share, expand_share, 0
    )
    modulation_bias_grad = lax.dynamic_slice_in_dim(
        summed_modulation, tensor_index * modulation_cols, modulation_cols, 0
    )
    return (
        block_output,
        tokens_grad,
        table_grad,
        grad_modulation_weight,
        modulation_bias_grad,
        grad_attend,
        attend_bias_grad,
        grad_output,
        summed_output,
        grad_expand,
        expand_bias_grad,
        grad_reduce,
        summed_reduce,
    )


def solution(mesh):
    placed = (
        P("dp", "tensor", None),
        P("dp", "tensor", None),
        P(),
        P(),
        P(),
        P("dp", "tensor"),
        P("tensor"),
        P("dp", None, "tensor"),
        P(None, "tensor"),
        P("dp", "tensor"),
        P(),
        P("dp", "tensor"),
        P("tensor"),
        P("dp", "tensor"),
        P(),
    )
    return jax.shard_map(
        on_device,
        mesh=mesh,
        in_specs=placed,
        out_specs=(
            P("dp", "tensor", None),
            P("dp", "tensor", None),
            P(None, "dp"),
            P("dp", "tensor"),
            P("tensor"),
            P("dp", None, "tensor"),
            P(None, "tensor"),
            P("dp", "tensor"),
            P(),
            P("dp", "tensor"),
            P("tensor"),
            P("dp", "tensor"),
            P(),
        ),
        check_vma=False,
    )
```

profile of v0, /device:TPU:0, one launch (start us, length us, event | category | flops | bytes accessed | tf_op | source)
XLA Modules:
  0.0 602.2 jit_solution(1955897125939069322)
XLA Ops:
  9.0 14.6 %all_gather.36 = bf16[768,3,192]{2,1,0:T(4,128)(2,1)S(1)} all-gather(bf16[96,3,192]{2,1,0:T(4,128)(2,1)S(1)} %copy.52), channel_id=1, replica_groups=mesh['dp'=8,'tensor'=4] {'dp'}, dimensions={0}, use_global_device_ids=true | all-gather | bytes 995328 | tf_op jit(solution)/shard_map/all_gather | solution.py:89
  23.7 2.1 copy.53
  26.5 10.5 %all_gather.37 = bf16[768,192]{1,0:T(8,128)(2,1)} all-gather(bf16[96,192]{1,0:T(8,128)(2,1)S(1)} %copy-done.25), channel_id=1, replica_groups=mesh['dp'=8,'tensor'=4] {'dp'}, dimensions={0}, use_global_device_ids=true | all-gather | bytes 331776 | tf_op jit(solution)/shard_map/all_gather | solution.py:90
  37.7 2.7 all-gather.5.cloned.1.call-done
  40.4 1.9 convolution_add_fusion
  42.4 13.2 %all_gather.34 = f32[2,4608]{1,0:T(2,128)S(1)} all-gather(f32[2,1152]{1,0:T(2,128)S(1)} %convolution_add_fusion), channel_id=1, replica_groups=mesh['dp'=8,'tensor'=4] {'tensor'}, dimensions={1}, use_global_device_ids=true | all-gather | bytes 46080 | tf_op jit(solution)/shard_map/all_gather | solution.py:99
  55.9 17.8 %all_gather.35 = bf16[2,256,768]{2,1,0:T(8,128)(2,1)S(1)} all-gather(bf16[2,64,768]{2,1,0:T(8,128)(2,1)S(1)} %fusion.33), channel_id=1, replica_groups=mesh['dp'=8,'tensor'=4] {'tensor'}, dimensions={1}, use_global_device_ids=true | all-gather | bytes 983040 | tf_op jit(solution)/shard_map/all_gather | solution.py:51
  76.7 1.6 fusion.43
  80.3 26.6 %all_gather.41 = bf16[2,256,768]{2,1,0:T(8,128)(2,1)} all-gather(bf16[2,64,768]{2,1,0:T(8,128)(2,1)S(1)} %fusion.31), channel_id=1, replica_groups=mesh['dp'=8,'tensor'=4] {'tensor'}, dimensions={1}, use_global_device_ids=true | all-gather | bytes 983040 | tf_op jit(solution)/shard_map/all_gather | solution.py:51
  106.9 14.2 %reduce-scatter.13.cloned.1.call-done = f32[2,64,768]{2,1,0:T(8,128)} async-done(((f32[2,256,768]{2,1,0:T(8,128)}), f32[2,64,768]{2,1,0:T(8,128)}) %reduce-scatter.13.cloned.1.call-update) | async-done | bytes 393232 | tf_op jit(solution)/shard_map/reduce_scatter | solution.py:55
  121.2 1.2 fusion.61
  123.8 18.7 %all_gather.38 = bf16[2,256,768]{2,1,0:T(8,128)(2,1)} all-gather(bf16[2,64,768]{2,1,0:T(8,128)(2,1)S(1)} %add_convert_fusion.1), channel_id=1, replica_groups=mesh['dp'=8,'tensor'=4] {'tensor'}, dimensions={1}, use_global_device_ids=true | all-gather | bytes 983040 | tf_op jit(solution)/shard_map/all_gather | solution.py:51
  142.5 3.7 all-gather.7.cloned.1.call-done
  146.2 3.5 convolution_add_fusion.1
  149.7 22.3 %all-gather.9.cloned.1.call-done = bf16[768,768]{1,0:T(8,128)(2,1)} async-done(((bf16[96,768]{1,0:T(8,128)(2,1)}), bf16[768,768]{1,0:T(8,128)(2,1)}) %all-gather.9.cloned.1.call-update) | async-done | bytes 1179664 | tf_op jit(solution)/shard_map/all_gather | solution.py:92
  172.0 4.2 fusion.68
  177.1 2.0 fusion.14
  179.2 4.0 fusion.12
  183.2 31.4 %reduce-scatter.17.cloned.1.call-done = f32[2,64,768]{2,1,0:T(8,128)} async-done(((f32[2,256,768]{2,1,0:T(8,128)}), f32[2,64,768]{2,1,0:T(8,128)}) %reduce-scatter.17.cloned.1.call-update) | async-done | bytes 393232 | tf_op jit(solution)/shard_map/reduce_scatter | solution.py:55
  214.6 1.9 multiply_reduce_fusion
  217.0 34.0 %reduce-scatter.15.cloned.1.call-done = f32[2,64,768]{2,1,0:T(8,128)} async-done(((f32[2,256,768]{2,1,0:T(8,128)}), f32[2,64,768]{2,1,0:T(8,128)}) %reduce-scatter.15.cloned.1.call-update) | async-done | bytes 393232 | tf_op jit(solution)/shard_map/reduce_scatter | solution.py:55
  251.0 3.0 fusion.30
  254.0 18.3 %all_gather.42 = bf16[2,256,768]{2,1,0:T(8,128)(2,1)S(1)} all-gather(bf16[2,64,768]{2,1,0:T(8,128)(2,1)S(1)} %multiply_convert_fusion.2), channel_id=1, replica_groups=mesh['dp'=8,'tensor'=4] {'tensor'}, dimensions={1}, use_global_device_ids=true | all-gather | bytes 983040 | tf_op jit(solution)/shard_map/all_gather | solution.py:51
  276.2 2.0 convolution_bitcast_fusion.3
  278.3 34.7 %reduce-scatter.19.cloned.1.call-done = f32[2,64,768]{2,1,0:T(8,128)} async-done(((f32[2,256,768]{2,1,0:T(8,128)}), f32[2,64,768]{2,1,0:T(8,128)}) %reduce-scatter.19.cloned.1.call-update) | async-done | bytes 393232 | tf_op jit(solution)/shard_map/reduce_scatter | solution.py:55
  313.0 1.9 fusion.38
  314.9 2.2 copy.82
  318.2 3.4 convolution_bitcast_fusion.2
  321.7 1.2 copy-done.22
  322.9 3.7 convolution_bitcast_fusion.1
  326.7 1.1 copy-done.4
  327.8 1.3 convolution_bitcast_fusion.4
  329.2 3.4 convolution_bitcast_fusion
  332.7 31.6 %reduce-scatter.31.cloned.1.call-done = f32[1152,2]{1,0:T(8,128)} async-done(((f32[4608,2]{1,0:T(8,128)}), f32[1152,2]{1,0:T(8,128)}) %reduce-scatter.31.cloned.1.call-update) | async-done | bytes 9232
  364.3 1.3 copy.83
  365.6 2.5 fusion.52
  370.4 1.3 stack.30
  371.7 1.3 stack.29
  374.3 1.3 dynamic_update_slice.10
  377.0 2.1 fusion.37
  379.1 1.2 fusion.20
  380.3 68.7 %all-gather = f32[32,2,768]{2,1,0:T(2,128)S(1)} all-gather(f32[1,2,768]{2,1,0:T(2,128)S(1)} %fusion.20), channel_id=1, replica_groups=mesh['dp'=8,'tensor'=4] {'dp','tensor'}, dimensions={0}, use_global_device_ids=true | all-gather | bytes 202752 | tf_op jit(solution)/shard_map/all_gather | solution.py:256
  449.1 1.3 bitcast_reduce_fusion
  450.8 38.4 %all-reduce = (f32[4608]{0:T(1024)S(1)}, f32[2,768]{1,0:T(2,128)S(1)}, f32[768]{0:T(1024)}, f32[3072]{0:T(1024)S(1)}, f32[768]{0:T(1024)}) all-reduce(f32[4608]{0:T(1024)S(1)} %dynamic_update_slice.9, f32[2,768]{1,0:T(2,128)} %dynamic_update_slice.10, f32[768]{0:T(1024)S(1)} %copy-done.37, ...), channel_id=1, replica_groups=mesh['dp'=8,'tensor'=4] {'dp','tensor'}, use_global_device_ids=true, to_apply=%region_23.24 | all-reduce | flops 10752 | bytes 86016 | tf_op jit(solution)/shard_map/psum | solution.py:289
  491.2 1.2 fusion.47
  492.4 4.4 reduce-scatter.25.cloned.1.call-done
  496.7 46.3 %reduce-scatter.23.cloned.1.call-done = f32[96,3,192]{2,0,1:T(8,128)} async-done(((f32[768,3,192]{2,0,1:T(8,128)}), f32[96,3,192]{2,0,1:T(8,128)}) %reduce-scatter.23.cloned.1.call-update) | async-done | bytes 221200 | tf_op jit(solution)/shard_map/reduce_scatter | solution.py:247
  543.1 52.6 %reduce-scatter.21.cloned.1.call-done = f32[96,1152]{1,0:T(8,128)} async-done(((f32[768,1152]{1,0:T(8,128)}), f32[96,1152]{1,0:T(8,128)}) %reduce-scatter.21.cloned.1.call-update) | async-done | bytes 442384 | tf_op jit(solution)/shard_map/reduce_scatter | solution.py:246
  (189 shorter events, 24.1 us)
Async XLA Ops:
  7.2 18.7 %copy-start = (bf16[1000,768]{1,0:T(8,128)(2,1)S(1)}, bf16[1000,768]{1,0:T(8,128)(2,1)}, u32[]{:S(2)}) copy-start(bf16[1000,768]{1,0:T(8,128)(2,1)} %param.19) | copy-start | bytes 4608004
  7.2 33.2 %all-gather.5.cloned.1.call-start = ((), (), s32[]{:S(2)}) async-start(), calls=%async_computation.10 | async-start | bytes 1990656 | tf_op jit(solution)/shard_map/all_gather | solution.py:88
  7.9 113.3 %reduce-scatter.13.cloned.1.call-start = ((), (), s32[]{:S(2)}) async-start(), calls=%async_computation.11 | async-start | bytes 1966080 | tf_op jit(solution)/shard_map/reduce_scatter | solution.py:55
  23.7 13.6 %copy-start.7 = (bf16[768,3,192]{2,1,0:T(4,128)(2,1)}, bf16[768,3,192]{2,1,0:T(4,128)(2,1)S(1)}, u32[]{:S(2)}) copy-start(bf16[768,3,192]{2,1,0:T(4,128)(2,1)S(1)} %all_gather.36) | copy-start | bytes 2654212
  23.7 2.1 copy-start.1
  23.7 2.9 copy-start.25
  23.7 13.4 %copy-start.47 = (s32[16]{0:T(128)S(1)}, s32[16]{0:T(128)}, u32[]{:S(2)}) copy-start(s32[16]{0:T(128)} %param.18) | copy-start | bytes 196
  23.7 13.5 %copy-start.5 = (bf16[2,64,768]{2,1,0:T(8,128)(2,1)S(1)}, bf16[2,64,768]{2,1,0:T(8,128)(2,1)}, u32[]{:S(2)}) copy-start(bf16[2,64,768]{2,1,0:T(8,128)(2,1)} %param.15) | copy-start | bytes 589828
  23.7 13.8 %copy-start.44 = (f32[2,192]{1,0:T(2,128)S(1)}, f32[2,192]{1,0:T(2,128)}, u32[]{:S(2)}) copy-start(f32[2,192]{1,0:T(2,128)} %param.23) | copy-start | bytes 4612
  23.7 16.7 %copy-start.41 = (f32[1152]{0:T(1024)S(1)}, f32[1152]{0:T(1024)}, u32[]{:S(2)}) copy-start(f32[1152]{0:T(1024)} %param.21) | copy-start | bytes 13828
  25.9 29.7 %copy-start.42 = (pred[2]{0:T(512)(128)(4,1)}, pred[2]{0:T(512)(128)(4,1)S(1)}, u32[]{:S(2)}) copy-start(pred[2]{0:T(512)(128)(4,1)S(1)} %get-tuple-element.33) | copy-start | bytes 10
  37.3 36.4 %copy-start.29 = (f32[2,64]{1,0:T(2,128)}, f32[2,64]{1,0:T(2,128)S(1)}, u32[]{:S(2)}) copy-start(f32[2,64]{1,0:T(2,128)S(1)} %broadcast_multiply_fusion.5) | copy-start | bytes 1540
  37.5 36.2 %copy-start.38 = (f32[2,64]{1,0:T(2,128)}, f32[2,64]{1,0:T(2,128)S(1)}, u32[]{:S(2)}) copy-start(f32[2,64]{1,0:T(2,128)S(1)} %add_rsqrt_fusion.1) | copy-start | bytes 1540
  37.7 4.6 copy-start.26
  40.4 33.2 %copy-start.20 = (bf16[768,3,192]{0,2,1:T(8,128)(2,1)S(1)}, bf16[768,3,192]{0,2,1:T(8,128)(2,1)}, u32[]{:S(2)}) copy-start(bf16[768,3,192]{0,2,1:T(8,128)(2,1)} %copy.53) | copy-start | bytes 2654212
  76.7 3.0 copy-start.24
  78.3 67.9 %all-gather.7.cloned.1.call-start = ((), (), s32[]{:S(2)}) async-start(), calls=%async_computation.12 | async-start | bytes 1327104 | tf_op jit(solution)/shard_map/all_gather | solution.py:91
  79.0 93.0 %all-gather.9.cloned.1.call-start = ((), (), s32[]{:S(2)}) async-start(), calls=%async_computation.13 | async-start | bytes 1327104 | tf_op jit(solution)/shard_map/all_gather | solution.py:92
  79.6 135.0 %reduce-scatter.17.cloned.1.call-start = ((), (), s32[]{:S(2)}) async-start(), calls=%async_computation.15 | async-start | bytes 1966080 | tf_op jit(solution)/shard_map/reduce_scatter | solution.py:55
  172.0 5.1 copy-start.46
  179.1 71.9 %reduce-scatter.15.cloned.1.call-start = ((), (), s32[]{:S(2)}) async-start(), calls=%async_computation.14 | async-start | bytes 1966080 | tf_op jit(solution)/shard_map/reduce_scatter | solution.py:55
  183.2 129.8 %reduce-scatter.19.cloned.1.call-start = ((), (), s32[]{:S(2)}) async-start(), calls=%async_computation.16 | async-start | bytes 1966080 | tf_op jit(solution)/shard_map/reduce_scatter | solution.py:55
  251.0 21.3 %copy-start.11 = (bf16[768,192]{1,0:T(8,128)(2,1)S(1)}, bf16[768,192]{1,0:T(8,128)(2,1)}, u32[]{:S(2)}) copy-start(bf16[768,192]{1,0:T(8,128)(2,1)} %all_gather.37) | copy-start | bytes 884740
  254.0 19.9 %copy-start.9 = (f32[2,64,768]{2,1,0:T(8,128)}, f32[2,64,768]{2,1,0:T(8,128)S(1)}, u32[]{:S(2)}) copy-start(f32[2,64,768]{2,1,0:T(8,128)S(1)} %get-tuple-element.41) | copy-start | bytes 1179652
  272.4 1.5 copy-start.3
  272.4 1.5 copy-start.13
  272.4 1.6 copy-start.19
  274.8 1.4 copy-start.8
  278.2 34.8 %copy-start.6 = (bf16[2,64,768]{2,1,0:T(8,128)(2,1)S(1)}, bf16[2,64,768]{2,1,0:T(8,128)(2,1)}, u32[]{:S(2)}) copy-start(bf16[2,64,768]{2,1,0:T(8,128)(2,1)} %param.15) | copy-start | bytes 589828
  278.2 34.8 %copy-start.30 = (f32[2,64]{1,0:T(2,128)S(1)}, f32[2,64]{1,0:T(2,128)}, u32[]{:S(2)}) copy-start(f32[2,64]{1,0:T(2,128)} %copy-done.29) | copy-start | bytes 1540
  278.2 34.8 %copy-start.39 = (f32[2,64]{1,0:T(2,128)S(1)}, f32[2,64]{1,0:T(2,128)}, u32[]{:S(2)}) copy-start(f32[2,64]{1,0:T(2,128)} %copy-done.38) | copy-start | bytes 1540
  278.2 36.7 %copy-start.34 = (f32[2,768]{1,0:T(2,128)S(1)}, f32[2,768]{1,0:T(2,128)}, u32[]{:S(2)}) copy-start(f32[2,768]{1,0:T(2,128)} %get-tuple-element.39) | copy-start | bytes 18436
  278.2 36.7 %copy-start.32 = (f32[2,768]{1,0:T(2,128)S(1)}, f32[2,768]{1,0:T(2,128)}, u32[]{:S(2)}) copy-start(f32[2,768]{1,0:T(2,128)} %get-tuple-element.21) | copy-start | bytes 18436
  278.2 36.7 %copy-start.31 = (f32[2,768]{1,0:T(2,128)S(1)}, f32[2,768]{1,0:T(2,128)}, u32[]{:S(2)}) copy-start(f32[2,768]{1,0:T(2,128)} %get-tuple-element.13) | copy-start | bytes 18436
  278.2 36.7 %copy-start.33 = (f32[2,768]{1,0:T(2,128)S(1)}, f32[2,768]{1,0:T(2,128)}, u32[]{:S(2)}) copy-start(f32[2,768]{1,0:T(2,128)} %get-tuple-element.24) | copy-start | bytes 18436
  278.3 86.0 %reduce-scatter.31.cloned.1.call-start = ((), (), s32[]{:S(2)}) async-start(), calls=%async_computation.22 | async-start | bytes 2949120
  317.1 175.3 %reduce-scatter.27.cloned.1.call-start = ((), (), s32[]{:S(2)}) async-start(), calls=%async_computation.20 | async-start | bytes 2654208 | tf_op jit(solution)/shard_map/reduce_scatter | solution.py:249
  321.6 170.8 %reduce-scatter.29.cloned.1.call-start = ((), (), s32[]{:S(2)}) async-start(), calls=%async_computation.21 | async-start | bytes 2654208 | tf_op jit(solution)/shard_map/reduce_scatter | solution.py:250
  326.7 170.1 %reduce-scatter.25.cloned.1.call-start = ((), (), s32[]{:S(2)}) async-start(), calls=%async_computation.19 | async-start | bytes 884736 | tf_op jit(solution)/shard_map/reduce_scatter | solution.py:248
  329.1 213.9 %reduce-scatter.23.cloned.1.call-start = ((), (), s32[]{:S(2)}) async-start(), calls=%async_computation.18 | async-start | bytes 2654208 | tf_op jit(solution)/shard_map/reduce_scatter | solution.py:247
  332.6 32.9 %copy-start.27 = (f32[2,384]{1,0:T(2,128)S(1)}, f32[2,384]{1,0:T(2,128)}, u32[]{:S(2)}) copy-start(f32[2,384]{1,0:T(2,128)} %copy-done.26) | copy-start | bytes 9220
  332.6 32.9 %copy-start.43 = (pred[2]{0:T(512)(128)(4,1)S(1)}, pred[2]{0:T(512)(128)(4,1)}, u32[]{:S(2)}) copy-start(pred[2]{0:T(512)(128)(4,1)} %copy-done.42) | copy-start | bytes 10
  332.6 263.0 %reduce-scatter.21.cloned.1.call-start = ((), (), s32[]{:S(2)}) async-start(), calls=%async_computation.17 | async-start | bytes 3981312 | tf_op jit(solution)/shard_map/reduce_scatter | solution.py:246
  368.1 8.9 %copy-start.40 = (f32[2,64]{1,0:T(2,128)S(1)}, f32[2,64]{1,0:T(2,128)}, u32[]{:S(2)}) copy-start(f32[2,64]{1,0:T(2,128)} %copy-done.38) | copy-start | bytes 1540
  368.1 10.9 %copy-start.2 = (bf16[768,1152]{1,0:T(8,128)(2,1)S(1)}, bf16[768,1152]{1,0:T(8,128)(2,1)}, u32[]{:S(2)}) copy-start(bf16[768,1152]{1,0:T(8,128)(2,1)} %all-gather.5.cloned.1.call-done) | copy-start | bytes 5308420
  379.1 71.7 %copy-start.36 = (f32[768]{0:T(1024)S(1)}, f32[768]{0:T(1024)}, u32[]{:S(2)}) copy-start(f32[768]{0:T(1024)} %get-tuple-element.23) | copy-start | bytes 9220
  379.1 71.7 %copy-start.37 = (f32[768]{0:T(1024)S(1)}, f32[768]{0:T(1024)}, u32[]{:S(2)}) copy-start(f32[768]{0:T(1024)} %get-tuple-element.40) | copy-start | bytes 9220
  379.1 112.1 %copy-start.45 = (s32[64]{0:T(128)S(1)}, s32[64]{0:T(128)}, u32[]{:S(2)}) copy-start(s32[64]{0:T(128)} %and_select_fusion.3) | copy-start | bytes 772
  (14 other events, 13.7 us)
Sparse Core Ops, SparseCore 0:
  9.9 30.4 all-gather.4
  78.4 42.7 reduce-scatter.12
  123.1 23.0 all-gather.6
  147.9 24.0 all-gather.8
  179.2 35.2 reduce-scatter.16
  216.7 34.2 reduce-scatter.14
  278.4 34.5 reduce-scatter.18
  317.2 46.9 reduce-scatter.30
  368.2 42.1 reduce-scatter.26
  414.5 42.8 reduce-scatter.28
  461.2 35.5 reduce-scatter.24
  500.5 42.5 reduce-scatter.22
  547.5 48.0 reduce-scatter.20
where the time goes:
time: 603 us; the launch traced here: 602 us
  waiting for transfers between devices  280 us (46%)
  blocking collectives  227 us (38%)
  matrix products  40.7 us (7%)
  local copies, waits for them, and re-layouts  23 us (4%)
  other arithmetic  16.8 us (3%)
  between operations  14.4 us (2%)
    reduce_scatter x4, waiting for transfers between devices, spread(): lax.psum_scatter(partial_rows, 'tensor', scatter_dimension=1, tiled=True)  114 us
    all_gather x4, blocking collectives, collect(): return lax.all_gather(local_rows, 'tensor', axis=1, tiled=True)  81.4 us
    all_gather x1, blocking collectives, on_device(): shard_rows = lax.all_gather(grad_cond, ('dp', 'tensor'), axis=0, tiled=True)  68.7 us
    reduce_scatter x1, waiting for transfers between devices, on_device(): lax.psum_scatter(grad_modulation_weight, 'dp', scatter_dimension=0, tiled...  52.6 us
    reduce_scatter x1, waiting for transfers between devices, on_device(): lax.psum_scatter(grad_attend, 'dp', scatter_dimension=0, tiled=True)  46.3 us
    psum x1, blocking collectives, on_device(): lax.psum((padded_attend, padded_expand, padded_modulation, grad_output_bi...  38.4 us
    unnamed x14, waiting for transfers between devices  33.6 us
    all_gather x1, waiting for transfers between devices, on_device(): lax.all_gather(reduce_weight, 'dp', axis=0, tiled=True)  22.3 us
  transfers between devices with their start and end apart: 13, of which 11 were waited for; matrix products, arithmetic and copies ran while one was open for 8% of the time, Pallas kernels for 0%

commit v1 on v0

--- a/solution.py
+++ b/solution.py
@@ -316,7 +316,374 @@
     )
 
 
+def swap(values, axis, mask):
+    count = lax.axis_size(axis)
+    return lax.ppermute(values, axis, [(place, place ^ mask) for place in range(count)])
+
+
+def unxor(parts, own):
+    bit = 1
+    while bit < len(parts):
+        odd = (own & bit) != 0
+        parts = [jnp.where(odd, parts[r ^ bit], parts[r]) for r in range(len(parts))]
+        bit *= 2
+    return parts
+
+
+def pick(values, place):
+    return lax.dynamic_index_in_dim(values, place, 0, keepdims=False)
+
+
+def spread_pairs(partial):
+    both = partial[0] + swap(partial[1], "dp", 1)
+    rows = both.shape[0] // 2
+    return both[:rows] + swap(both[rows:].astype(jnp.bfloat16), "tensor", 1).astype(jnp.float32)
+
+
+def collect_pairs(rows):
+    near = swap(rows, "tensor", 1)
+    return jnp.concatenate([rows, near, swap(rows, "dp", 1), swap(near, "dp", 1)], axis=0)
+
+
+def gather_weight(shard, is_own, core, chip):
+    far = swap(shard, "tensor", 2)
+    mine = jnp.where(is_own, shard, far)
+    other = swap(jnp.where(is_own, far, shard), "dp", 1)
+    first = core == 0
+    share = jnp.concatenate(
+        [jnp.where(first, mine, other), jnp.where(first, other, mine)], axis=0
+    )
+    shares = [share] + [swap(share, "dp", 2 * r) for r in (1, 2, 3)]
+    return shares
+
+
+def in_order(shares, chip, start, stop):
+    return jnp.concatenate(unxor([s[:, start:stop] for s in shares], chip), axis=0)
+
+
+def scatter_weight(partial, is_own, core, chip):
+    blocks = partial.reshape(4, -1, partial.shape[1])
+    total = pick(blocks, chip)
+    for r in (1, 2, 3):
+        sent = pick(blocks, chip ^ r).astype(jnp.bfloat16)
+        total = total + swap(sent, "dp", 2 * r).astype(jnp.float32)
+    halves = total.reshape(2, -1, total.shape[1])
+    mine = pick(halves, core)
+    other = swap(pick(halves, 1 - core), "dp", 1)
+    kept = jnp.where(is_own, mine, other)
+    sent = jnp.where(is_own, other, mine).astype(jnp.bfloat16)
+    return kept + swap(sent, "tensor", 2).astype(jnp.float32)
+
+
+def on_paired_device(
+    tokens,
+    cotangent,
+    labels,
+    timesteps,
+    class_table,
+    modulation_weight,
+    modulation_bias,
+    attend_weight,
+    attend_bias,
+    output_weight,
+    output_bias,
+    expand_weight,
+    expand_bias,
+    reduce_weight,
+    reduce_bias,
+):
+    data_index = lax.axis_index("dp")
+    tensor_index = lax.axis_index("tensor")
+    core, chip = data_index & 1, data_index >> 1
+    half = tensor_index >> 1
+    is_own = half == core
+    model_width = tokens.shape[2]
+    row_share = modulation_weight.shape[0]
+    head_width = attend_weight.shape[2]
+    head_count = head_width // HD
+    ff_width = expand_weight.shape[1]
+    mod_width = modulation_weight.shape[1]
+    latent_total = labels.shape[0]
+    classes_total = class_table.shape[0]
+    score_scale = 1.0 / math.sqrt(HD)
+
+    slot = jnp.arange(latent_total, dtype=jnp.int32)
+    latent_ids = ((slot >> 1) ^ data_index) * 2 + (slot & 1)
+    chosen = latent_ids[:, None] == slot[None, :]
+    labels_rel = jnp.sum(jnp.where(chosen, labels[None, :], 0), axis=1)
+    steps_rel = jnp.sum(jnp.where(chosen, timesteps[None, :], 0), axis=1)
+    looked = lax.dynamic_slice_in_dim(
+        jnp.take(class_table, labels_rel, axis=0), data_index * row_share, row_share, 1
+    ).astype(jnp.float32)
+    halfway = model_width // 2
+    column = data_index * row_share + jnp.arange(row_share, dtype=jnp.int32)
+    is_cos = column < halfway
+    place = jnp.where(is_cos, column, column - halfway).astype(jnp.float32)
+    frequency = jnp.exp(-math.log(10000.0) * place / halfway)
+    angles = steps_rel.astype(jnp.float32)[:, None] * frequency[None, :]
+    cond = looked + jnp.where(is_cos[None, :], jnp.cos(angles), jnp.sin(angles))
+    silu_act = jax.nn.silu(cond).astype(jnp.bfloat16)
+    partial = jnp.dot(silu_act, modulation_weight, preferred_element_type=jnp.float32)
+    partial = partial.reshape(8, 2, mod_width)
+    partial = partial[:4] + swap(partial[4:], "dp", 4)
+    partial = partial[:2] + swap(partial[2:], "dp", 2)
+    crossed = swap(partial, "dp", 1)
+    mod_cols = jnp.stack([partial[0] + crossed[1], partial[1] + crossed[0]]) + modulation_bias
+    mod_parts = [mod_cols] + [swap(mod_cols, "tensor", r) for r in (1, 2, 3)]
+    mod_full = jnp.concatenate(
+        unxor([jnp.where(half == 0, m[:, 0], m[:, 1]) for m in mod_parts], tensor_index), axis=1
+    )
+    pieces = mod_full.reshape(2, 6, 1, model_width)
+    own_pieces = pieces[0]
+
+    paired = jnp.stack([tokens, cotangent], axis=1)
+    kept, sent = pick(paired, half), pick(paired, 1 - half)
+    own_pair = jnp.concatenate([kept, swap(sent, "tensor", 2)], axis=1)
+    line = jnp.concatenate([own_pair, swap(own_pair, "tensor", 1)], axis=1)
+    across = swap(line, "dp", 1)
+    tokens_all = jnp.stack([line[0], across[0]]).astype(jnp.float32)
+    upstream_all = jnp.stack([line[1], across[1]]).astype(jnp.float32)
+    tokens_own = own_pair[0].astype(jnp.float32)
+    upstream = own_pair[1].astype(jnp.float32)
+
+    attn_shares = gather_weight(
+        jnp.concatenate([attend_weight.reshape(row_share, -1), output_weight], axis=1),
+        is_own,
+        core,
+        chip,
+    )
+    attend_full = in_order(attn_shares, chip, 0, 3 * head_width)
+    output_full = in_order(attn_shares, chip, 3 * head_width, 4 * head_width)
+    ff_shares = gather_weight(
+        jnp.concatenate([expand_weight, reduce_weight], axis=1), is_own, core, chip
+    )
+    expand_full = in_order(ff_shares, chip, 0, ff_width)
+    reduce_full = in_order(ff_shares, chip, ff_width, 2 * ff_width)
+    bias_vec = jnp.concatenate([attend_bias.reshape(-1), expand_bias])
+    bias_vec = jnp.where(is_own, bias_vec, swap(bias_vec, "tensor", 2))
+    query_bias = bias_vec[:head_width]
+    value_bias = bias_vec[head_width : 2 * head_width]
+    expand_bias_q = bias_vec[2 * head_width :]
+
+    normed_all, _ = normalize(tokens_all)
+    attend_rows = (normed_all * (1.0 + pieces[:, 1]) + pieces[:, 0]).astype(jnp.bfloat16)
+    seq_len = attend_rows.shape[1]
+    bias_rows = jnp.concatenate([query_bias, jnp.zeros_like(query_bias), value_bias])
+    projected = (
+        jnp.einsum("bsd,de->bse", attend_rows, attend_full, preferred_element_type=jnp.float32)
+        + bias_rows
+    ).astype(jnp.bfloat16)
+    split_heads = projected.reshape(2, seq_len, 3, head_count, HD)
+    query_heads, key_heads, value_heads = (
+        split_heads[:, :, 0],
+        split_heads[:, :, 1],
+        split_heads[:, :, 2],
+    )
+    scores = (
+        jnp.einsum("bqhe,bkhe->bhqk", query_heads, key_heads, preferred_element_type=jnp.float32)
+        * score_scale
+    )
+    log_total = jax.nn.logsumexp(scores, axis=-1)
+    prob_wide = jnp.exp(scores - log_total[..., None])
+    probs = prob_wide.astype(jnp.bfloat16)
+    mixed = jnp.einsum(
+        "bhqk,bkhe->bqhe", probs, value_heads, preferred_element_type=jnp.float32
+    ).astype(jnp.bfloat16)
+    mixed_rows = mixed.reshape(2, seq_len, head_width)
+    attend_out = (
+        spread_pairs(
+            jnp.einsum("bsi,oi->bso", mixed_rows, output_full, preferred_element_type=jnp.float32)
+        )
+        + output_bias
+    )
+    normed_first, inverse_first = normalize(tokens_own)
+    residual = tokens_own + own_pieces[2] * attend_out
+    normed_second, inverse_second = normalize(residual)
+    hidden_in = (normed_second * (1.0 + own_pieces[4]) + own_pieces[3]).astype(jnp.bfloat16)
+    hidden_rows = collect_pairs(hidden_in)
+
+    pre_act = (
+        jnp.dot(hidden_rows, expand_full, preferred_element_type=jnp.float32) + expand_bias_q
+    )
+    activated = jax.nn.gelu(pre_act, approximate=True).astype(jnp.bfloat16)
+    reduce_term = upstream_all * pieces[:, 5]
+    reduce_rows = reduce_term.astype(jnp.bfloat16).reshape(-1, model_width)
+    blocks = jnp.sum(reduce_term.reshape(4, -1, model_width), axis=1)
+    grad_reduce_bias = (blocks[0] + blocks[1]) + (blocks[2] + blocks[3])
+    grad_act = jnp.dot(reduce_rows, reduce_full, preferred_element_type=jnp.float32)
+    grad_pre = gelu_back(pre_act, grad_act)
+    grad_expand_bias = jnp.sum(grad_pre, axis=0)
+    grad_pre_low = grad_pre.astype(jnp.bfloat16)
+    grad_hidden_in = spread_pairs(
+        jnp.einsum(
+            "sf,df->sd", grad_pre_low, expand_full, preferred_element_type=jnp.float32
+        ).reshape(2, seq_len, model_width)
+    )
+    hidden_out = (
+        spread_pairs(
+            jnp.einsum(
+                "sf,of->so", activated, reduce_full, preferred_element_type=jnp.float32
+            ).reshape(2, seq_len, model_width)
+        )
+        + reduce_bias
+    )
+    block_own = (residual + own_pieces[5] * hidden_out).astype(jnp.bfloat16)
+    grad_gate_hidden = jnp.sum(upstream * hidden_out, axis=0)
+    grad_reduce = jnp.einsum(
+        "so,sf->of", reduce_rows, activated, preferred_element_type=jnp.float32
+    )
+    grad_expand = jnp.einsum(
+        "sd,sf->df", hidden_rows, grad_pre_low, preferred_element_type=jnp.float32
+    )
+
+    grad_shift_hidden = jnp.sum(grad_hidden_in, axis=0)
+    grad_scale_hidden = jnp.sum(grad_hidden_in * normed_second, axis=0)
+    grad_residual = upstream + norm_back(
+        grad_hidden_in * (1.0 + own_pieces[4]), normed_second, inverse_second
+    )
+    grad_gate_attend = jnp.sum(grad_residual * attend_out, axis=0)
+    output_term = grad_residual * own_pieces[2]
+    grad_output_bias = jnp.sum(output_term, axis=0)
+    output_rows = collect_pairs(output_term.astype(jnp.bfloat16)).reshape(2, seq_len, model_width)
+
+    grad_mixed = jnp.einsum(
+        "bso,oi->bsi", output_rows, output_full, preferred_element_type=jnp.float32
+    ).astype(jnp.bfloat16)
+    grad_mixed_heads = grad_mixed.reshape(2, seq_len, head_count, HD)
+    row_dot = jnp.einsum(
+        "bqhe,bqhe->bhq", grad_mixed_heads, mixed, preferred_element_type=jnp.float32
+    )
+    grad_probs = jnp.einsum(
+        "bqhe,bkhe->bhqk", grad_mixed_heads, value_heads, preferred_element_type=jnp.float32
+    )
+    grad_logit = (prob_wide * (grad_probs - row_dot[..., None])).astype(jnp.bfloat16)
+    grad_query = (
+        jnp.einsum("bhqk,bkhe->bqhe", grad_logit, key_heads, preferred_element_type=jnp.float32)
+        * score_scale
+    )
+    grad_key = (
+        jnp.einsum("bhqk,bqhe->bkhe", grad_logit, query_heads, preferred_element_type=jnp.float32)
+        * score_scale
+    )
+    grad_value = jnp.einsum(
+        "bhqk,bqhe->bkhe", probs, grad_mixed_heads, preferred_element_type=jnp.float32
+    )
+    grad_projected = jnp.concatenate(
+        [g.reshape(2, seq_len, head_width) for g in (grad_query, grad_key, grad_value)], axis=2
+    )
+    summed_projected = jnp.sum(grad_projected, axis=(0, 1))
+    grad_projected_low = grad_projected.astype(jnp.bfloat16)
+    grad_attend_in = spread_pairs(
+        jnp.einsum(
+            "bse,de->bsd", grad_projected_low, attend_full, preferred_element_type=jnp.float32
+        )
+    )
+    grad_attend = jnp.einsum(
+        "bsd,bse->de", attend_rows, grad_projected_low, preferred_element_type=jnp.float32
+    )
+    grad_output = jnp.einsum(
+        "bso,bsi->oi", output_rows, mixed_rows, preferred_element_type=jnp.float32
+    )
+    grad_shift_attend = jnp.sum(grad_attend_in, axis=0)
+    grad_scale_attend = jnp.sum(grad_attend_in * normed_first, axis=0)
+    tokens_grad_own = grad_residual + norm_back(
+        grad_attend_in * (1.0 + own_pieces[1]), normed_first, inverse_first
+    )
+
+    ff_grad = scatter_weight(
+        jnp.concatenate([grad_expand, grad_reduce], axis=1), is_own, core, chip
+    )
+    attn_grad = scatter_weight(
+        jnp.concatenate([grad_attend, grad_output], axis=1), is_own, core, chip
+    )
+
+    def back(rows):
+        count = rows.shape[0] // 2
+        own, far = rows[:count], swap(rows[count:], "tensor", 2)
+        return jnp.where(half == 0, jnp.stack([own, far]), jnp.stack([far, own]))
+
+    block_output = back(block_own)
+    tokens_grad = back(tokens_grad_own)
+
+    grad_rows = jnp.concatenate(
+        [
+            grad_shift_attend,
+            grad_scale_attend,
+            grad_gate_attend,
+            grad_shift_hidden,
+            grad_scale_hidden,
+            grad_gate_hidden,
+        ]
+    ).reshape(4, mod_width)
+    here = pick(grad_rows, tensor_index) + swap(pick(grad_rows, tensor_index ^ 1), "tensor", 1)
+    there = swap(pick(grad_rows, tensor_index ^ 2), "tensor", 2) + swap(
+        pick(grad_rows, tensor_index ^ 3), "tensor", 3
+    )
+    grad_mod = jnp.where(half == 0, jnp.stack([here, there]), jnp.stack([there, here]))
+    for mask in (1, 2, 4):
+        grad_mod = jnp.concatenate([grad_mod, swap(grad_mod, "dp", mask)], axis=0)
+    bias_sum = grad_mod
+    while bias_sum.shape[0] > 1:
+        bias_sum = bias_sum.reshape(-1, 2, mod_width)
+        bias_sum = bias_sum[:, 0] + bias_sum[:, 1]
+    modulation_bias_grad = bias_sum[0]
+    grad_mod_low = grad_mod.astype(jnp.bfloat16)
+    modulation_weight_grad = jnp.einsum(
+        "ld,lc->dc", silu_act, grad_mod_low, preferred_element_type=jnp.float32
+    )
+    grad_silu = jnp.einsum(
+        "lc,dc->ld", grad_mod_low, modulation_weight, preferred_element_type=jnp.float32
+    )
+    near = grad_silu + swap(grad_silu, "tensor", 1)
+    grad_silu = near + swap(near, "tensor", 2)
+    grad_cond = silu_back(cond, grad_silu)
+    onehot = (
+        labels_rel[:, None] == jnp.arange(classes_total, dtype=jnp.int32)[None, :]
+    ).astype(jnp.float32)
+    table_grad = jnp.einsum(
+        "rc,rd->cd",
+        onehot,
+        grad_cond,
+        precision=lax.Precision.HIGHEST,
+        preferred_element_type=jnp.float32,
+    )
+
+    grad_output_bias = grad_output_bias + swap(grad_output_bias, "dp", 1)
+    grad_output_bias = grad_output_bias + swap(grad_output_bias, "tensor", 1)
+    sums = jnp.concatenate(
+        [
+            grad_output_bias,
+            grad_reduce_bias,
+            grad_expand_bias,
+            summed_projected[:head_width],
+            summed_projected[2 * head_width :],
+        ]
+    )
+    sums = sums + swap(sums, "dp", 2)
+    sums = sums + swap(sums, "dp", 4)
+    sums = sums + swap(sums, "tensor", 2)
+    split = sums[2 * model_width :]
+    split = jnp.where(is_own, split, swap(split, "dp", 1))
+    return (
+        block_output,
+        tokens_grad,
+        table_grad,
+        modulation_weight_grad,
+        modulation_bias_grad,
+        attn_grad[:, : 3 * head_width].reshape(row_share, 3, head_width),
+        split[ff_width:].reshape(2, head_width),
+        attn_grad[:, 3 * head_width :],
+        sums[:model_width],
+        ff_grad[:, :ff_width],
+        split[:ff_width],
+        ff_grad[:, ff_width:],
+        sums[model_width : 2 * model_width],
+    )
+
+
 def solution(mesh):
+    paired = mesh.shape["dp"] == 8 and mesh.shape["tensor"] == 4
+    per_device = on_paired_device if paired else on_device
     placed = (
         P("dp", "tensor", None),
         P("dp", "tensor", None),
@@ -335,7 +702,7 @@
         P(),
     )
     return jax.shard_map(
-        on_device,
+        per_device,
         mesh=mesh,
         in_specs=placed,
         out_specs=(

time: 603 us -> 259 us (0.43)
  blocking collectives: 227 us -> 0 us
  waiting for transfers between devices: 280 us -> 126 us
  starting transfers between devices: 0.53 us -> 61.6 us
  matrix products: 40.7 us -> 17.8 us
  between operations: 14.4 us -> 2.54 us
  local copies, waits for them, and re-layouts: 23 us -> 29.8 us
    reduce_scatter x9 -> x0, waiting for transfers between devices: 217 us -> none  [the longest x4 114 us: spread(): lax.psum_scatter(partial_rows, 'tensor', scatter_dimension=1, tiled=True)]
    all_gather x8 -> x0, blocking collectives: 188 us -> none  [the longest x4 81.4 us: collect(): return lax.all_gather(local_rows, 'tensor', axis=1, tiled=True)]
    ppermute x0 -> x60, waiting for transfers between devices: none -> 126 us  [swap(): lax.ppermute(values, axis, [(place, place ^ mask) for place in range(coun...]
    ppermute x0 -> x60, starting transfers between devices: none -> 61.6 us  [swap(): lax.ppermute(values, axis, [(place, place ^ mask) for place in range(coun...]
    psum x1 -> x0, blocking collectives: 38.4 us -> none  [on_device(): lax.psum((padded_attend, padded_expand, padded_modulation, grad_output_bi...]
    unnamed x14 -> x0, waiting for transfers between devices: 33.6 us -> none
    all_gather x3 -> x0, waiting for transfers between devices: 28.7 us -> none  [the longest x1 22.3 us: on_device(): lax.all_gather(reduce_weight, 'dp', axis=0, tiled=True)]
    dot_general x22, matrix products: 40.7 us -> 17.8 us  [the longest x1 2.12 us: on_paired_device(): jnp.einsum('bsd,bse->de', attend_rows, grad_projected_low, preferred_elem...]
  transfers between devices with their start and end apart: 13 -> 60, of which waited for: 11 -> 32; matrix products, arithmetic and copies ran while one was open for 8% -> 17% of each run, Pallas kernels for 0% -> 0%
where the time goes in v1:
time: 259 us
  waiting for transfers between devices  126 us (49%)
  starting transfers between devices  61.6 us (24%)
  local copies, waits for them, and re-layouts  29.8 us (12%)
  other arithmetic  21 us (8%)
  matrix products  17.8 us (7%)
    ppermute x60, waiting for transfers between devices, swap(): lax.ppermute(values, axis, [(place, place ^ mask) for place in range(coun...  126 us
    ppermute x60, starting transfers between devices, swap(): lax.ppermute(values, axis, [(place, place ^ mask) for place in range(coun...  61.6 us
    unnamed x177, local copies, waits for them, and re-layouts  7.41 us
    concatenate x1, local copies, waits for them, and re-layouts, on_paired_device(): jnp.concatenate([grad_expand, grad_reduce], axis=1)  6.1 us
  transfers between devices with their start and end apart: 60, of which 32 were waited for; matrix products, arithmetic and copies ran while one was open for 17% of the time, Pallas kernels for 0%

profile of v1, /device:TPU:0, one launch (start us, length us, event | category | flops | bytes accessed | tf_op | source)
XLA Modules:
  0.0 258.5 jit_solution(13386147279287951831)
XLA Ops:
  2.7 4.1 %collective-permute-start.20 = (bf16[96,1536]{1,0:T(8,128)(2,1)S(1)}, bf16[96,1536]{1,0:T(8,128)(2,1)S(1)}, u32[]{:S(2)}, u32[]{:S(2)}) collective-permute-start(bf16[96,1536]{1,0:T(8,128)(2,1)S(1)} %constant_dynamic-update-slice_fusion.1), channel_id=1, source_target_pairs={{0,2},{1,3},{2,0},{3,1},{4,6},{5,7},{6,4},{7,5},{8,10},{9,11},{10,... | collective-permute-start | bytes 884744 | tf_op jit(solution)/shard_map/ppermute | solution.py:321
  11.7 1.9 collective-permute-start.1
  13.6 2.7 %collective-permute-start = (bf16[2,64,768]{2,1,0:T(8,128)(2,1)S(1)}, bf16[2,64,768]{2,1,0:T(8,128)(2,1)S(1)}, u32[]{:S(2)}, u32[]{:S(2)}) collective-permute-start(bf16[2,64,768]{2,1,0:T(8,128)(2,1)S(1)} %get-tuple-element.132), channel_id=1, source_target_pairs={{0,2},{1,3},{2,0},{3,1},{4,6},{5,7},{6,4},{7,5},{8,10},{9,11},{10,... | collective-permute-start | bytes 589832 | tf_op jit(solution)/shard_map/ppermute | solution.py:321
  16.8 1.6 collective-permute-start.2
  18.4 7.1 %collective-permute-done.14 = f32[1152]{0:T(1024)S(1)} collective-permute-done((f32[1152]{0:T(1024)S(1)}, f32[1152]{0:T(1024)S(1)}, u32[]{:S(2)}, u32[]{:S(2)}) %collective-permute-start.14) | collective-permute-done | bytes 4640 | tf_op jit(solution)/shard_map/ppermute | solution.py:321
  27.0 2.9 %collective-permute-start.5 = (f32[2,2,1152]{2,0,1:T(2,128)S(1)}, f32[2,2,1152]{2,0,1:T(2,128)S(1)}, u32[]{:S(2)}, u32[]{:S(2)}) collective-permute-start(f32[2,2,1152]{2,0,1:T(2,128)S(1)} %maximum_add_fusion), channel_id=1, source_target_pairs={{0,3},{1,2},{2,1},{3,0},{4,7},{5,6},{6,5},{7,4},{8,11},{9,10},{10,... | collective-permute-start | bytes 55304 | tf_op jit(solution)/shard_map/ppermute | solution.py:321
  31.1 2.3 collective-permute-start.9
  36.2 6.8 %collective-permute-done.9 = bf16[96,768]{0,1:T(8,128)(2,1)S(1)} collective-permute-done((bf16[96,768]{0,1:T(8,128)(2,1)S(1)}, bf16[96,768]{0,1:T(8,128)(2,1)S(1)}, u32[]{:S(2)}, u32[]{:S(2)}) %collective-permute-start.9) | collective-permute-done | bytes 147488 | tf_op jit(solution)/shard_map/ppermute | solution.py:321
  44.8 1.7 collective-permute-start.13
  48.5 1.7 collective-permute-start.24
  50.2 4.5 %collective-permute-done.7 = bf16[2,128,768]{2,1,0:T(8,128)(2,1)S(1)} collective-permute-done((bf16[2,128,768]{2,1,0:T(8,128)(2,1)S(1)}, bf16[2,128,768]{2,1,0:T(8,128)(2,1)S(1)}, u32[]{:S(2)}, u32[]{:S(2)}) %collective-permute-start.7) | collective-permute-done | bytes 393248 | tf_op jit(solution)/shard_map/ppermute | solution.py:321
  54.7 1.7 collective-permute-start.23
  56.8 2.6 %collective-permute-start.22 = (bf16[192,1536]{1,0:T(8,128)(2,1)S(1)}, bf16[192,1536]{1,0:T(8,128)(2,1)S(1)}, u32[]{:S(2)}, u32[]{:S(2)}) collective-permute-start(bf16[192,1536]{1,0:T(8,128)(2,1)S(1)} %pad_maximum_fusion.9), channel_id=1, source_target_pairs={{0,24},{4,28},{8,16},{12,20},{16,8},{20,12},{24,0},{28,4},{1,25},{... | collective-permute-start | bytes 1769480 | tf_op jit(solution)/shard_map/ppermute | solution.py:321
  59.5 7.1 %collective-permute-done.12 = bf16[192,768]{0,1:T(8,128)(2,1)S(1)} collective-permute-done((bf16[192,768]{0,1:T(8,128)(2,1)S(1)}, bf16[192,768]{0,1:T(8,128)(2,1)S(1)}, u32[]{:S(2)}, u32[]{:S(2)}) %collective-permute-start.12) | collective-permute-done | bytes 294944 | tf_op jit(solution)/shard_map/ppermute | solution.py:321
  67.2 1.6 collective-permute-done.8
  72.6 5.4 %collective-permute-done.24 = bf16[192,1536]{1,0:T(8,128)(2,1)S(1)} collective-permute-done((bf16[192,1536]{1,0:T(8,128)(2,1)S(1)}, bf16[192,1536]{1,0:T(8,128)(2,1)S(1)}, u32[]{:S(2)}, u32[]{:S(2)}) %collective-permute-start.24) | collective-permute-done | bytes 589856 | tf_op jit(solution)/shard_map/ppermute | solution.py:321
  77.9 13.2 %collective-permute-done.23 = bf16[192,1536]{1,0:T(8,128)(2,1)S(1)} collective-permute-done((bf16[192,1536]{1,0:T(8,128)(2,1)S(1)}, bf16[192,1536]{1,0:T(8,128)(2,1)S(1)}, u32[]{:S(2)}, u32[]{:S(2)}) %collective-permute-start.23) | collective-permute-done | bytes 589856 | tf_op jit(solution)/shard_map/ppermute | solution.py:321
  93.3 4.5 %collective-permute-done.16 = bf16[128,768]{1,0:T(8,128)(2,1)S(1)} collective-permute-done((bf16[128,768]{1,0:T(8,128)(2,1)S(1)}, bf16[128,768]{1,0:T(8,128)(2,1)S(1)}, u32[]{:S(2)}, u32[]{:S(2)}) %collective-permute-start.16) | collective-permute-done | bytes 196640 | tf_op jit(solution)/shard_map/ppermute | solution.py:321
  100.6 4.0 %collective-permute-done.17 = bf16[128,768]{1,0:T(8,128)(2,1)S(1)} collective-permute-done((bf16[128,768]{1,0:T(8,128)(2,1)S(1)}, bf16[128,768]{1,0:T(8,128)(2,1)S(1)}, u32[]{:S(2)}, u32[]{:S(2)}) %collective-permute-start.17) | collective-permute-done | bytes 196640 | tf_op jit(solution)/shard_map/ppermute | solution.py:321
  108.0 2.1 fusion.148
  111.9 2.5 pad_maximum_fusion
  114.4 6.1 %copy.93 = f32[768,1536]{1,0:T(8,128)} copy(f32[768,1536]{0,1:T(8,128)} %pad_maximum_fusion) | data formatting | bytes 9437184 | tf_op jit(solution)/shard_map/concatenate | solution.py:594
  120.5 2.3 fusion.19
  122.8 2.6 %collective-permute-start.57 = (bf16[192,1536]{1,0:T(8,128)(2,1)S(1)}, bf16[192,1536]{1,0:T(8,128)(2,1)S(1)}, u32[]{:S(2)}, u32[]{:S(2)}) collective-permute-start(bf16[192,1536]{1,0:T(8,128)(2,1)S(1)} %get-tuple-element.92), channel_id=1, source_target_pairs={{0,24},{4,28},{8,16},{12,20},{16,8},{20,12},{24,0},{28,4},{1,25},{... | collective-permute-start | bytes 1769480 | tf_op jit(solution)/shard_map/ppermute | solution.py:321
  129.7 10.3 %collective-permute-done.57 = bf16[192,1536]{1,0:T(8,128)(2,1)S(1)} collective-permute-done((bf16[192,1536]{1,0:T(8,128)(2,1)S(1)}, bf16[192,1536]{1,0:T(8,128)(2,1)S(1)}, u32[]{:S(2)}, u32[]{:S(2)}) %collective-permute-start.57) | collective-permute-done | bytes 589856 | tf_op jit(solution)/shard_map/ppermute | solution.py:321
  140.0 11.8 %collective-permute-done.56 = bf16[192,1536]{1,0:T(8,128)(2,1)S(1)} collective-permute-done((bf16[192,1536]{1,0:T(8,128)(2,1)S(1)}, bf16[192,1536]{1,0:T(8,128)(2,1)S(1)}, u32[]{:S(2)}, u32[]{:S(2)}) %collective-permute-start.56) | collective-permute-done | bytes 589856 | tf_op jit(solution)/shard_map/ppermute | solution.py:321
  151.8 1.5 fusion.14
  155.9 5.4 %collective-permute-done.26 = bf16[128,768]{1,0:T(8,128)(2,1)S(1)} collective-permute-done((bf16[128,768]{1,0:T(8,128)(2,1)S(1)}, bf16[128,768]{1,0:T(8,128)(2,1)S(1)}, u32[]{:S(2)}, u32[]{:S(2)}) %collective-permute-start.26) | collective-permute-done | bytes 196640 | tf_op jit(solution)/shard_map/ppermute | solution.py:321
  161.3 3.3 %collective-permute-done.29 = bf16[128,768]{1,0:T(8,128)(2,1)S(1)} collective-permute-done((bf16[128,768]{1,0:T(8,128)(2,1)S(1)}, bf16[128,768]{1,0:T(8,128)(2,1)S(1)}, u32[]{:S(2)}, u32[]{:S(2)}) %collective-permute-start.29) | collective-permute-done | bytes 196640 | tf_op jit(solution)/shard_map/ppermute | solution.py:321
  165.0 2.0 collective-permute-start.27
  169.7 5.8 %collective-permute-done.50 = f32[768]{0:T(1024)S(1)} collective-permute-done((f32[768]{0:T(1024)S(1)}, f32[768]{0:T(1024)S(1)}, u32[]{:S(2)}, u32[]{:S(2)}) %collective-permute-start.50) | collective-permute-done | bytes 3104 | tf_op jit(solution)/shard_map/ppermute | solution.py:321
  182.4 2.1 convolution_bitcast_fusion
  187.6 1.9 collective-permute-done.51
  190.9 1.6 pad_maximum_fusion.1
  192.5 3.1 %copy.90 = f32[768,768]{1,0:T(8,128)} copy(f32[768,768]{0,1:T(8,128)} %pad_maximum_fusion.1) | data formatting | bytes 4718592 | tf_op jit(solution)/shard_map/concatenate | solution.py:597
  195.5 2.1 collective-permute-start.53
  197.7 2.3 fusion.55
  201.8 1.6 collective-permute-start.44
  206.2 4.9 %collective-permute-done.46 = bf16[192,768]{1,0:T(8,128)(2,1)S(1)} collective-permute-done((bf16[192,768]{1,0:T(8,128)(2,1)}, bf16[192,768]{1,0:T(8,128)(2,1)S(1)}, u32[]{:S(2)}, u32[]{:S(2)}) %collective-permute-start.46) | collective-permute-done | bytes 294944 | tf_op jit(solution)/shard_map/ppermute | solution.py:321
  211.0 3.8 %collective-permute-done.45 = bf16[192,768]{1,0:T(8,128)(2,1)S(1)} collective-permute-done((bf16[192,768]{1,0:T(8,128)(2,1)}, bf16[192,768]{1,0:T(8,128)(2,1)S(1)}, u32[]{:S(2)}, u32[]{:S(2)}) %collective-permute-start.45) | collective-permute-done | bytes 294944 | tf_op jit(solution)/shard_map/ppermute | solution.py:321
  222.4 8.6 %collective-permute-done.48 = bf16[96,768]{0,1:T(8,128)(2,1)S(1)} collective-permute-done((bf16[96,768]{0,1:T(8,128)(2,1)S(1)}, bf16[96,768]{0,1:T(8,128)(2,1)S(1)}, u32[]{:S(2)}, u32[]{:S(2)}) %collective-permute-start.48) | collective-permute-done | bytes 147488 | tf_op jit(solution)/shard_map/ppermute | solution.py:321
  233.3 1.8 collective-permute-start.38
  235.1 1.7 collective-permute-start.36
  241.1 3.0 %collective-permute-done.40 = f32[4,1152]{1,0:T(4,128)S(1)} collective-permute-done((f32[4,1152]{1,0:T(4,128)S(1)}, f32[4,1152]{1,0:T(4,128)S(1)}, u32[]{:S(2)}, u32[]{:S(2)}) %collective-permute-start.40) | collective-permute-done | bytes 18464 | tf_op jit(solution)/shard_map/ppermute | solution.py:321
  244.9 1.9 collective-permute-start.35
  248.2 1.6 collective-permute-start.42
  252.0 1.9 collective-permute-start.43
  254.4 2.1 collective-permute-done.43
  (425 shorter events, 76.9 us)
Async XLA Ops:
  2.7 40.5 %collective-permute-start.20 = (bf16[96,1536]{1,0:T(8,128)(2,1)S(1)}, bf16[96,1536]{1,0:T(8,128)(2,1)S(1)}, u32[]{:S(2)}, u32[]{:S(2)}) collective-permute-start(bf16[96,1536]{1,0:T(8,128)(2,1)S(1)} %constant_dynamic-update-slice_fusion.1), channel_id=1, source_target_pairs={{0,2},{1,3},{2,0},{3,1},{4,6},{5,7},{6,4},{7,5},{8,10},{9,11},{10,... | collective-permute-start | bytes 884744 | tf_op jit(solution)/shard_map/ppermute | solution.py:321
  8.3 17.3 %collective-permute-start.14 = (f32[1152]{0:T(1024)S(1)}, f32[1152]{0:T(1024)S(1)}, u32[]{:S(2)}, u32[]{:S(2)}) collective-permute-start(f32[1152]{0:T(1024)S(1)} %constant_dynamic-update-slice_fusion.5), channel_id=1, source_target_pairs={{0,2},{1,3},{2,0},{3,1},{4,6},{5,7},{6,4},{7,5},{8,10},{9,11},{10,... | collective-permute-start | bytes 13832 | tf_op jit(solution)/shard_map/ppermute | solution.py:321
  11.7 5.1 %collective-permute-start.1 = (f32[4,2,1152]{2,0,1:T(4,128)S(1)}, f32[4,2,1152]{2,0,1:T(4,128)S(1)}, u32[]{:S(2)}, u32[]{:S(2)}) collective-permute-start(f32[4,2,1152]{2,0,1:T(4,128)S(1)} %copy.78), channel_id=1, source_target_pairs={{0,16},{4,20},{8,24},{12,28},{16,0},{20,4},{24,8},{28,12},{1,17},{... | collective-permute-start | bytes 110600 | tf_op jit(solution)/shard_map/ppermute | solution.py:321
  13.6 29.4 %collective-permute-start = (bf16[2,64,768]{2,1,0:T(8,128)(2,1)S(1)}, bf16[2,64,768]{2,1,0:T(8,128)(2,1)S(1)}, u32[]{:S(2)}, u32[]{:S(2)}) collective-permute-start(bf16[2,64,768]{2,1,0:T(8,128)(2,1)S(1)} %get-tuple-element.132), channel_id=1, source_target_pairs={{0,2},{1,3},{2,0},{3,1},{4,6},{5,7},{6,4},{7,5},{8,10},{9,11},{10,... | collective-permute-start | bytes 589832 | tf_op jit(solution)/shard_map/ppermute | solution.py:321
  16.8 8.7 %collective-permute-start.2 = (f32[2,2,1152]{2,0,1:T(2,128)S(1)}, f32[2,2,1152]{2,0,1:T(2,128)S(1)}, u32[]{:S(2)}, u32[]{:S(2)}) collective-permute-start(f32[2,2,1152]{2,0,1:T(2,128)S(1)} %slice.433), channel_id=1, source_target_pairs={{0,8},{4,12},{8,0},{12,4},{16,24},{20,28},{24,16},{28,20},{1,9},{5... | collective-permute-start | bytes 55304 | tf_op jit(solution)/shard_map/ppermute | solution.py:321
  26.9 4.2 %collective-permute-start.6 = (f32[2,2,1152]{2,0,1:T(2,128)S(1)}, f32[2,2,1152]{2,0,1:T(2,128)S(1)}, u32[]{:S(2)}, u32[]{:S(2)}) collective-permute-start(f32[2,2,1152]{2,0,1:T(2,128)S(1)} %maximum_add_fusion), channel_id=1, source_target_pairs={{0,1},{1,0},{2,3},{3,2},{4,5},{5,4},{6,7},{7,6},{8,9},{9,8},{10,11... | collective-permute-start | bytes 55304 | tf_op jit(solution)/shard_map/ppermute | solution.py:321
  27.0 6.5 %collective-permute-start.5 = (f32[2,2,1152]{2,0,1:T(2,128)S(1)}, f32[2,2,1152]{2,0,1:T(2,128)S(1)}, u32[]{:S(2)}, u32[]{:S(2)}) collective-permute-start(f32[2,2,1152]{2,0,1:T(2,128)S(1)} %maximum_add_fusion), channel_id=1, source_target_pairs={{0,3},{1,2},{2,1},{3,0},{4,7},{5,6},{6,5},{7,4},{8,11},{9,10},{10,... | collective-permute-start | bytes 55304 | tf_op jit(solution)/shard_map/ppermute | solution.py:321
  29.8 4.9 %collective-permute-start.4 = (f32[2,2,1152]{2,0,1:T(2,128)S(1)}, f32[2,2,1152]{2,0,1:T(2,128)S(1)}, u32[]{:S(2)}, u32[]{:S(2)}) collective-permute-start(f32[2,2,1152]{2,0,1:T(2,128)S(1)} %maximum_add_fusion), channel_id=1, source_target_pairs={{0,2},{1,3},{2,0},{3,1},{4,6},{5,7},{6,4},{7,5},{8,10},{9,11},{10,... | collective-permute-start | bytes 55304 | tf_op jit(solution)/shard_map/ppermute | solution.py:321
  31.1 11.8 %collective-permute-start.9 = (bf16[96,768]{0,1:T(8,128)(2,1)S(1)}, bf16[96,768]{0,1:T(8,128)(2,1)S(1)}, u32[]{:S(2)}, u32[]{:S(2)}) collective-permute-start(bf16[96,768]{0,1:T(8,128)(2,1)S(1)} %pad_maximum_fusion.18), channel_id=1, source_target_pairs={{0,2},{1,3},{2,0},{3,1},{4,6},{5,7},{6,4},{7,5},{8,10},{9,11},{10,... | collective-permute-start | bytes 442376 | tf_op jit(solution)/shard_map/ppermute | solution.py:321
  43.1 11.6 %collective-permute-start.7 = (bf16[2,128,768]{2,1,0:T(8,128)(2,1)S(1)}, bf16[2,128,768]{2,1,0:T(8,128)(2,1)S(1)}, u32[]{:S(2)}, u32[]{:S(2)}) collective-permute-start(bf16[2,128,768]{2,1,0:T(8,128)(2,1)S(1)} %pad_maximum_fusion.10), channel_id=1, source_target_pairs={{0,1},{1,0},{2,3},{3,2},{4,5},{5,4},{6,7},{7,6},{8,9},{9,8},{10,11... | collective-permute-start | bytes 1179656 | tf_op jit(solution)/shard_map/ppermute | solution.py:321
  43.2 5.1 %collective-permute-start.21 = (bf16[96,1536]{1,0:T(8,128)(2,1)S(1)}, bf16[96,1536]{1,0:T(8,128)(2,1)S(1)}, u32[]{:S(2)}, u32[]{:S(2)}) collective-permute-start(bf16[96,1536]{1,0:T(8,128)(2,1)S(1)} %broadcast_select_fusion), channel_id=1, source_target_pairs={{0,4},{4,0},{8,12},{12,8},{16,20},{20,16},{24,28},{28,24},{1,5},{5... | collective-permute-start | bytes 884744 | tf_op jit(solution)/shard_map/ppermute | solution.py:321
  44.8 12.0 %collective-permute-start.13 = (bf16[192,768]{0,1:T(8,128)(2,1)S(1)}, bf16[192,768]{0,1:T(8,128)(2,1)S(1)}, u32[]{:S(2)}, u32[]{:S(2)}) collective-permute-start(bf16[192,768]{0,1:T(8,128)(2,1)S(1)} %pad_maximum_fusion.11), channel_id=1, source_target_pairs={{0,8},{4,12},{8,0},{12,4},{16,24},{20,28},{24,16},{28,20},{1,9},{5... | collective-permute-start | bytes 884744 | tf_op jit(solution)/shard_map/ppermute | solution.py:321
  46.5 20.0 %collective-permute-start.12 = (bf16[192,768]{0,1:T(8,128)(2,1)S(1)}, bf16[192,768]{0,1:T(8,128)(2,1)S(1)}, u32[]{:S(2)}, u32[]{:S(2)}) collective-permute-start(bf16[192,768]{0,1:T(8,128)(2,1)S(1)} %pad_maximum_fusion.11), channel_id=1, source_target_pairs={{0,16},{4,20},{8,24},{12,28},{16,0},{20,4},{24,8},{28,12},{1,17},{... | collective-permute-start | bytes 884744 | tf_op jit(solution)/shard_map/ppermute | solution.py:321
  48.1 18.5 %collective-permute-start.11 = (bf16[192,768]{0,1:T(8,128)(2,1)S(1)}, bf16[192,768]{0,1:T(8,128)(2,1)S(1)}, u32[]{:S(2)}, u32[]{:S(2)}) collective-permute-start(bf16[192,768]{0,1:T(8,128)(2,1)S(1)} %pad_maximum_fusion.11), channel_id=1, source_target_pairs={{0,24},{4,28},{8,16},{12,20},{16,8},{20,12},{24,0},{28,4},{1,25},{... | collective-permute-start | bytes 884744 | tf_op jit(solution)/shard_map/ppermute | solution.py:321
  48.5 29.5 %collective-permute-start.24 = (bf16[192,1536]{1,0:T(8,128)(2,1)S(1)}, bf16[192,1536]{1,0:T(8,128)(2,1)S(1)}, u32[]{:S(2)}, u32[]{:S(2)}) collective-permute-start(bf16[192,1536]{1,0:T(8,128)(2,1)S(1)} %pad_maximum_fusion.9), channel_id=1, source_target_pairs={{0,8},{4,12},{8,0},{12,4},{16,24},{20,28},{24,16},{28,20},{1,9},{5... | collective-permute-start | bytes 1769480 | tf_op jit(solution)/shard_map/ppermute | solution.py:321
  54.7 36.4 %collective-permute-start.23 = (bf16[192,1536]{1,0:T(8,128)(2,1)S(1)}, bf16[192,1536]{1,0:T(8,128)(2,1)S(1)}, u32[]{:S(2)}, u32[]{:S(2)}) collective-permute-start(bf16[192,1536]{1,0:T(8,128)(2,1)S(1)} %pad_maximum_fusion.9), channel_id=1, source_target_pairs={{0,16},{4,20},{8,24},{12,28},{16,0},{20,4},{24,8},{28,12},{1,17},{... | collective-permute-start | bytes 1769480 | tf_op jit(solution)/shard_map/ppermute | solution.py:321
  56.8 34.3 %collective-permute-start.22 = (bf16[192,1536]{1,0:T(8,128)(2,1)S(1)}, bf16[192,1536]{1,0:T(8,128)(2,1)S(1)}, u32[]{:S(2)}, u32[]{:S(2)}) collective-permute-start(bf16[192,1536]{1,0:T(8,128)(2,1)S(1)} %pad_maximum_fusion.9), channel_id=1, source_target_pairs={{0,24},{4,28},{8,16},{12,20},{16,8},{20,12},{24,0},{28,4},{1,25},{... | collective-permute-start | bytes 1769480 | tf_op jit(solution)/shard_map/ppermute | solution.py:321
  72.3 19.3 %collective-permute-start.15 = (f32[256,768]{1,0:T(8,128)S(1)}, f32[256,768]{1,0:T(8,128)S(1)}, u32[]{:S(2)}, u32[]{:S(2)}) collective-permute-start(f32[256,768]{1,0:T(8,128)S(1)} %slice_bitcast_fusion.2), channel_id=1, source_target_pairs={{0,4},{4,0},{8,12},{12,8},{16,20},{20,16},{24,28},{28,24},{1,5},{5... | collective-permute-start | bytes 2359304 | tf_op jit(solution)/shard_map/ppermute | solution.py:321
  91.7 6.0 %collective-permute-start.16 = (bf16[128,768]{1,0:T(8,128)(2,1)S(1)}, bf16[128,768]{1,0:T(8,128)(2,1)S(1)}, u32[]{:S(2)}, u32[]{:S(2)}) collective-permute-start(bf16[128,768]{1,0:T(8,128)(2,1)S(1)} %slice.805), channel_id=1, source_target_pairs={{0,1},{1,0},{2,3},{3,2},{4,5},{5,4},{6,7},{7,6},{8,9},{9,8},{10,11... | collective-permute-start | bytes 589832 | tf_op jit(solution)/shard_map/ppermute | solution.py:321
  98.9 5.7 %collective-permute-start.17 = (bf16[128,768]{1,0:T(8,128)(2,1)S(1)}, bf16[128,768]{1,0:T(8,128)(2,1)S(1)}, u32[]{:S(2)}, u32[]{:S(2)}) collective-permute-start(bf16[128,768]{1,0:T(8,128)(2,1)S(1)} %add_convert_fusion.2), channel_id=1, source_target_pairs={{0,1},{1,0},{2,3},{3,2},{4,5},{5,4},{6,7},{7,6},{8,9},{9,8},{10,11... | collective-permute-start | bytes 589832 | tf_op jit(solution)/shard_map/ppermute | solution.py:321
  100.5 4.3 %collective-permute-start.18 = (bf16[128,768]{1,0:T(8,128)(2,1)S(1)}, bf16[128,768]{1,0:T(8,128)(2,1)S(1)}, u32[]{:S(2)}, u32[]{:S(2)}) collective-permute-start(bf16[128,768]{1,0:T(8,128)(2,1)S(1)} %add_convert_fusion.2), channel_id=1, source_target_pairs={{0,4},{4,0},{8,12},{12,8},{16,20},{20,16},{24,28},{28,24},{1,5},{5... | collective-permute-start | bytes 589832 | tf_op jit(solution)/shard_map/ppermute | solution.py:321
  122.8 17.2 %collective-permute-start.57 = (bf16[192,1536]{1,0:T(8,128)(2,1)S(1)}, bf16[192,1536]{1,0:T(8,128)(2,1)S(1)}, u32[]{:S(2)}, u32[]{:S(2)}) collective-permute-start(bf16[192,1536]{1,0:T(8,128)(2,1)S(1)} %get-tuple-element.92), channel_id=1, source_target_pairs={{0,24},{4,28},{8,16},{12,20},{16,8},{20,12},{24,0},{28,4},{1,25},{... | collective-permute-start | bytes 1769480 | tf_op jit(solution)/shard_map/ppermute | solution.py:321
  125.5 26.3 %collective-permute-start.56 = (bf16[192,1536]{1,0:T(8,128)(2,1)S(1)}, bf16[192,1536]{1,0:T(8,128)(2,1)S(1)}, u32[]{:S(2)}, u32[]{:S(2)}) collective-permute-start(bf16[192,1536]{1,0:T(8,128)(2,1)S(1)} %get-tuple-element.93), channel_id=1, source_target_pairs={{0,16},{4,20},{8,24},{12,28},{16,0},{20,4},{24,8},{28,12},{1,17},{... | collective-permute-start | bytes 1769480 | tf_op jit(solution)/shard_map/ppermute | solution.py:321
  125.8 26.0 %collective-permute-start.55 = (bf16[192,1536]{1,0:T(8,128)(2,1)S(1)}, bf16[192,1536]{1,0:T(8,128)(2,1)S(1)}, u32[]{:S(2)}, u32[]{:S(2)}) collective-permute-start(bf16[192,1536]{1,0:T(8,128)(2,1)S(1)} %get-tuple-element.91), channel_id=1, source_target_pairs={{0,8},{4,12},{8,0},{12,4},{16,24},{20,28},{24,16},{28,20},{1,9},{5... | collective-permute-start | bytes 1769480 | tf_op jit(solution)/shard_map/ppermute | solution.py:321
  127.6 25.7 %collective-permute-start.25 = (f32[256,768]{1,0:T(8,128)S(1)}, f32[256,768]{1,0:T(8,128)S(1)}, u32[]{:S(2)}, u32[]{:S(2)}) collective-permute-start(f32[256,768]{1,0:T(8,128)S(1)} %slice.484), channel_id=1, source_target_pairs={{0,4},{4,0},{8,12},{12,8},{16,20},{20,16},{24,28},{28,24},{1,5},{5... | collective-permute-start | bytes 2359304 | tf_op jit(solution)/shard_map/ppermute | solution.py:321
  129.6 25.3 %collective-permute-start.28 = (f32[256,768]{1,0:T(8,128)S(1)}, f32[256,768]{1,0:T(8,128)S(1)}, u32[]{:S(2)}, u32[]{:S(2)}) collective-permute-start(f32[256,768]{1,0:T(8,128)S(1)} %slice.495), channel_id=1, source_target_pairs={{0,4},{4,0},{8,12},{12,8},{16,20},{20,16},{24,28},{28,24},{1,5},{5... | collective-permute-start | bytes 2359304 | tf_op jit(solution)/shard_map/ppermute | solution.py:321
  153.5 7.8 %collective-permute-start.26 = (bf16[128,768]{1,0:T(8,128)(2,1)S(1)}, bf16[128,768]{1,0:T(8,128)(2,1)S(1)}, u32[]{:S(2)}, u32[]{:S(2)}) collective-permute-start(bf16[128,768]{1,0:T(8,128)(2,1)S(1)} %slice.804), channel_id=1, source_target_pairs={{0,1},{1,0},{2,3},{3,2},{4,5},{5,4},{6,7},{7,6},{8,9},{9,8},{10,11... | collective-permute-start | bytes 589832 | tf_op jit(solution)/shard_map/ppermute | solution.py:321
  155.1 9.5 %collective-permute-start.29 = (bf16[128,768]{1,0:T(8,128)(2,1)S(1)}, bf16[128,768]{1,0:T(8,128)(2,1)S(1)}, u32[]{:S(2)}, u32[]{:S(2)}) collective-permute-start(bf16[128,768]{1,0:T(8,128)(2,1)S(1)} %slice.803), channel_id=1, source_target_pairs={{0,1},{1,0},{2,3},{3,2},{4,5},{5,4},{6,7},{7,6},{8,9},{9,8},{10,11... | collective-permute-start | bytes 589832 | tf_op jit(solution)/shard_map/ppermute | solution.py:321
  155.9 20.3 %collective-permute-start.58 = (f32[96,1536]{1,0:T(8,128)S(1)}, f32[96,1536]{1,0:T(8,128)S(1)}, u32[]{:S(2)}, u32[]{:S(2)}) collective-permute-start(f32[96,1536]{1,0:T(8,128)S(1)} %dynamic-slice_bitcast_fusion), channel_id=1, source_target_pairs={{0,4},{4,0},{8,12},{12,8},{16,20},{20,16},{24,28},{28,24},{1,5},{5... | collective-permute-start | bytes 1769480 | tf_op jit(solution)/shard_map/ppermute | solution.py:321
  165.0 10.4 %collective-permute-start.27 = (bf16[64,768]{1,0:T(8,128)(2,1)S(1)}, bf16[64,768]{1,0:T(8,128)(2,1)S(1)}, u32[]{:S(2)}, u32[]{:S(2)}) collective-permute-start(bf16[64,768]{1,0:T(8,128)(2,1)S(1)} %get-tuple-element.135), channel_id=1, source_target_pairs={{0,2},{1,3},{2,0},{3,1},{4,6},{5,7},{6,4},{7,5},{8,10},{9,11},{10,... | collective-permute-start | bytes 294920 | tf_op jit(solution)/shard_map/ppermute | solution.py:321
  167.5 8.6 %collective-permute-start.30 = (bf16[128,768]{1,0:T(8,128)(2,1)S(1)}, bf16[128,768]{1,0:T(8,128)(2,1)S(1)}, u32[]{:S(2)}, u32[]{:S(2)}) collective-permute-start(bf16[128,768]{1,0:T(8,128)(2,1)S(1)} %multiply_convert_fusion.3), channel_id=1, source_target_pairs={{0,1},{1,0},{2,3},{3,2},{4,5},{5,4},{6,7},{7,6},{8,9},{9,8},{10,11... | collective-permute-start | bytes 589832 | tf_op jit(solution)/shard_map/ppermute | solution.py:321
  168.7 6.8 %collective-permute-start.50 = (f32[768]{0:T(1024)S(1)}, f32[768]{0:T(1024)S(1)}, u32[]{:S(2)}, u32[]{:S(2)}) collective-permute-start(f32[768]{0:T(1024)S(1)} %add.464), channel_id=1, source_target_pairs={{0,1},{1,0},{2,3},{3,2},{4,5},{5,4},{6,7},{7,6},{8,9},{9,8},{10,11... | collective-permute-start | bytes 9224 | tf_op jit(solution)/shard_map/ppermute | solution.py:321
  169.6 8.3 %collective-permute-start.31 = (bf16[128,768]{1,0:T(8,128)(2,1)S(1)}, bf16[128,768]{1,0:T(8,128)(2,1)S(1)}, u32[]{:S(2)}, u32[]{:S(2)}) collective-permute-start(bf16[128,768]{1,0:T(8,128)(2,1)S(1)} %multiply_convert_fusion.3), channel_id=1, source_target_pairs={{0,4},{4,0},{8,12},{12,8},{16,20},{20,16},{24,28},{28,24},{1,5},{5... | collective-permute-start | bytes 589832 | tf_op jit(solution)/shard_map/ppermute | solution.py:321
  177.1 39.2 %collective-permute-start.59 = (bf16[96,1536]{1,0:T(8,128)(2,1)}, bf16[96,1536]{1,0:T(8,128)(2,1)}, u32[]{:S(2)}, u32[]{:S(2)}) collective-permute-start(bf16[96,1536]{1,0:T(8,128)(2,1)} %fusion.23), channel_id=1, source_target_pairs={{0,2},{1,3},{2,0},{3,1},{4,6},{5,7},{6,4},{7,5},{8,10},{9,11},{10,... | collective-permute-start | bytes 884744 | tf_op jit(solution)/shard_map/ppermute | solution.py:321
  189.5 6.0 %collective-permute-start.52 = (f32[2688]{0:T(1024)S(1)}, f32[2688]{0:T(1024)S(1)}, u32[]{:S(2)}, u32[]{:S(2)}) collective-permute-start(f32[2688]{0:T(1024)S(1)} %add.470), channel_id=1, source_target_pairs={{0,16},{4,20},{8,24},{12,28},{16,0},{20,4},{24,8},{28,12},{1,17},{... | collective-permute-start | bytes 32264 | tf_op jit(solution)/shard_map/ppermute | solution.py:321
  195.5 7.9 %collective-permute-start.53 = (f32[2688]{0:T(1024)S(1)}, f32[2688]{0:T(1024)S(1)}, u32[]{:S(2)}, u32[]{:S(2)}) collective-permute-start(f32[2688]{0:T(1024)S(1)} %add.471), channel_id=1, source_target_pairs={{0,2},{1,3},{2,0},{3,1},{4,6},{5,7},{6,4},{7,5},{8,10},{9,11},{10,... | collective-permute-start | bytes 32264 | tf_op jit(solution)/shard_map/ppermute | solution.py:321
  200.0 11.1 %collective-permute-start.46 = (bf16[192,768]{1,0:T(8,128)(2,1)}, bf16[192,768]{1,0:T(8,128)(2,1)S(1)}, u32[]{:S(2)}, u32[]{:S(2)}) collective-permute-start(bf16[192,768]{1,0:T(8,128)(2,1)} %get-tuple-element.95), channel_id=1, source_target_pairs={{0,24},{4,28},{8,16},{12,20},{16,8},{20,12},{24,0},{28,4},{1,25},{... | collective-permute-start | bytes 884744 | tf_op jit(solution)/shard_map/ppermute | solution.py:321
  201.3 13.5 %collective-permute-start.45 = (bf16[192,768]{1,0:T(8,128)(2,1)}, bf16[192,768]{1,0:T(8,128)(2,1)S(1)}, u32[]{:S(2)}, u32[]{:S(2)}) collective-permute-start(bf16[192,768]{1,0:T(8,128)(2,1)} %get-tuple-element.96), channel_id=1, source_target_pairs={{0,16},{4,20},{8,24},{12,28},{16,0},{20,4},{24,8},{28,12},{1,17},{... | collective-permute-start | bytes 884744 | tf_op jit(solution)/shard_map/ppermute | solution.py:321
  201.8 13.0 %collective-permute-start.44 = (bf16[192,768]{1,0:T(8,128)(2,1)S(1)}, bf16[192,768]{1,0:T(8,128)(2,1)S(1)}, u32[]{:S(2)}, u32[]{:S(2)}) collective-permute-start(bf16[192,768]{1,0:T(8,128)(2,1)S(1)} %get-tuple-element.94), channel_id=1, source_target_pairs={{0,8},{4,12},{8,0},{12,4},{16,24},{20,28},{24,16},{28,20},{1,9},{5... | collective-permute-start | bytes 884744 | tf_op jit(solution)/shard_map/ppermute | solution.py:321
  204.7 15.1 %collective-permute-start.33 = (f32[256,768]{1,0:T(8,128)}, f32[256,768]{1,0:T(8,128)}, u32[]{:S(2)}, u32[]{:S(2)}) collective-permute-start(f32[256,768]{1,0:T(8,128)} %slice_bitcast_fusion), channel_id=1, source_target_pairs={{0,4},{4,0},{8,12},{12,8},{16,20},{20,16},{24,28},{28,24},{1,5},{5... | collective-permute-start | bytes 2359304 | tf_op jit(solution)/shard_map/ppermute | solution.py:321
  218.5 12.6 %collective-permute-start.48 = (bf16[96,768]{0,1:T(8,128)(2,1)S(1)}, bf16[96,768]{0,1:T(8,128)(2,1)S(1)}, u32[]{:S(2)}, u32[]{:S(2)}) collective-permute-start(bf16[96,768]{0,1:T(8,128)(2,1)S(1)} %fusion.48), channel_id=1, source_target_pairs={{0,2},{1,3},{2,0},{3,1},{4,6},{5,7},{6,4},{7,5},{8,10},{9,11},{10,... | collective-permute-start | bytes 442376 | tf_op jit(solution)/shard_map/ppermute | solution.py:321
  221.3 11.5 %collective-permute-start.34 = (bf16[128,768]{1,0:T(8,128)(2,1)S(1)}, bf16[128,768]{1,0:T(8,128)(2,1)S(1)}, u32[]{:S(2)}, u32[]{:S(2)}) collective-permute-start(bf16[128,768]{1,0:T(8,128)(2,1)S(1)} %slice.802), channel_id=1, source_target_pairs={{0,1},{1,0},{2,3},{3,2},{4,5},{5,4},{6,7},{7,6},{8,9},{9,8},{10,11... | collective-permute-start | bytes 589832 | tf_op jit(solution)/shard_map/ppermute | solution.py:321
  233.2 4.6 %collective-permute-start.37 = (f32[1152]{0:T(1024)S(1)}, f32[1152]{0:T(1024)S(1)}, u32[]{:S(2)}, u32[]{:S(2)}) collective-permute-start(f32[1152]{0:T(1024)S(1)} %get-tuple-element.64), channel_id=1, source_target_pairs={{0,2},{1,3},{2,0},{3,1},{4,6},{5,7},{6,4},{7,5},{8,10},{9,11},{10,... | collective-permute-start | bytes 13832 | tf_op jit(solution)/shard_map/ppermute | solution.py:321
  233.3 5.5 %collective-permute-start.38 = (f32[1152]{0:T(1024)S(1)}, f32[1152]{0:T(1024)S(1)}, u32[]{:S(2)}, u32[]{:S(2)}) collective-permute-start(f32[1152]{0:T(1024)S(1)} %get-tuple-element.63), channel_id=1, source_target_pairs={{0,3},{1,2},{2,1},{3,0},{4,7},{5,6},{6,5},{7,4},{8,11},{9,10},{10,... | collective-permute-start | bytes 13832 | tf_op jit(solution)/shard_map/ppermute | solution.py:321
  240.2 3.8 %collective-permute-start.40 = (f32[4,1152]{1,0:T(4,128)S(1)}, f32[4,1152]{1,0:T(4,128)S(1)}, u32[]{:S(2)}, u32[]{:S(2)}) collective-permute-start(f32[4,1152]{1,0:T(4,128)S(1)} %pad_maximum_fusion.24), channel_id=1, source_target_pairs={{0,8},{4,12},{8,0},{12,4},{16,24},{20,28},{24,16},{28,20},{1,9},{5... | collective-permute-start | bytes 55304 | tf_op jit(solution)/shard_map/ppermute | solution.py:321
  244.1 4.0 %collective-permute-start.41 = (f32[8,1152]{1,0:T(8,128)S(1)}, f32[8,1152]{1,0:T(8,128)S(1)}, u32[]{:S(2)}, u32[]{:S(2)}) collective-permute-start(f32[8,1152]{1,0:T(8,128)S(1)} %pad_maximum_fusion.23), channel_id=1, source_target_pairs={{0,16},{4,20},{8,24},{12,28},{16,0},{20,4},{24,8},{28,12},{1,17},{... | collective-permute-start | bytes 110600 | tf_op jit(solution)/shard_map/ppermute | solution.py:321
  244.9 12.8 %collective-permute-start.35 = (f32[64,768]{1,0:T(8,128)S(1)}, f32[64,768]{1,0:T(8,128)S(1)}, u32[]{:S(2)}, u32[]{:S(2)}) collective-permute-start(f32[64,768]{1,0:T(8,128)S(1)} %get-tuple-element.130), channel_id=1, source_target_pairs={{0,2},{1,3},{2,0},{3,1},{4,6},{5,7},{6,4},{7,5},{8,10},{9,11},{10,... | collective-permute-start | bytes 589832 | tf_op jit(solution)/shard_map/ppermute | solution.py:321
  252.0 4.5 %collective-permute-start.43 = (f32[16,96]{1,0:T(8,128)S(1)}, f32[16,96]{1,0:T(8,128)S(1)}, u32[]{:S(2)}, u32[]{:S(2)}) collective-permute-start(f32[16,96]{1,0:T(8,128)S(1)} %add.443), channel_id=1, source_target_pairs={{0,2},{1,3},{2,0},{3,1},{4,6},{5,7},{6,4},{7,5},{8,10},{9,11},{10,... | collective-permute-start | bytes 18440 | tf_op jit(solution)/shard_map/ppermute | solution.py:321
  (94 other events, 745.5 us)

commit v2 on v0

--- a/solution.py
+++ b/solution.py
@@ -1,8 +1,11 @@
+import functools
 import math
 
 import jax
 import jax.numpy as jnp
 from jax import lax
+from jax.experimental import pallas as pl
+from jax.experimental.pallas import tpu as pltpu
 from jax.sharding import PartitionSpec as P
 
 HD = 64
@@ -316,7 +319,755 @@
     )
 
 
+def swap(values, axis, mask):
+    count = lax.axis_size(axis)
+    return lax.ppermute(values, axis, [(place, place ^ mask) for place in range(count)])
+
+
+def unxor(parts, own):
+    bit = 1
+    while bit < len(parts):
+        odd = (own & bit) != 0
+        parts = [jnp.where(odd, parts[r ^ bit], parts[r]) for r in range(len(parts))]
+        bit *= 2
+    return parts
+
+
+def pick(values, place):
+    return lax.dynamic_index_in_dim(values, place, 0, keepdims=False)
+
+
+def exchange_latents(pair, half):
+    return jnp.concatenate([pick(pair, half), swap(pick(pair, 1 - half), "tensor", 2)])
+
+
+def spread_pairs(own_half, other_half):
+    return spread_rows(own_half + swap(other_half, "dp", 1))
+
+
+def spread_rows(both):
+    rows = both.shape[0] // 2
+    return both[:rows] + swap(both[rows:].astype(jnp.bfloat16), "tensor", 1).astype(jnp.float32)
+
+
+def collect_pairs(rows):
+    near = swap(rows, "tensor", 1)
+    return [rows, near, swap(rows, "dp", 1), swap(near, "dp", 1)]
+
+
+def after(values, *earlier):
+    return lax.optimization_barrier((values,) + earlier)[0]
+
+
+def near_weight(shard, far, is_own, core):
+    mine = jnp.where(is_own, shard, far)
+    other = swap(jnp.where(is_own, far, shard), "dp", 1)
+    first = core == 0
+    return jnp.concatenate(
+        [jnp.where(first, mine, other), jnp.where(first, other, mine)], axis=0
+    )
+
+
+def chip_rows(share):
+    count = share.shape[0] // 2
+    first, second = share[:count], share[count:]
+    first_x, second_y = swap(first, "dp", 2), swap(second, "dp", 4)
+    first_y = swap(jnp.concatenate([first, first_x]), "dp", 4)
+    second_x = swap(jnp.concatenate([second, second_y]), "dp", 2)
+    return [share, first_x, second_y, first_y, second_x]
+
+
+def place_rows(chip, parts, out_refs):
+    share, first_x, second_y, first_y, second_x = parts
+    count = first_x.shape[0]
+    plan = [
+        (0, 0, share, 0),
+        (0, 1, share, 1),
+        (1, 0, first_x, 0),
+        (1, 1, second_x, 0),
+        (2, 0, first_y, 0),
+        (2, 1, second_y, 0),
+        (3, 0, first_y, 1),
+        (3, 1, second_x, 1),
+    ]
+    for r, part, source, block in plan:
+        target = pl.ds(pl.multiple_of((chip ^ r) * (2 * count) + part * count, 16), count)
+        start = 0
+        for out_ref in out_refs:
+            stop = start + out_ref.shape[1]
+            out_ref[target, :] = source[block * count : (block + 1) * count, start:stop]
+            start = stop
+
+
+def dot(left, right, left_dim=1, right_dim=0):
+    return lax.dot_general(
+        left, right, (((left_dim,), (right_dim,)), ((), ())), preferred_element_type=jnp.float32
+    )
+
+
+def join_rows(pieces, target):
+    start = 0
+    for piece in pieces:
+        target[start : start + piece.shape[0], :] = piece[...]
+        start += piece.shape[0]
+
+
+def attend_probs(query, key, scale):
+    scores = dot(query, key, 1, 1) * scale
+    top = jnp.max(scores, axis=1, keepdims=True)
+    total = jnp.log(jnp.sum(jnp.exp(scores - top), axis=1, keepdims=True)) + top
+    return jnp.exp(scores - total)
+
+
+def attend_forward_body(heads, scale, chip_ref, *refs):
+    pieces, mod_ref, bias_ref, parts = refs[:3], refs[3], refs[4], refs[5:10]
+    rows_ref, normed_ref, qkv_ref, mixed_ref, attend_ref, output_ref = refs[10:16]
+    partials, joined = refs[16:18], refs[18]
+    place_rows(chip_ref[0], parts, (attend_ref, output_ref))
+    join_rows(pieces, joined)
+    seq = joined.shape[0] // 2
+    model_width = joined.shape[1]
+    width = output_ref.shape[1]
+    for n in (1, 0):
+        rows = slice(n * seq, (n + 1) * seq)
+        normed, _ = normalize(joined[rows, :].astype(jnp.float32))
+        normed_ref[rows, :] = normed
+        shift = mod_ref[n : n + 1, :model_width]
+        gain = mod_ref[n : n + 1, model_width : 2 * model_width]
+        attend_in = (normed * (1.0 + gain) + shift).astype(jnp.bfloat16)
+        rows_ref[rows, :] = attend_in
+        qkv_ref[rows, :] = (dot(attend_in, attend_ref[...]) + bias_ref[...]).astype(jnp.bfloat16)
+        mixed = []
+        for head in range(heads):
+            query, key, value = (
+                qkv_ref[rows, j * width + head * HD : j * width + (head + 1) * HD]
+                for j in range(3)
+            )
+            probs = attend_probs(query, key, scale).astype(jnp.bfloat16)
+            mixed.append(dot(probs, value))
+        mixed = jnp.concatenate(mixed, axis=1).astype(jnp.bfloat16)
+        mixed_ref[rows, :] = mixed
+        partials[n][...] = dot(mixed, output_ref[...], 1, 1)
+
+
+def kernel_call(body, name, outs, operands, scratch, limit, flops, transcendentals=0):
+    specs = [
+        pl.BlockSpec(memory_space=pltpu.SMEM if x.dtype == jnp.int32 else pltpu.VMEM)
+        for x in operands
+    ]
+    shapes = [jax.ShapeDtypeStruct(*out) for out in outs]
+    moved = sum(x.size * x.dtype.itemsize for x in list(operands) + shapes)
+    return pl.pallas_call(
+        body,
+        out_shape=shapes,
+        in_specs=specs,
+        out_specs=[pl.BlockSpec(memory_space=pltpu.VMEM)] * len(outs),
+        scratch_shapes=scratch,
+        compiler_params=pltpu.CompilerParams(vmem_limit_bytes=limit * 2**20),
+        cost_estimate=pl.CostEstimate(
+            flops=flops, bytes_accessed=moved, transcendentals=transcendentals
+        ),
+        name=name,
+    )(*operands)
+
+
+def attend_forward(chip, pieces, mod_full, bias_rows, parts, heads, scale):
+    seq = pieces[-1].shape[0]
+    rows, model_width = 2 * seq, pieces[0].shape[1]
+    width = heads * HD
+    return kernel_call(
+        functools.partial(attend_forward_body, heads, scale),
+        "attend_forward",
+        [
+            ((rows, model_width), jnp.bfloat16),
+            ((rows, model_width), jnp.float32),
+            ((rows, 3 * width), jnp.bfloat16),
+            ((rows, width), jnp.bfloat16),
+            ((model_width, 3 * width), jnp.bfloat16),
+            ((model_width, width), jnp.bfloat16),
+            ((seq, model_width), jnp.float32),
+            ((seq, model_width), jnp.float32),
+        ],
+        [chip.reshape(1), *pieces, mod_full, bias_rows, *parts],
+        [pltpu.VMEM((rows, model_width), jnp.bfloat16)],
+        20,
+        2 * rows * model_width * 4 * width + 8 * seq * seq * width,
+        2 * 2 * heads * seq * seq,
+    )
+
+
+def feed_forward_body(chip_ref, *refs):
+    pieces, ups, mod_ref, bias_ref, parts = refs[:4], refs[4:7], refs[7], refs[8], refs[9:14]
+    act_ref, sums_ref, reduce_ref = refs[14:17]
+    partials, blocks, expand_ref, joined = refs[17:19], refs[19:23], refs[23], refs[24]
+    rows_ref, back_ref, low_ref, grad_ref = refs[25:29]
+    place_rows(chip_ref[0], parts, (expand_ref, reduce_ref))
+    join_rows(pieces, rows_ref)
+    join_rows(ups, joined)
+    seq = joined.shape[0] // 2
+    model_width = joined.shape[1]
+    sums = None
+    for n in (1, 0):
+        rows = slice(n * seq, (n + 1) * seq)
+        value = dot(rows_ref[rows, :], expand_ref[...]) + bias_ref[...]
+        gate = mod_ref[n : n + 1, 5 * model_width : 6 * model_width]
+        back = (joined[rows, :].astype(jnp.float32) * gate).astype(jnp.bfloat16)
+        back_ref[rows, :] = back
+        grad_act = dot(back, reduce_ref[...])
+        square = value * value
+        slope = math.sqrt(2.0 / math.pi)
+        bent = jnp.tanh(slope * (value + 0.044715 * (square * value)))
+        share = 0.5 * (1.0 + bent)
+        act_ref[rows, :] = (value * share).astype(jnp.bfloat16)
+        curve = 0.5 * value * (1.0 - bent * bent) * (slope * (1.0 + 3 * 0.044715 * square))
+        grad_pre = grad_act * (share + curve)
+        part = jnp.sum(grad_pre, axis=0, keepdims=True)
+        sums = part if sums is None else sums + part
+        low = grad_pre.astype(jnp.bfloat16)
+        low_ref[rows, :] = low
+        partials[n][...] = dot(low, expand_ref[...], 1, 1)
+    sums_ref[...] = sums
+    width = act_ref.shape[1]
+    grad_ref[:, :width] = dot(rows_ref[...], low_ref[...], 0, 0)
+    grad_ref[:, width:] = dot(back_ref[...], act_ref[...], 0, 0)
+    write_blocks(chip_ref[0], grad_ref, blocks)
+
+
+def feed_forward(chip, pieces, ups, mod_full, bias, parts):
+    seq = ups[-1].shape[0]
+    rows, model_width = 2 * seq, pieces[0].shape[1]
+    width = bias.shape[1]
+    return kernel_call(
+        feed_forward_body,
+        "feed_forward",
+        [
+            ((rows, width), jnp.bfloat16),
+            ((1, width), jnp.float32),
+            ((model_width, width), jnp.bfloat16),
+            ((seq, model_width), jnp.float32),
+            ((seq, model_width), jnp.float32),
+        ]
+        + block_shapes(model_width, 2 * width),
+        [chip.reshape(1), *pieces, *ups, mod_full, bias, *parts],
+        [
+            pltpu.VMEM((model_width, width), jnp.bfloat16),
+            pltpu.VMEM((rows, model_width), jnp.bfloat16),
+            pltpu.VMEM((rows, model_width), jnp.bfloat16),
+            pltpu.VMEM((rows, model_width), jnp.bfloat16),
+            pltpu.VMEM((rows, width), jnp.bfloat16),
+            pltpu.VMEM((model_width, 2 * width), jnp.float32),
+        ],
+        36,
+        10 * rows * model_width * width,
+        rows * width,
+    )
+
+
+def write_blocks(chip, grad_ref, out_refs):
+    keep_first, keep_second, send_first, send_second = out_refs
+    count = keep_first.shape[0] // 2
+    plan = [
+        (keep_first, 0, (0, 2)),
+        (keep_second, 1, (0, 1)),
+        (send_first, 0, (1, 3)),
+        (send_second, 1, (2, 3)),
+    ]
+    for out_ref, part, places in plan:
+        for block, r in enumerate(places):
+            source = pl.ds(pl.multiple_of((chip ^ r) * (2 * count) + part * count, 8), count)
+            out_ref[block * count : (block + 1) * count, :] = grad_ref[source, :].astype(
+                out_ref.dtype
+            )
+
+
+def block_shapes(height, width):
+    shape = (height // 4, width)
+    return [(shape, jnp.float32)] * 2 + [(shape, jnp.bfloat16)] * 2
+
+
+def grad_blocks_body(chip_ref, *refs):
+    out_refs, grad_ref = refs[-5:-1], refs[-1]
+    start = 0
+    for rows, cols in zip(refs[:-5:2], refs[1:-5:2]):
+        stop = start + cols.shape[1]
+        grad_ref[:, start:stop] = dot(rows[...], cols[...], 0, 0)
+        start = stop
+    write_blocks(chip_ref[0], grad_ref, out_refs)
+
+
+def grad_blocks(pairs, chip):
+    height = pairs[0][0].shape[1]
+    width = sum(cols.shape[1] for _, cols in pairs)
+    return kernel_call(
+        grad_blocks_body,
+        "grad_blocks",
+        block_shapes(height, width),
+        [chip.reshape(1)] + [part for pair in pairs for part in pair],
+        [pltpu.VMEM((height, width), jnp.float32)],
+        16,
+        sum(2 * rows.size * cols.shape[1] for rows, cols in pairs),
+    )
+
+
+def first_step(sends):
+    return [swap(sends[0], "dp", 2), swap(sends[1], "dp", 4)]
+
+
+def middle_body(keep_first, keep_second, got_first, got_second, *outs):
+    count = keep_first.shape[0] // 2
+    for keep, got, base, going in (
+        (keep_first, got_first, outs[0], outs[2]),
+        (keep_second, got_second, outs[1], outs[3]),
+    ):
+        total = keep[...] + got[...].astype(jnp.float32)
+        base[...] = total[:count]
+        going[...] = total[count:].astype(jnp.bfloat16)
+
+
+def middle_step(keeps, received):
+    rows, width = keeps[0].shape
+    shape = (rows // 2, width)
+    outs = [(shape, jnp.float32)] * 2 + [(shape, jnp.bfloat16)] * 2
+    return kernel_call(middle_body, "middle_step", outs, [*keeps, *received], [], 16, 0)
+
+
+def second_step(going):
+    return [swap(going[0], "dp", 4), swap(going[1], "dp", 2)]
+
+
+def core_body(core_ref, base_first, base_second, got_first, got_second, mine, other):
+    first = base_first[...] + got_first[...].astype(jnp.float32)
+    second = base_second[...] + got_second[...].astype(jnp.float32)
+    is_first = core_ref[0] == 0
+    mine[...] = jnp.where(is_first, first, second)
+    other[...] = jnp.where(is_first, second, first)
+
+
+def core_step(core, bases, received):
+    outs = [(bases[0].shape, jnp.float32)] * 2
+    operands = [core.reshape(1), *bases, *received]
+    return kernel_call(core_body, "core_step", outs, operands, [], 12, 0)
+
+
+def half_body(own_ref, mine, other, kept, sent):
+    is_own = own_ref[0] == 1
+    kept[...] = jnp.where(is_own, mine[...], other[...])
+    sent[...] = jnp.where(is_own, other[...], mine[...]).astype(jnp.bfloat16)
+
+
+def half_step(is_own, mine, other):
+    outs = [(mine.shape, jnp.float32), (mine.shape, jnp.bfloat16)]
+    operands = [is_own.astype(jnp.int32).reshape(1), mine, other]
+    return kernel_call(half_body, "half_step", outs, operands, [], 12, 0)
+
+
+def pack_body(norm, got, gate_a, shift_m, scale_m, gate_m, out_b, red_b, expand, bias, packed):
+    wide = gate_a.shape[1]
+    part = packed.shape[1] - wide
+    packed[...] = jnp.zeros_like(packed)
+    both = norm[0:1, :] + got[...]
+    packed[0:1, :wide] = both[:, :wide]
+    packed[0:1, wide:] = both[:, wide : wide + part]
+    packed[1:2, : wide - part] = both[:, wide + part :]
+    packed[1:2, wide - part :] = gate_a[...]
+    packed[2:3, :wide] = shift_m[...]
+    packed[2:3, wide:] = scale_m[:, :part]
+    packed[3:4, : wide - part] = scale_m[:, part:]
+    packed[3:4, wide - part :] = gate_m[...]
+    packed[4:5, :wide] = out_b[...]
+    packed[4:5, wide:] = red_b[:, :part]
+    packed[5:6, : wide - part] = red_b[:, part:]
+    heads = bias.shape[1] // 3
+    packed[6:7, :wide] = expand[...]
+    packed[6:7, wide : wide + heads] = bias[:, :heads]
+    packed[6:7, wide + heads : wide + 2 * heads] = bias[:, 2 * heads :]
+
+
+def choose_body(place_ref, line, far, packed):
+    z, half, own = place_ref[0], place_ref[1], place_ref[2]
+    packed[pl.ds(half, 1), :] = line[pl.ds(z, 1), :]
+    packed[pl.ds(1 - half, 1), :] = far[pl.ds(z, 1), :]
+    packed[2:3, :] = jnp.where(own == 1, line[6:7, :] + far[6:7, :], 0.0)
+    packed[3:5, :] = line[4:6, :] + far[4:6, :]
+
+
+def modulation_back_body(gathered, silu, weight, weight_grad, grad_silu, bias_grad, rest, rows):
+    parts = [gathered[m] for m in range(gathered.shape[0])]
+    for m, part in enumerate(parts):
+        rows[2 * m : 2 * m + 2, :] = part[0:2, :]
+    low = rows[...].astype(jnp.bfloat16)
+    weight_grad[...] = dot(silu[...], low, 0, 0)
+    grad_silu[...] = dot(low, weight[...], 1, 1)
+    while len(parts) > 1:
+        parts = [left + right for left, right in zip(parts[::2], parts[1::2])]
+    bias_grad[...] = parts[0][0:1, :] + parts[0][1:2, :]
+    rest[...] = parts[0][2:5, :]
+
+
+def table_body(labels, cond, near, far, table):
+    value = cond[...]
+    share = 1.0 / (1.0 + jnp.exp(-value))
+    grad = (near[...] + far[...]) * share * (1.0 + value * (1.0 - share))
+    table[...] = jnp.zeros_like(table)
+    for row in range(grad.shape[0]):
+        place = pl.ds(labels[row], 1)
+        table[place, :] = table[place, :] + grad[row : row + 1, :]
+
+
+def attend_back_body(heads, scale, *refs):
+    pieces = refs[:4]
+    output_ref, qkv_ref, mixed_ref, attend_ref, normed_ref = refs[4:9]
+    rows_ref, low_ref, sums_ref, norm_sums_ref = refs[9:13]
+    partials = refs[13:15]
+    join_rows(pieces, rows_ref)
+    seq = rows_ref.shape[0] // 2
+    model_width, width = output_ref.shape
+    sums = None
+    for n in (1, 0):
+        rows = slice(n * seq, (n + 1) * seq)
+        grad_mixed = dot(rows_ref[rows, :], output_ref[...]).astype(jnp.bfloat16)
+        grads = [[], [], []]
+        for head in range(heads):
+            query, key, value = (
+                qkv_ref[rows, j * width + head * HD : j * width + (head + 1) * HD]
+                for j in range(3)
+            )
+            mixed = mixed_ref[rows, head * HD : (head + 1) * HD]
+            up = grad_mixed[:, head * HD : (head + 1) * HD]
+            probs = attend_probs(query, key, scale)
+            delta = jnp.sum(
+                up.astype(jnp.float32) * mixed.astype(jnp.float32), axis=1, keepdims=True
+            )
+            logit = (probs * (dot(up, value, 1, 1) - delta)).astype(jnp.bfloat16)
+            grads[0].append(dot(logit, key) * scale)
+            grads[1].append(dot(logit, query, 0, 0) * scale)
+            grads[2].append(dot(probs.astype(jnp.bfloat16), up, 0, 0))
+        whole = jnp.concatenate([part for group in grads for part in group], axis=1)
+        part = jnp.sum(whole, axis=0, keepdims=True)
+        sums = part if sums is None else sums + part
+        low = whole.astype(jnp.bfloat16)
+        low_ref[rows, :] = low
+        partial = dot(low, attend_ref[...], 1, 1)
+        partials[n][...] = partial
+        norm_sums_ref[n : n + 1, :model_width] = jnp.sum(partial, axis=0, keepdims=True)
+        norm_sums_ref[n : n + 1, model_width:] = jnp.sum(
+            partial * normed_ref[rows, :], axis=0, keepdims=True
+        )
+    sums_ref[...] = sums
+
+
+def attend_back(pieces, output_full, qkv, mixed, attend_full, normed, heads, scale):
+    rows, model_width = normed.shape
+    seq, width = rows // 2, mixed.shape[1]
+    return kernel_call(
+        functools.partial(attend_back_body, heads, scale),
+        "attend_back",
+        [
+            ((rows, model_width), jnp.bfloat16),
+            ((rows, 3 * width), jnp.bfloat16),
+            ((1, 3 * width), jnp.float32),
+            ((2, 2 * model_width), jnp.float32),
+            ((seq, model_width), jnp.float32),
+            ((seq, model_width), jnp.float32),
+        ],
+        [*pieces, output_full, qkv, mixed, attend_full, normed],
+        [],
+        20,
+        2 * rows * model_width * 4 * width + 20 * seq * seq * width,
+        2 * 2 * heads * seq * seq,
+    )
+
+
+def on_paired_device(
+    tokens,
+    cotangent,
+    labels,
+    timesteps,
+    class_table,
+    modulation_weight,
+    modulation_bias,
+    attend_weight,
+    attend_bias,
+    output_weight,
+    output_bias,
+    expand_weight,
+    expand_bias,
+    reduce_weight,
+    reduce_bias,
+):
+    data_index = lax.axis_index("dp")
+    tensor_index = lax.axis_index("tensor")
+    core, chip = data_index & 1, data_index >> 1
+    half = tensor_index >> 1
+    is_own = half == core
+    model_width = tokens.shape[2]
+    row_share = modulation_weight.shape[0]
+    head_width = attend_weight.shape[2]
+    head_count = head_width // HD
+    ff_width = expand_weight.shape[1]
+    mod_width = modulation_weight.shape[1]
+    latent_total = labels.shape[0]
+    classes_total = class_table.shape[0]
+    score_scale = 1.0 / math.sqrt(HD)
+
+    slot = jnp.arange(latent_total, dtype=jnp.int32)
+    latent_ids = ((slot >> 1) ^ data_index) * 2 + (slot & 1)
+    chosen = latent_ids[:, None] == slot[None, :]
+    labels_rel = jnp.sum(jnp.where(chosen, labels[None, :], 0), axis=1)
+    steps_rel = jnp.sum(jnp.where(chosen, timesteps[None, :], 0), axis=1)
+    looked = lax.dynamic_slice_in_dim(
+        jnp.take(class_table, labels_rel, axis=0), data_index * row_share, row_share, 1
+    ).astype(jnp.float32)
+    halfway = model_width // 2
+    column = data_index * row_share + jnp.arange(row_share, dtype=jnp.int32)
+    is_cos = column < halfway
+    place = jnp.where(is_cos, column, column - halfway).astype(jnp.float32)
+    frequency = jnp.exp(-math.log(10000.0) * place / halfway)
+    angles = steps_rel.astype(jnp.float32)[:, None] * frequency[None, :]
+    cond = looked + jnp.where(is_cos[None, :], jnp.cos(angles), jnp.sin(angles))
+    silu_act = jax.nn.silu(cond).astype(jnp.bfloat16)
+    partial = jnp.dot(silu_act, modulation_weight, preferred_element_type=jnp.float32)
+    attn_shard = jnp.concatenate([attend_weight.reshape(row_share, -1), output_weight], axis=1)
+    attn_far = swap(attn_shard, "tensor", 2)
+    attn_share = near_weight(attn_shard, attn_far, is_own, core)
+    partial = partial[:8] + swap(partial[8:], "dp", 4)
+    partial = partial[:4] + swap(after(partial, attn_far)[4:], "dp", 2)
+    crossed = swap(after(partial, attn_share), "dp", 1)
+    bias_vec = jnp.concatenate([attend_bias.reshape(-1), expand_bias])
+    mod_cols = jnp.concatenate(
+        [
+            partial + jnp.concatenate([crossed[2:], crossed[:2]]) + modulation_bias,
+            bias_vec[None],
+        ]
+    )
+    mod_near = jnp.stack([mod_cols, swap(mod_cols, "tensor", 1)])
+    mod_far = swap(mod_near, "tensor", 2)
+    mod_parts = [mod_near[0], mod_near[1], mod_far[0], mod_far[1]]
+    mod_full = jnp.concatenate(
+        unxor([jnp.where(half == 0, m[0:4:2], m[1:4:2]) for m in mod_parts], tensor_index), axis=1
+    )
+    bias_vec = jnp.where(is_own, bias_vec, mod_parts[2][4])
+    pieces = mod_full.reshape(2, 6, 1, model_width)
+    own_pieces = pieces[0]
+
+    tokens_half = exchange_latents(after(tokens, attn_shard), half)
+    own_rows = tokens_half.shape[0]
+    tokens_near = swap(tokens_half, "tensor", 1)
+    tokens_across = swap(jnp.concatenate([tokens_half, tokens_near]), "dp", 1)
+    tokens_own = tokens_half.astype(jnp.float32)
+
+    attn_parts = chip_rows(attn_share)
+    ff_shard = after(
+        jnp.concatenate([expand_weight, reduce_weight], axis=1), attn_far, tokens_half
+    )
+    ff_far = swap(ff_shard, "tensor", 2)
+    ff_share = near_weight(ff_shard, ff_far, is_own, core)
+    ff_parts = chip_rows(after(ff_share, *attn_parts))
+
+    upstream_half = exchange_latents(after(cotangent, mod_far), half)
+    upstream_near = swap(upstream_half, "tensor", 1)
+    upstream_across = swap(jnp.concatenate([upstream_half, upstream_near]), "dp", 1)
+    upstream = upstream_half.astype(jnp.float32)
+    query_bias = bias_vec[:head_width]
+    value_bias = bias_vec[head_width : 2 * head_width]
+    expand_bias_q = bias_vec[2 * head_width :]
+
+    bias_rows = jnp.concatenate([query_bias, jnp.zeros_like(query_bias), value_bias])[None]
+    (
+        attend_rows,
+        normed_all,
+        projected,
+        mixed_rows,
+        attend_full,
+        output_full,
+        own_partial,
+        other_partial,
+    ) = attend_forward(
+        chip,
+        [tokens_half, tokens_near, tokens_across],
+        mod_full,
+        bias_rows,
+        attn_parts,
+        head_count,
+        score_scale,
+    )
+    attend_out = spread_pairs(own_partial, other_partial) + output_bias
+    normed_first, inverse_first = normalize(tokens_own)
+    residual = tokens_own + own_pieces[2] * attend_out
+    normed_second, inverse_second = normalize(residual)
+    hidden_in = (normed_second * (1.0 + own_pieces[4]) + own_pieces[3]).astype(jnp.bfloat16)
+    hidden_pieces = collect_pairs(hidden_in)
+
+    (
+        activated,
+        grad_expand_bias,
+        reduce_full,
+        own_partial,
+        other_partial,
+        *ff_blocks,
+    ) = feed_forward(
+        chip,
+        hidden_pieces,
+        [upstream_half, upstream_near, upstream_across],
+        mod_full,
+        expand_bias_q[None],
+        ff_parts,
+    )
+    ff_first = first_step(ff_blocks[2:])
+    grad_reduce_bias = jnp.sum(upstream * own_pieces[5], axis=0, keepdims=True)
+    seq_len = tokens_across.shape[0]
+    hidden_sum = own_partial + swap(other_partial, "dp", 1)
+    grad_hidden_in = spread_rows(hidden_sum)
+    act_later = after(activated, own_partial)
+    other_out, own_out = (
+        jnp.einsum("sf,of->so", act_half, reduce_full, preferred_element_type=jnp.float32)
+        for act_half in (act_later[seq_len:], act_later[:seq_len])
+    )
+    out_sum = own_out + swap(other_out, "dp", 1)
+
+    grad_shift_hidden = jnp.sum(grad_hidden_in, axis=0, keepdims=True)
+    grad_scale_hidden = jnp.sum(grad_hidden_in * normed_second, axis=0, keepdims=True)
+    grad_residual = upstream + norm_back(
+        grad_hidden_in * (1.0 + own_pieces[4]), normed_second, inverse_second
+    )
+    grad_gate_attend = jnp.sum(grad_residual * attend_out, axis=0, keepdims=True)
+    output_term = grad_residual * own_pieces[2]
+    grad_output_bias = jnp.sum(output_term, axis=0, keepdims=True)
+    output_pieces = collect_pairs(output_term.astype(jnp.bfloat16))
+    *ff_bases, ff_going, ff_going_second = middle_step(ff_blocks[:2], after(ff_first, output_term))
+    ff_second = second_step([ff_going, ff_going_second])
+    hidden_out = spread_rows(after(out_sum, output_term)) + reduce_bias
+    block_own = (residual + own_pieces[5] * hidden_out).astype(jnp.bfloat16)
+    grad_gate_hidden = jnp.sum(upstream * hidden_out, axis=0, keepdims=True)
+
+    (
+        output_rows,
+        projected_low,
+        bias_sums,
+        norm_sums,
+        own_partial,
+        other_partial,
+    ) = attend_back(
+        after(output_pieces, out_sum, ff_going),
+        output_full,
+        projected,
+        mixed_rows,
+        attend_full,
+        normed_all,
+        head_count,
+        score_scale,
+    )
+    attend_sum = own_partial + swap(other_partial, "dp", 1)
+    norm_crossed = swap(norm_sums[1:], "dp", 1)
+    grad_attend_in = spread_rows(attend_sum)
+    attn_blocks = grad_blocks(
+        [(attend_rows, after(projected_low, norm_crossed)), (output_rows, mixed_rows)], chip
+    )
+    attn_first = first_step(attn_blocks[2:])
+    tokens_grad_own = grad_residual + norm_back(
+        grad_attend_in * (1.0 + own_pieces[1]), normed_first, inverse_first
+    )
+
+    count = tokens_grad_own.shape[0] // 2
+    far = swap(
+        jnp.concatenate([block_own[count:], tokens_grad_own[count:].astype(jnp.bfloat16)]),
+        "tensor",
+        2,
+    )
+    block_output, tokens_grad = (
+        jnp.where(half == 0, jnp.stack([own, moved]), jnp.stack([moved, own]))
+        for own, moved in (
+            (block_own[:count], far[:count]),
+            (tokens_grad_own[:count], far[count:].astype(jnp.float32)),
+        )
+    )
+
+    line = kernel_call(
+        pack_body,
+        "pack",
+        [((8, mod_width), jnp.float32)],
+        [
+            norm_sums,
+            norm_crossed,
+            grad_gate_attend,
+            grad_shift_hidden,
+            grad_scale_hidden,
+            grad_gate_hidden,
+            grad_output_bias,
+            grad_reduce_bias,
+            grad_expand_bias,
+            bias_sums,
+        ],
+        [],
+        4,
+        0,
+    )[0]
+    summed = lax.broadcasted_iota(jnp.int32, line.shape, 0) < 6
+    line = line + jnp.where(summed, swap(line, "tensor", 1), 0.0)
+    far = swap(line, "tensor", 2)
+    ff_mine, ff_other = core_step(core, ff_bases, ff_second)
+    ff_kept, ff_sent = half_step(is_own, ff_mine, swap(ff_other, "dp", 1))
+    ff_moved = swap(after(ff_sent, far), "tensor", 2)
+    place = jnp.stack([tensor_index, half, is_own.astype(jnp.int32)])
+    packed = kernel_call(
+        choose_body, "choose", [((5, mod_width), jnp.float32)], [place, line, far], [], 4, 0
+    )[0][None]
+    packed = jnp.concatenate([packed, swap(packed, "dp", 1)], axis=0)
+    *attn_bases, attn_going, attn_going_second = middle_step(attn_blocks[:2], attn_first)
+    packed = after(packed, attn_going, grad_attend_in, ff_sent)
+    packed = jnp.concatenate([packed, swap(packed, "dp", 2)], axis=0)
+    attn_second = second_step([attn_going, attn_going_second])
+    packed = jnp.concatenate([packed, swap(packed, "dp", 4)], axis=0)
+    modulation_weight_grad, grad_silu, modulation_bias_grad, rest = kernel_call(
+        modulation_back_body,
+        "modulation_back",
+        [
+            ((row_share, mod_width), jnp.float32),
+            ((latent_total, row_share), jnp.float32),
+            ((1, mod_width), jnp.float32),
+            ((3, mod_width), jnp.float32),
+        ],
+        [packed, silu_act, modulation_weight],
+        [pltpu.VMEM((latent_total, mod_width), jnp.float32)],
+        8,
+        4 * latent_total * row_share * mod_width,
+    )
+    attn_mine, attn_other = core_step(core, attn_bases, attn_second)
+    grad_silu = after(grad_silu, attn_mine, tokens_grad_own)
+    near = grad_silu + swap(grad_silu, "tensor", 1)
+    attn_kept, attn_sent = half_step(is_own, attn_mine, swap(attn_other, "dp", 1))
+    attn_grad = attn_kept + swap(attn_sent, "tensor", 2).astype(jnp.float32)
+    ff_grad = ff_kept + after(ff_moved, near).astype(jnp.float32)
+    table_grad = kernel_call(
+        table_body,
+        "table",
+        [((classes_total, row_share), jnp.float32)],
+        [labels_rel, cond, near, swap(near, "tensor", 2)],
+        [],
+        4,
+        0,
+    )[0]
+    wide = model_width
+    return (
+        block_output,
+        tokens_grad,
+        table_grad,
+        modulation_weight_grad,
+        modulation_bias_grad[0],
+        attn_grad[:, : 3 * head_width].reshape(row_share, 3, head_width),
+        rest[0, wide:].reshape(2, head_width),
+        attn_grad[:, 3 * head_width :],
+        rest[1, :wide],
+        ff_grad[:, :ff_width],
+        rest[0, :wide],
+        ff_grad[:, ff_width:],
+        jnp.concatenate([rest[1, wide:], rest[2, : 2 * wide - mod_width]]),
+    )
+
+
 def solution(mesh):
+    paired = mesh.shape["dp"] == 8 and mesh.shape["tensor"] == 4
+    per_device = on_paired_device if paired else on_device
     placed = (
         P("dp", "tensor", None),
         P("dp", "tensor", None),
@@ -335,7 +1086,7 @@
         P(),
     )
     return jax.shard_map(
-        on_device,
+        per_device,
         mesh=mesh,
         in_specs=placed,
         out_specs=(

time: 603 us -> 211 us (0.35)
  blocking collectives: 227 us -> 0 us
  waiting for transfers between devices: 280 us -> 93.9 us
  starting transfers between devices: 0.53 us -> 48 us
  matrix products: 40.7 us -> 3.18 us
  Pallas kernels: 0 us -> 18 us
  between operations: 14.4 us -> 1.68 us
    reduce_scatter x9 -> x0, waiting for transfers between devices: 217 us -> none  [the longest x4 114 us: spread(): lax.psum_scatter(partial_rows, 'tensor', scatter_dimension=1, tiled=True)]
    all_gather x8 -> x0, blocking collectives: 188 us -> none  [the longest x4 81.4 us: collect(): return lax.all_gather(local_rows, 'tensor', axis=1, tiled=True)]
    ppermute x0 -> x58, waiting for transfers between devices: none -> 93.9 us  [swap(): lax.ppermute(values, axis, [(place, place ^ mask) for place in range(coun...]
    ppermute x0 -> x58, starting transfers between devices: none -> 48 us  [swap(): lax.ppermute(values, axis, [(place, place ^ mask) for place in range(coun...]
    psum x1 -> x0, blocking collectives: 38.4 us -> none  [on_device(): lax.psum((padded_attend, padded_expand, padded_modulation, grad_output_bi...]
    dot_general x22 -> x3, matrix products: 40.7 us -> 3.18 us  [the longest x2 2.09 us: on_paired_device(): jnp.einsum('sf,of->so', act_half, reduce_full, preferred_element_type=jnp...]
    unnamed x14 -> x0, waiting for transfers between devices: 33.6 us -> none
    all_gather x3 -> x0, waiting for transfers between devices: 28.7 us -> none  [the longest x1 22.3 us: on_device(): lax.all_gather(reduce_weight, 'dp', axis=0, tiled=True)]
  transfers between devices with their start and end apart: 13 -> 58, of which waited for: 11 -> 27; matrix products, arithmetic and copies ran while one was open for 8% -> 18% of each run, Pallas kernels for 0% -> 4%
where the time goes in v2:
time: 211 us; the launch traced here: 210 us
  waiting for transfers between devices  93.9 us (45%)
  starting transfers between devices  48 us (23%)
  local copies, waits for them, and re-layouts  26.9 us (13%)
  other arithmetic  18 us (9%)
  Pallas kernels  18 us (9%)
  matrix products  3.18 us (2%)
    ppermute x58, waiting for transfers between devices, swap(): lax.ppermute(values, axis, [(place, place ^ mask) for place in range(coun...  93.9 us
    ppermute x58, starting transfers between devices, swap(): lax.ppermute(values, axis, [(place, place ^ mask) for place in range(coun...  48 us
    pallas_call x14, Pallas kernels, kernel_call(): pl.pallas_call(body, out_shape=shapes, in_specs=specs, out_specs=[pl.Bloc...  18 us
    unnamed x102, local copies, waits for them, and re-layouts  7.87 us
  transfers between devices with their start and end apart: 58, of which 27 were waited for; matrix products, arithmetic and copies ran while one was open for 18% of the time, Pallas kernels for 4%

profile of v2, /device:TPU:0, one launch (start us, length us, event | category | flops | bytes accessed | tf_op | source)
XLA Modules:
  0.0 209.7 jit_solution(14720542805522355489)
XLA Ops:
  3.9 3.0 %collective-permute-start.1 = (f32[8,1152]{1,0:T(8,128)S(1)}, f32[8,1152]{1,0:T(8,128)S(1)}, u32[]{:S(2)}, u32[]{:S(2)}) collective-permute-start(f32[8,1152]{1,0:T(8,128)S(1)} %slice.242), channel_id=1, source_target_pairs={{0,16},{4,20},{8,24},{12,28},{16,0},{20,4},{24,8},{28,12},{1,17},{... | collective-permute-start | bytes 110600 | tf_op jit(solution)/shard_map/ppermute | solution.py:324
  8.3 2.7 %collective-permute-start.2 = (bf16[96,768]{1,0:T(8,128)(2,1)S(1)}, bf16[96,768]{1,0:T(8,128)(2,1)S(1)}, u32[]{:S(2)}, u32[]{:S(2)}) collective-permute-start(bf16[96,768]{1,0:T(8,128)(2,1)S(1)} %pad_maximum_fusion.13), channel_id=1, source_target_pairs={{0,2},{1,3},{2,0},{3,1},{4,6},{5,7},{6,4},{7,5},{8,10},{9,11},{10,... | collective-permute-start | bytes 442376 | tf_op jit(solution)/shard_map/ppermute | solution.py:324
  12.2 9.7 %collective-permute-done = bf16[64,768]{1,0:T(8,128)(2,1)S(1)} collective-permute-done((bf16[64,768]{1,0:T(8,128)(2,1)S(1)}, bf16[64,768]{1,0:T(8,128)(2,1)S(1)}, u32[]{:S(2)}, u32[]{:S(2)}) %collective-permute-start) | collective-permute-done | bytes 98336 | tf_op jit(solution)/shard_map/ppermute | solution.py:324
  22.8 1.6 collective-permute-start.3
  26.6 3.9 %collective-permute-done.11.refs_7_ = bf16[96,768]{1,0:T(8,128)(2,1)S(1)} collective-permute-done((bf16[96,768]{1,0:T(8,128)(2,1)S(1)}, bf16[96,768]{1,0:T(8,128)(2,1)S(1)}, u32[]{:S(2)}, u32[]{:S(2)}) %collective-permute-start.11) | collective-permute-done | bytes 147488 | tf_op jit(solution)/shard_map/ppermute | solution.py:324
  32.3 3.4 %collective-permute-start.22 = (bf16[96,1536]{1,0:T(8,128)(2,1)S(1)}, bf16[96,1536]{1,0:T(8,128)(2,1)S(1)}, u32[]{:S(2)}, u32[]{:S(2)}) collective-permute-start(bf16[96,1536]{1,0:T(8,128)(2,1)S(1)} %pad_maximum_fusion.8), channel_id=1, source_target_pairs={{0,2},{1,3},{2,0},{3,1},{4,6},{5,7},{6,4},{7,5},{8,10},{9,11},{10,... | collective-permute-start | bytes 884744 | tf_op jit(solution)/shard_map/ppermute | solution.py:324
  35.9 7.4 %collective-permute-done.8.refs_1_ = bf16[128,768]{1,0:T(8,128)(2,1)S(1)} collective-permute-done((bf16[128,768]{1,0:T(8,128)(2,1)S(1)}, bf16[128,768]{1,0:T(8,128)(2,1)S(1)}, u32[]{:S(2)}, u32[]{:S(2)}) %collective-permute-start.8) | collective-permute-done | bytes 196640 | tf_op jit(solution)/shard_map/ppermute | solution.py:324
  45.0 4.1 %collective-permute-start.7 = (f32[2,5,1152]{2,1,0:T(8,128)}, f32[2,5,1152]{2,1,0:T(8,128)}, u32[]{:S(2)}, u32[]{:S(2)}) collective-permute-start(f32[2,5,1152]{2,1,0:T(8,128)} %pad_maximum_fusion.15), channel_id=1, source_target_pairs={{0,2},{1,3},{2,0},{3,1},{4,6},{5,7},{6,4},{7,5},{8,10},{9,11},{10,... | collective-permute-start | bytes 138248 | tf_op jit(solution)/shard_map/ppermute | solution.py:324
  51.0 1.5 collective-permute-start.12
  53.7 1.4 slice.201
  55.1 1.4 slice.200
  56.5 1.4 slice_bitcast_fusion.5
  57.9 1.4 slice.194
  59.2 1.4 slice.193
  65.5 6.0 %collective-permute-done.19 = bf16[64,768]{1,0:T(8,128)(2,1)S(1)} collective-permute-done((bf16[64,768]{1,0:T(8,128)(2,1)S(1)}, bf16[64,768]{1,0:T(8,128)(2,1)S(1)}, u32[]{:S(2)}, u32[]{:S(2)}) %collective-permute-start.19) | collective-permute-done | bytes 98336 | tf_op jit(solution)/shard_map/ppermute | solution.py:324
  74.4 3.0 %attend_forward.1 = (bf16[512,768]{1,0:T(8,128)(2,1)S(1)}, f32[512,768]{1,0:T(8,128)S(1)}, bf16[512,576]{1,0:T(8,128)(2,1)S(1)}, bf16[512,192]{1,0:T(8,128)(2,1)...) custom-call(s32[1]{0:T(128)} %bitcast.9.chip_ref, ...), custom_call_target="tpu_custom_call" | custom-call | flops 704643072 | bytes 7903492 | tf_op jit(solution)/shard_map/attend_forward/pallas_call | solution.py:460
  77.6 1.4 collective-permute-start.24
  80.2 6.8 %collective-permute-done.24.refs_10_ = bf16[96,1536]{1,0:T(8,128)(2,1)S(1)} collective-permute-done((bf16[96,1536]{1,0:T(8,128)(2,1)S(1)}, bf16[96,1536]{1,0:T(8,128)(2,1)S(1)}, u32[]{:S(2)}, u32[]{:S(2)}) %collective-permute-start.24) | collective-permute-done | bytes 294944 | tf_op jit(solution)/shard_map/ppermute | solution.py:324
  87.8 2.1 collective-permute-start.15
  89.9 1.4 collective-permute-start.27
  91.3 3.0 %collective-permute-done.15 = bf16[128,768]{1,0:T(8,128)(2,1)S(1)} collective-permute-done((bf16[128,768]{1,0:T(8,128)(2,1)S(1)}, bf16[128,768]{1,0:T(8,128)(2,1)S(1)}, u32[]{:S(2)}, u32[]{:S(2)}) %collective-permute-start.15) | collective-permute-done | bytes 196640 | tf_op jit(solution)/shard_map/ppermute | solution.py:324
  95.5 1.8 collective-permute-start.16
  97.3 3.9 %collective-permute-done.16.refs_1_ = bf16[128,768]{1,0:T(8,128)(2,1)S(1)} collective-permute-done((bf16[128,768]{1,0:T(8,128)(2,1)S(1)}, bf16[128,768]{1,0:T(8,128)(2,1)S(1)}, u32[]{:S(2)}, u32[]{:S(2)}) %collective-permute-start.16) | collective-permute-done | bytes 196640 | tf_op jit(solution)/shard_map/ppermute | solution.py:324
  102.1 2.3 %collective-permute-done.27.refs_13_ = bf16[192,1536]{1,0:T(8,128)(2,1)S(1)} collective-permute-done((bf16[192,1536]{1,0:T(8,128)(2,1)S(1)}, bf16[192,1536]{1,0:T(8,128)(2,1)S(1)}, u32[]{:S(2)}, u32[]{:S(2)}) %collective-permute-start.27) | collective-permute-done | bytes 589856 | tf_op jit(solution)/shard_map/ppermute | solution.py:324
  104.4 4.1 %feed_forward.1 = (bf16[512,768]{1,0:T(8,128)(2,1)S(1)}, f32[1,768]{1,0:T(1,128)S(1)}, bf16[768,768]{1,0:T(8,128)(2,1)S(1)}, f32[256,768]{1,0:T(8,128)S(1)}, f32...) custom-call(s32[1]{0:T(128)} %bitcast.9.chip_ref, ...), custom_call_target="tpu_custom_call" | custom-call | flops 3019898880 | bytes 11053060 | tf_op jit(solution)/shard_map/feed_forward/pallas_call | solution.py:460
  108.6 1.4 collective-permute-start.35
  110.0 1.5 collective-permute-start.36
  112.9 5.5 %collective-permute-done.30 = bf16[128,768]{1,0:T(8,128)(2,1)S(1)} collective-permute-done((bf16[128,768]{1,0:T(8,128)(2,1)S(1)}, bf16[128,768]{1,0:T(8,128)(2,1)S(1)}, u32[]{:S(2)}, u32[]{:S(2)}) %collective-permute-start.30) | collective-permute-done | bytes 196640 | tf_op jit(solution)/shard_map/ppermute | solution.py:324
  119.2 1.6 fusion.30
  121.4 5.2 %collective-permute-done.32.refs_1_ = bf16[128,768]{1,0:T(8,128)(2,1)S(1)} collective-permute-done((bf16[128,768]{1,0:T(8,128)(2,1)S(1)}, bf16[128,768]{1,0:T(8,128)(2,1)S(1)}, u32[]{:S(2)}, u32[]{:S(2)}) %collective-permute-start.32) | collective-permute-done | bytes 196640 | tf_op jit(solution)/shard_map/ppermute | solution.py:324
  126.6 1.4 convolution_add_fusion
  129.6 4.8 %attend_back.1 = (bf16[512,768]{1,0:T(8,128)(2,1)S(1)}, bf16[512,576]{1,0:T(8,128)(2,1)S(1)}, f32[1,576]{1,0:T(1,128)S(1)}, f32[2,1536]{1,0:T(2,128)S(1)}, f32[256,768]{1,0:T(8,128)S(1)}, /*index=5*/f32[256,768]{1,0:T(8,128)}) custom-call(bf16[128,768]{1,0:T(8,128)(2,1)S(1)} %get-tuple-element.100.refs_0_, ...), custom_call_target="tpu_custom_call" | custom-call | flops 855638016 | bytes 7289088 | tf_op jit(solution)/shard_map/attend_back/pallas_call | solution.py:460
  135.0 1.7 collective-permute-done.40.got
  136.7 1.9 grad_blocks.1
  139.4 1.2 collective-permute-start.44
  140.6 1.5 collective-permute-start.45
  144.2 4.7 %collective-permute-done.44.got_first = bf16[192,768]{1,0:T(8,128)(2,1)} collective-permute-done((bf16[192,768]{1,0:T(8,128)(2,1)}, bf16[192,768]{1,0:T(8,128)(2,1)}, u32[]{:S(2)}, u32[]{:S(2)}) %collective-permute-start.44) | collective-permute-done | bytes 294944 | tf_op jit(solution)/shard_map/ppermute | solution.py:324
  148.9 1.2 collective-permute-start.47
  154.8 1.4 collective-permute-start.51
  156.2 1.4 add.212
  160.8 2.6 %collective-permute-done.38 = bf16[128,768]{1,0:T(8,128)(2,1)S(1)} collective-permute-done((bf16[128,768]{1,0:T(8,128)(2,1)S(1)}, bf16[128,768]{1,0:T(8,128)(2,1)S(1)}, u32[]{:S(2)}, u32[]{:S(2)}) %collective-permute-start.38) | collective-permute-done | bytes 196640 | tf_op jit(solution)/shard_map/ppermute | solution.py:324
  165.2 1.9 collective-permute-start.56
  167.1 1.2 collective-permute-done.41
  168.7 5.9 %collective-permute-done.56 = bf16[96,768]{1,0:T(8,128)(2,1)S(1)} collective-permute-done((bf16[96,768]{1,0:T(8,128)(2,1)S(1)}, bf16[96,768]{1,0:T(8,128)(2,1)S(1)}, u32[]{:S(2)}, u32[]{:S(2)}) %collective-permute-start.56) | collective-permute-done | bytes 147488 | tf_op jit(solution)/shard_map/ppermute | solution.py:324
  179.1 2.9 %collective-permute-start.57 = (bf16[96,1536]{1,0:T(8,128)(2,1)S(1)}, bf16[96,1536]{1,0:T(8,128)(2,1)S(1)}, u32[]{:S(2)}, u32[]{:S(2)}) collective-permute-start(bf16[96,1536]{1,0:T(8,128)(2,1)S(1)} %get-tuple-element.143), channel_id=1, source_target_pairs={{0,2},{1,3},{2,0},{3,1},{4,6},{5,7},{6,4},{7,5},{8,10},{9,11},{10,... | collective-permute-start | bytes 884744 | tf_op jit(solution)/shard_map/ppermute | solution.py:324
  183.5 12.7 %collective-permute-done.39 = bf16[128,768]{1,0:T(8,128)(2,1)S(1)} collective-permute-done((bf16[128,768]{1,0:T(8,128)(2,1)S(1)}, bf16[128,768]{1,0:T(8,128)(2,1)S(1)}, u32[]{:S(2)}, u32[]{:S(2)}) %collective-permute-start.39) | collective-permute-done | bytes 196640 | tf_op jit(solution)/shard_map/ppermute | solution.py:324
  199.5 3.2 %collective-permute-done.53 = f32[16,96]{1,0:T(8,128)S(1)} collective-permute-done((f32[16,96]{1,0:T(8,128)S(1)}, f32[16,96]{1,0:T(8,128)S(1)}, u32[]{:S(2)}, u32[]{:S(2)}) %collective-permute-start.53) | collective-permute-done | bytes 6176 | tf_op jit(solution)/shard_map/ppermute | solution.py:324
  205.2 2.0 collective-permute-done.54.far
  (304 shorter events, 59.3 us)
Async XLA Ops:
  3.9 8.3 %collective-permute-start.1 = (f32[8,1152]{1,0:T(8,128)S(1)}, f32[8,1152]{1,0:T(8,128)S(1)}, u32[]{:S(2)}, u32[]{:S(2)}) collective-permute-start(f32[8,1152]{1,0:T(8,128)S(1)} %slice.242), channel_id=1, source_target_pairs={{0,16},{4,20},{8,24},{12,28},{16,0},{20,4},{24,8},{28,12},{1,17},{... | collective-permute-start | bytes 110600 | tf_op jit(solution)/shard_map/ppermute | solution.py:324
  8.3 13.8 %collective-permute-start.2 = (bf16[96,768]{1,0:T(8,128)(2,1)S(1)}, bf16[96,768]{1,0:T(8,128)(2,1)S(1)}, u32[]{:S(2)}, u32[]{:S(2)}) collective-permute-start(bf16[96,768]{1,0:T(8,128)(2,1)S(1)} %pad_maximum_fusion.13), channel_id=1, source_target_pairs={{0,2},{1,3},{2,0},{3,1},{4,6},{5,7},{6,4},{7,5},{8,10},{9,11},{10,... | collective-permute-start | bytes 442376 | tf_op jit(solution)/shard_map/ppermute | solution.py:324
  11.0 11.0 %collective-permute-start = (bf16[64,768]{1,0:T(8,128)(2,1)S(1)}, bf16[64,768]{1,0:T(8,128)(2,1)S(1)}, u32[]{:S(2)}, u32[]{:S(2)}) collective-permute-start(bf16[64,768]{1,0:T(8,128)(2,1)S(1)} %get-tuple-element.236), channel_id=1, source_target_pairs={{0,2},{1,3},{2,0},{3,1},{4,6},{5,7},{6,4},{7,5},{8,10},{9,11},{10,... | collective-permute-start | bytes 294920 | tf_op jit(solution)/shard_map/ppermute | solution.py:324
  24.4 6.0 %collective-permute-start.11 = (bf16[96,768]{1,0:T(8,128)(2,1)S(1)}, bf16[96,768]{1,0:T(8,128)(2,1)S(1)}, u32[]{:S(2)}, u32[]{:S(2)}) collective-permute-start(bf16[96,768]{1,0:T(8,128)(2,1)S(1)} %get-tuple-element.224), channel_id=1, source_target_pairs={{0,16},{4,20},{8,24},{12,28},{16,0},{20,4},{24,8},{28,12},{1,17},{... | collective-permute-start | bytes 442376 | tf_op jit(solution)/shard_map/ppermute | solution.py:324
  25.0 5.7 %collective-permute-start.10 = (bf16[96,768]{1,0:T(8,128)(2,1)S(1)}, bf16[96,768]{1,0:T(8,128)(2,1)S(1)}, u32[]{:S(2)}, u32[]{:S(2)}) collective-permute-start(bf16[96,768]{1,0:T(8,128)(2,1)S(1)} %get-tuple-element.225), channel_id=1, source_target_pairs={{0,8},{4,12},{8,0},{12,4},{16,24},{20,28},{24,16},{28,20},{1,9},{5... | collective-permute-start | bytes 442376 | tf_op jit(solution)/shard_map/ppermute | solution.py:324
  31.6 11.8 %collective-permute-start.8 = (bf16[128,768]{1,0:T(8,128)(2,1)S(1)}, bf16[128,768]{1,0:T(8,128)(2,1)S(1)}, u32[]{:S(2)}, u32[]{:S(2)}) collective-permute-start(bf16[128,768]{1,0:T(8,128)(2,1)S(1)} %pad_maximum_fusion.10.refs_0_), channel_id=1, source_target_pairs={{0,1},{1,0},{2,3},{3,2},{4,5},{5,4},{6,7},{7,6},{8,9},{9,8},{10,11... | collective-permute-start | bytes 589832 | tf_op jit(solution)/shard_map/ppermute | solution.py:324
  32.3 17.1 %collective-permute-start.22 = (bf16[96,1536]{1,0:T(8,128)(2,1)S(1)}, bf16[96,1536]{1,0:T(8,128)(2,1)S(1)}, u32[]{:S(2)}, u32[]{:S(2)}) collective-permute-start(bf16[96,1536]{1,0:T(8,128)(2,1)S(1)} %pad_maximum_fusion.8), channel_id=1, source_target_pairs={{0,2},{1,3},{2,0},{3,1},{4,6},{5,7},{6,4},{7,5},{8,10},{9,11},{10,... | collective-permute-start | bytes 884744 | tf_op jit(solution)/shard_map/ppermute | solution.py:324
  35.8 8.5 %collective-permute-start.6 = (f32[5,1152]{1,0:T(8,128)S(1)}, f32[5,1152]{1,0:T(8,128)S(1)}, u32[]{:S(2)}, u32[]{:S(2)}) collective-permute-start(f32[5,1152]{1,0:T(8,128)S(1)} %get-tuple-element.246), channel_id=1, source_target_pairs={{0,1},{1,0},{2,3},{3,2},{4,5},{5,4},{6,7},{7,6},{8,9},{9,8},{10,11... | collective-permute-start | bytes 69128 | tf_op jit(solution)/shard_map/ppermute | solution.py:324
  44.1 28.5 %collective-permute-start.9 = (bf16[256,768]{1,0:T(8,128)(2,1)}, bf16[256,768]{1,0:T(8,128)(2,1)S(1)}, u32[]{:S(2)}, u32[]{:S(2)}) collective-permute-start(bf16[256,768]{1,0:T(8,128)(2,1)} %pad_maximum_fusion.3), channel_id=1, source_target_pairs={{0,4},{4,0},{8,12},{12,8},{16,20},{20,16},{24,28},{28,24},{1,5},{5... | collective-permute-start | bytes 1179656 | tf_op jit(solution)/shard_map/ppermute | solution.py:324
  45.0 11.5 %collective-permute-start.7 = (f32[2,5,1152]{2,1,0:T(8,128)}, f32[2,5,1152]{2,1,0:T(8,128)}, u32[]{:S(2)}, u32[]{:S(2)}) collective-permute-start(f32[2,5,1152]{2,1,0:T(8,128)} %pad_maximum_fusion.15), channel_id=1, source_target_pairs={{0,2},{1,3},{2,0},{3,1},{4,6},{5,7},{6,4},{7,5},{8,10},{9,11},{10,... | collective-permute-start | bytes 138248 | tf_op jit(solution)/shard_map/ppermute | solution.py:324
  50.3 21.2 %collective-permute-start.23 = (bf16[96,1536]{1,0:T(8,128)(2,1)}, bf16[96,1536]{1,0:T(8,128)(2,1)}, u32[]{:S(2)}, u32[]{:S(2)}) collective-permute-start(bf16[96,1536]{1,0:T(8,128)(2,1)} %broadcast_select_fusion), channel_id=1, source_target_pairs={{0,4},{4,0},{8,12},{12,8},{16,20},{20,16},{24,28},{28,24},{1,5},{5... | collective-permute-start | bytes 884744 | tf_op jit(solution)/shard_map/ppermute | solution.py:324
  50.3 22.3 %collective-permute-start.13 = (bf16[192,768]{1,0:T(8,128)(2,1)}, bf16[192,768]{1,0:T(8,128)(2,1)S(1)}, u32[]{:S(2)}, u32[]{:S(2)}) collective-permute-start(bf16[192,768]{1,0:T(8,128)(2,1)} %get-tuple-element.237), channel_id=1, source_target_pairs={{0,8},{4,12},{8,0},{12,4},{16,24},{20,28},{24,16},{28,20},{1,9},{5... | collective-permute-start | bytes 884744 | tf_op jit(solution)/shard_map/ppermute | solution.py:324
  51.0 21.7 %collective-permute-start.12 = (bf16[192,768]{1,0:T(8,128)(2,1)}, bf16[192,768]{1,0:T(8,128)(2,1)S(1)}, u32[]{:S(2)}, u32[]{:S(2)}) collective-permute-start(bf16[192,768]{1,0:T(8,128)(2,1)} %get-tuple-element.239), channel_id=1, source_target_pairs={{0,16},{4,20},{8,24},{12,28},{16,0},{20,4},{24,8},{28,12},{1,17},{... | collective-permute-start | bytes 884744 | tf_op jit(solution)/shard_map/ppermute | solution.py:324
  64.4 7.0 %collective-permute-start.19 = (bf16[64,768]{1,0:T(8,128)(2,1)S(1)}, bf16[64,768]{1,0:T(8,128)(2,1)S(1)}, u32[]{:S(2)}, u32[]{:S(2)}) collective-permute-start(bf16[64,768]{1,0:T(8,128)(2,1)S(1)} %get-tuple-element.234), channel_id=1, source_target_pairs={{0,2},{1,3},{2,0},{3,1},{4,6},{5,7},{6,4},{7,5},{8,10},{9,11},{10,... | collective-permute-start | bytes 294920 | tf_op jit(solution)/shard_map/ppermute | solution.py:324
  71.4 8.7 %collective-permute-start.20 = (bf16[128,768]{1,0:T(8,128)(2,1)S(1)}, bf16[128,768]{1,0:T(8,128)(2,1)S(1)}, u32[]{:S(2)}, u32[]{:S(2)}) collective-permute-start(bf16[128,768]{1,0:T(8,128)(2,1)S(1)} %pad_maximum_fusion.11.refs_4_), channel_id=1, source_target_pairs={{0,1},{1,0},{2,3},{3,2},{4,5},{5,4},{6,7},{7,6},{8,9},{9,8},{10,11... | collective-permute-start | bytes 589832 | tf_op jit(solution)/shard_map/ppermute | solution.py:324
  77.4 10.2 %collective-permute-start.14 = (f32[256,768]{1,0:T(8,128)S(1)}, f32[256,768]{1,0:T(8,128)S(1)}, u32[]{:S(2)}, u32[]{:S(2)}) collective-permute-start(f32[256,768]{1,0:T(8,128)S(1)} %get-tuple-element.83), channel_id=1, source_target_pairs={{0,4},{4,0},{8,12},{12,8},{16,20},{20,16},{24,28},{28,24},{1,5},{5... | collective-permute-start | bytes 2359304 | tf_op jit(solution)/shard_map/ppermute | solution.py:324
  77.6 9.5 %collective-permute-start.24 = (bf16[96,1536]{1,0:T(8,128)(2,1)S(1)}, bf16[96,1536]{1,0:T(8,128)(2,1)S(1)}, u32[]{:S(2)}, u32[]{:S(2)}) collective-permute-start(bf16[96,1536]{1,0:T(8,128)(2,1)S(1)} %get-tuple-element.223), channel_id=1, source_target_pairs={{0,8},{4,12},{8,0},{12,4},{16,24},{20,28},{24,16},{28,20},{1,9},{5... | collective-permute-start | bytes 884744 | tf_op jit(solution)/shard_map/ppermute | solution.py:324
  79.6 10.3 %collective-permute-start.25 = (bf16[96,1536]{1,0:T(8,128)(2,1)S(1)}, bf16[96,1536]{1,0:T(8,128)(2,1)S(1)}, u32[]{:S(2)}, u32[]{:S(2)}) collective-permute-start(bf16[96,1536]{1,0:T(8,128)(2,1)S(1)} %get-tuple-element.222), channel_id=1, source_target_pairs={{0,16},{4,20},{8,24},{12,28},{16,0},{20,4},{24,8},{28,12},{1,17},{... | collective-permute-start | bytes 884744 | tf_op jit(solution)/shard_map/ppermute | solution.py:324
  80.2 21.1 %collective-permute-start.21 = (bf16[256,768]{1,0:T(8,128)(2,1)S(1)}, bf16[256,768]{1,0:T(8,128)(2,1)S(1)}, u32[]{:S(2)}, u32[]{:S(2)}) collective-permute-start(bf16[256,768]{1,0:T(8,128)(2,1)S(1)} %pad_maximum_fusion.4), channel_id=1, source_target_pairs={{0,4},{4,0},{8,12},{12,8},{16,20},{20,16},{24,28},{28,24},{1,5},{5... | collective-permute-start | bytes 1179656 | tf_op jit(solution)/shard_map/ppermute | solution.py:324
  87.1 15.0 %collective-permute-start.26 = (bf16[192,1536]{1,0:T(8,128)(2,1)S(1)}, bf16[192,1536]{1,0:T(8,128)(2,1)S(1)}, u32[]{:S(2)}, u32[]{:S(2)}) collective-permute-start(bf16[192,1536]{1,0:T(8,128)(2,1)S(1)} %pad_maximum_fusion.1), channel_id=1, source_target_pairs={{0,16},{4,20},{8,24},{12,28},{16,0},{20,4},{24,8},{28,12},{1,17},{... | collective-permute-start | bytes 1769480 | tf_op jit(solution)/shard_map/ppermute | solution.py:324
  87.8 6.5 %collective-permute-start.15 = (bf16[128,768]{1,0:T(8,128)(2,1)S(1)}, bf16[128,768]{1,0:T(8,128)(2,1)S(1)}, u32[]{:S(2)}, u32[]{:S(2)}) collective-permute-start(bf16[128,768]{1,0:T(8,128)(2,1)S(1)} %slice.327), channel_id=1, source_target_pairs={{0,1},{1,0},{2,3},{3,2},{4,5},{5,4},{6,7},{7,6},{8,9},{9,8},{10,11... | collective-permute-start | bytes 589832 | tf_op jit(solution)/shard_map/ppermute | solution.py:324
  89.9 14.4 %collective-permute-start.27 = (bf16[192,1536]{1,0:T(8,128)(2,1)S(1)}, bf16[192,1536]{1,0:T(8,128)(2,1)S(1)}, u32[]{:S(2)}, u32[]{:S(2)}) collective-permute-start(bf16[192,1536]{1,0:T(8,128)(2,1)S(1)} %pad_maximum_fusion.2), channel_id=1, source_target_pairs={{0,8},{4,12},{8,0},{12,4},{16,24},{20,28},{24,16},{28,20},{1,9},{5... | collective-permute-start | bytes 1769480 | tf_op jit(solution)/shard_map/ppermute | solution.py:324
  95.5 5.7 %collective-permute-start.16 = (bf16[128,768]{1,0:T(8,128)(2,1)S(1)}, bf16[128,768]{1,0:T(8,128)(2,1)S(1)}, u32[]{:S(2)}, u32[]{:S(2)}) collective-permute-start(bf16[128,768]{1,0:T(8,128)(2,1)S(1)} %add_convert_fusion.1.refs_0_), channel_id=1, source_target_pairs={{0,1},{1,0},{2,3},{3,2},{4,5},{5,4},{6,7},{7,6},{8,9},{9,8},{10,11... | collective-permute-start | bytes 589832 | tf_op jit(solution)/shard_map/ppermute | solution.py:324
  97.3 7.0 %collective-permute-start.17 = (bf16[128,768]{1,0:T(8,128)(2,1)S(1)}, bf16[128,768]{1,0:T(8,128)(2,1)S(1)}, u32[]{:S(2)}, u32[]{:S(2)}) collective-permute-start(bf16[128,768]{1,0:T(8,128)(2,1)S(1)} %add_convert_fusion.1.refs_0_), channel_id=1, source_target_pairs={{0,4},{4,0},{8,12},{12,8},{16,20},{20,16},{24,28},{28,24},{1,5},{5... | collective-permute-start | bytes 589832 | tf_op jit(solution)/shard_map/ppermute | solution.py:324
  108.6 19.4 %collective-permute-start.35 = (bf16[192,1536]{1,0:T(8,128)(2,1)S(1)}, bf16[192,1536]{1,0:T(8,128)(2,1)S(1)}, u32[]{:S(2)}, u32[]{:S(2)}) collective-permute-start(bf16[192,1536]{1,0:T(8,128)(2,1)S(1)} %get-tuple-element.95), channel_id=1, source_target_pairs={{0,8},{4,12},{8,0},{12,4},{16,24},{20,28},{24,16},{28,20},{1,9},{5... | collective-permute-start | bytes 1769480 | tf_op jit(solution)/shard_map/ppermute | solution.py:324
  110.0 18.0 %collective-permute-start.36 = (bf16[192,1536]{1,0:T(8,128)(2,1)S(1)}, bf16[192,1536]{1,0:T(8,128)(2,1)S(1)}, u32[]{:S(2)}, u32[]{:S(2)}) collective-permute-start(bf16[192,1536]{1,0:T(8,128)(2,1)S(1)} %get-tuple-element.96), channel_id=1, source_target_pairs={{0,16},{4,20},{8,24},{12,28},{16,0},{20,4},{24,8},{28,12},{1,17},{... | collective-permute-start | bytes 1769480 | tf_op jit(solution)/shard_map/ppermute | solution.py:324
  111.7 6.8 %collective-permute-start.30 = (bf16[128,768]{1,0:T(8,128)(2,1)S(1)}, bf16[128,768]{1,0:T(8,128)(2,1)S(1)}, u32[]{:S(2)}, u32[]{:S(2)}) collective-permute-start(bf16[128,768]{1,0:T(8,128)(2,1)S(1)} %slice.326), channel_id=1, source_target_pairs={{0,1},{1,0},{2,3},{3,2},{4,5},{5,4},{6,7},{7,6},{8,9},{9,8},{10,11... | collective-permute-start | bytes 589832 | tf_op jit(solution)/shard_map/ppermute | solution.py:324
  112.9 13.7 %collective-permute-start.28 = (f32[256,768]{1,0:T(8,128)S(1)}, f32[256,768]{1,0:T(8,128)S(1)}, u32[]{:S(2)}, u32[]{:S(2)}) collective-permute-start(f32[256,768]{1,0:T(8,128)S(1)} %fusion.12), channel_id=1, source_target_pairs={{0,4},{4,0},{8,12},{12,8},{16,20},{20,16},{24,28},{28,24},{1,5},{5... | collective-permute-start | bytes 2359304 | tf_op jit(solution)/shard_map/ppermute | solution.py:324
  120.8 5.8 %collective-permute-start.32 = (bf16[128,768]{1,0:T(8,128)(2,1)S(1)}, bf16[128,768]{1,0:T(8,128)(2,1)S(1)}, u32[]{:S(2)}, u32[]{:S(2)}) collective-permute-start(bf16[128,768]{1,0:T(8,128)(2,1)S(1)} %get-tuple-element.100.refs_0_), channel_id=1, source_target_pairs={{0,1},{1,0},{2,3},{3,2},{4,5},{5,4},{6,7},{7,6},{8,9},{9,8},{10,11... | collective-permute-start | bytes 589832 | tf_op jit(solution)/shard_map/ppermute | solution.py:324
  121.4 8.2 %collective-permute-start.33 = (bf16[128,768]{1,0:T(8,128)(2,1)S(1)}, bf16[128,768]{1,0:T(8,128)(2,1)S(1)}, u32[]{:S(2)}, u32[]{:S(2)}) collective-permute-start(bf16[128,768]{1,0:T(8,128)(2,1)S(1)} %get-tuple-element.100.refs_0_), channel_id=1, source_target_pairs={{0,4},{4,0},{8,12},{12,8},{16,20},{20,16},{24,28},{28,24},{1,5},{5... | collective-permute-start | bytes 589832 | tf_op jit(solution)/shard_map/ppermute | solution.py:324
  134.4 20.3 %collective-permute-start.37 = (f32[256,768]{1,0:T(8,128)}, f32[256,768]{1,0:T(8,128)}, u32[]{:S(2)}, u32[]{:S(2)}) collective-permute-start(f32[256,768]{1,0:T(8,128)} %get-tuple-element.110), channel_id=1, source_target_pairs={{0,4},{4,0},{8,12},{12,8},{16,20},{20,16},{24,28},{28,24},{1,5},{5... | collective-permute-start | bytes 2359304 | tf_op jit(solution)/shard_map/ppermute | solution.py:324
  139.4 9.5 %collective-permute-start.44 = (bf16[192,768]{1,0:T(8,128)(2,1)}, bf16[192,768]{1,0:T(8,128)(2,1)}, u32[]{:S(2)}, u32[]{:S(2)}) collective-permute-start(bf16[192,768]{1,0:T(8,128)(2,1)} %get-tuple-element.120), channel_id=1, source_target_pairs={{0,8},{4,12},{8,0},{12,4},{16,24},{20,28},{24,16},{28,20},{1,9},{5... | collective-permute-start | bytes 884744 | tf_op jit(solution)/shard_map/ppermute | solution.py:324
  140.6 12.2 %collective-permute-start.45 = (bf16[192,768]{1,0:T(8,128)(2,1)}, bf16[192,768]{1,0:T(8,128)(2,1)S(1)}, u32[]{:S(2)}, u32[]{:S(2)}) collective-permute-start(bf16[192,768]{1,0:T(8,128)(2,1)} %copy-done.10), channel_id=1, source_target_pairs={{0,16},{4,20},{8,24},{12,28},{16,0},{20,4},{24,8},{28,12},{1,17},{... | collective-permute-start | bytes 884744 | tf_op jit(solution)/shard_map/ppermute | solution.py:324
  142.2 16.8 %collective-permute-start.46 = (bf16[96,1536]{1,0:T(8,128)(2,1)}, bf16[96,1536]{1,0:T(8,128)(2,1)S(1)}, u32[]{:S(2)}, u32[]{:S(2)}) collective-permute-start(bf16[96,1536]{1,0:T(8,128)(2,1)} %copy-done.8), channel_id=1, source_target_pairs={{0,16},{4,20},{8,24},{12,28},{16,0},{20,4},{24,8},{28,12},{1,17},{... | collective-permute-start | bytes 884744 | tf_op jit(solution)/shard_map/ppermute | solution.py:324
  143.7 13.9 %collective-permute-start.31 = (bf16[128,768]{1,0:T(8,128)(2,1)S(1)}, bf16[128,768]{1,0:T(8,128)(2,1)S(1)}, u32[]{:S(2)}, u32[]{:S(2)}) collective-permute-start(bf16[128,768]{1,0:T(8,128)(2,1)S(1)} %slice.325), channel_id=1, source_target_pairs={{0,1},{1,0},{2,3},{3,2},{4,5},{5,4},{6,7},{7,6},{8,9},{9,8},{10,11... | collective-permute-start | bytes 589832 | tf_op jit(solution)/shard_map/ppermute | solution.py:324
  148.9 10.2 %collective-permute-start.47 = (bf16[96,1536]{1,0:T(8,128)(2,1)}, bf16[96,1536]{1,0:T(8,128)(2,1)S(1)}, u32[]{:S(2)}, u32[]{:S(2)}) collective-permute-start(bf16[96,1536]{1,0:T(8,128)(2,1)} %copy-done.9), channel_id=1, source_target_pairs={{0,8},{4,12},{8,0},{12,4},{16,24},{20,28},{24,16},{28,20},{1,9},{5... | collective-permute-start | bytes 884744 | tf_op jit(solution)/shard_map/ppermute | solution.py:324
  153.9 6.7 %collective-permute-start.52 = (bf16[96,768]{1,0:T(8,128)(2,1)S(1)}, bf16[96,768]{1,0:T(8,128)(2,1)S(1)}, u32[]{:S(2)}, u32[]{:S(2)}) collective-permute-start(bf16[96,768]{1,0:T(8,128)(2,1)S(1)} %get-tuple-element.133), channel_id=1, source_target_pairs={{0,8},{4,12},{8,0},{12,4},{16,24},{20,28},{24,16},{28,20},{1,9},{5... | collective-permute-start | bytes 442376 | tf_op jit(solution)/shard_map/ppermute | solution.py:324
  154.8 5.8 %collective-permute-start.51 = (bf16[96,768]{1,0:T(8,128)(2,1)S(1)}, bf16[96,768]{1,0:T(8,128)(2,1)S(1)}, u32[]{:S(2)}, u32[]{:S(2)}) collective-permute-start(bf16[96,768]{1,0:T(8,128)(2,1)S(1)} %get-tuple-element.122), channel_id=1, source_target_pairs={{0,16},{4,20},{8,24},{12,28},{16,0},{20,4},{24,8},{28,12},{1,17},{... | collective-permute-start | bytes 442376 | tf_op jit(solution)/shard_map/ppermute | solution.py:324
  157.7 5.7 %collective-permute-start.38 = (bf16[128,768]{1,0:T(8,128)(2,1)S(1)}, bf16[128,768]{1,0:T(8,128)(2,1)S(1)}, u32[]{:S(2)}, u32[]{:S(2)}) collective-permute-start(bf16[128,768]{1,0:T(8,128)(2,1)S(1)} %slice.324), channel_id=1, source_target_pairs={{0,1},{1,0},{2,3},{3,2},{4,5},{5,4},{6,7},{7,6},{8,9},{9,8},{10,11... | collective-permute-start | bytes 589832 | tf_op jit(solution)/shard_map/ppermute | solution.py:324
  159.4 5.6 %collective-permute-start.48 = (f32[96,1536]{1,0:T(8,128)S(1)}, f32[96,1536]{1,0:T(8,128)S(1)}, u32[]{:S(2)}, u32[]{:S(2)}) collective-permute-start(f32[96,1536]{1,0:T(8,128)S(1)} %get-tuple-element.127), channel_id=1, source_target_pairs={{0,4},{4,0},{8,12},{12,8},{16,20},{20,16},{24,28},{28,24},{1,5},{5... | collective-permute-start | bytes 1769480 | tf_op jit(solution)/shard_map/ppermute | solution.py:324
  160.7 4.5 %collective-permute-start.55 = (f32[96,768]{1,0:T(8,128)S(1)}, f32[96,768]{1,0:T(8,128)S(1)}, u32[]{:S(2)}, u32[]{:S(2)}) collective-permute-start(f32[96,768]{1,0:T(8,128)S(1)} %get-tuple-element.138), channel_id=1, source_target_pairs={{0,4},{4,0},{8,12},{12,8},{16,20},{20,16},{24,28},{28,24},{1,5},{5... | collective-permute-start | bytes 884744 | tf_op jit(solution)/shard_map/ppermute | solution.py:324
  165.2 9.3 %collective-permute-start.56 = (bf16[96,768]{1,0:T(8,128)(2,1)S(1)}, bf16[96,768]{1,0:T(8,128)(2,1)S(1)}, u32[]{:S(2)}, u32[]{:S(2)}) collective-permute-start(bf16[96,768]{1,0:T(8,128)(2,1)S(1)} %get-tuple-element.140), channel_id=1, source_target_pairs={{0,2},{1,3},{2,0},{3,1},{4,6},{5,7},{6,4},{7,5},{8,10},{9,11},{10,... | collective-permute-start | bytes 442376 | tf_op jit(solution)/shard_map/ppermute | solution.py:324
  168.4 8.0 %collective-permute-start.42 = (f32[8,1152]{1,0:T(8,128)S(1)}, f32[8,1152]{1,0:T(8,128)S(1)}, u32[]{:S(2)}, u32[]{:S(2)}) collective-permute-start(f32[8,1152]{1,0:T(8,128)S(1)} %select_add_fusion.line), channel_id=1, source_target_pairs={{0,2},{1,3},{2,0},{3,1},{4,6},{5,7},{6,4},{7,5},{8,10},{9,11},{10,... | collective-permute-start | bytes 110600 | tf_op jit(solution)/shard_map/ppermute | solution.py:324
  178.3 4.4 %collective-permute-start.49 = (f32[2,5,1152]{2,1,0:T(8,128)S(1)}, f32[2,5,1152]{2,1,0:T(8,128)S(1)}, u32[]{:S(2)}, u32[]{:S(2)}) collective-permute-start(f32[2,5,1152]{2,1,0:T(8,128)S(1)} %pad_maximum_fusion.16), channel_id=1, source_target_pairs={{0,8},{4,12},{8,0},{12,4},{16,24},{20,28},{24,16},{28,20},{1,9},{5... | collective-permute-start | bytes 138248 | tf_op jit(solution)/shard_map/ppermute | solution.py:324
  179.0 17.2 %collective-permute-start.39 = (bf16[128,768]{1,0:T(8,128)(2,1)S(1)}, bf16[128,768]{1,0:T(8,128)(2,1)S(1)}, u32[]{:S(2)}, u32[]{:S(2)}) collective-permute-start(bf16[128,768]{1,0:T(8,128)(2,1)S(1)} %pad_maximum_fusion.12), channel_id=1, source_target_pairs={{0,2},{1,3},{2,0},{3,1},{4,6},{5,7},{6,4},{7,5},{8,10},{9,11},{10,... | collective-permute-start | bytes 589832 | tf_op jit(solution)/shard_map/ppermute | solution.py:324
  179.1 29.6 %collective-permute-start.57 = (bf16[96,1536]{1,0:T(8,128)(2,1)S(1)}, bf16[96,1536]{1,0:T(8,128)(2,1)S(1)}, u32[]{:S(2)}, u32[]{:S(2)}) collective-permute-start(bf16[96,1536]{1,0:T(8,128)(2,1)S(1)} %get-tuple-element.143), channel_id=1, source_target_pairs={{0,2},{1,3},{2,0},{3,1},{4,6},{5,7},{6,4},{7,5},{8,10},{9,11},{10,... | collective-permute-start | bytes 884744 | tf_op jit(solution)/shard_map/ppermute | solution.py:324
  182.7 15.0 %collective-permute-start.50 = (f32[4,5,1152]{2,1,0:T(8,128)S(1)}, f32[4,5,1152]{2,1,0:T(8,128)S(1)}, u32[]{:S(2)}, u32[]{:S(2)}) collective-permute-start(f32[4,5,1152]{2,1,0:T(8,128)S(1)} %pad_maximum_fusion.14), channel_id=1, source_target_pairs={{0,16},{4,20},{8,24},{12,28},{16,0},{20,4},{24,8},{28,12},{1,17},{... | collective-permute-start | bytes 276488 | tf_op jit(solution)/shard_map/ppermute | solution.py:324
  202.6 4.5 %collective-permute-start.54 = (f32[16,96]{1,0:T(8,128)S(1)}, f32[16,96]{1,0:T(8,128)S(1)}, u32[]{:S(2)}, u32[]{:S(2)}) collective-permute-start(f32[16,96]{1,0:T(8,128)S(1)} %add.217.near), channel_id=1, source_target_pairs={{0,2},{1,3},{2,0},{3,1},{4,6},{5,7},{6,4},{7,5},{8,10},{9,11},{10,... | collective-permute-start | bytes 18440 | tf_op jit(solution)/shard_map/ppermute | solution.py:324
  (59 other events, 470.6 us)

commit v3 on v2

--- a/solution.py
+++ b/solution.py
@@ -324,30 +324,8 @@
     return lax.ppermute(values, axis, [(place, place ^ mask) for place in range(count)])
 
 
-def unxor(parts, own):
-    bit = 1
-    while bit < len(parts):
-        odd = (own & bit) != 0
-        parts = [jnp.where(odd, parts[r ^ bit], parts[r]) for r in range(len(parts))]
-        bit *= 2
-    return parts
-
-
 def pick(values, place):
     return lax.dynamic_index_in_dim(values, place, 0, keepdims=False)
-
-
-def exchange_latents(pair, half):
-    return jnp.concatenate([pick(pair, half), swap(pick(pair, 1 - half), "tensor", 2)])
-
-
-def spread_pairs(own_half, other_half):
-    return spread_rows(own_half + swap(other_half, "dp", 1))
-
-
-def spread_rows(both):
-    rows = both.shape[0] // 2
-    return both[:rows] + swap(both[rows:].astype(jnp.bfloat16), "tensor", 1).astype(jnp.float32)
 
 
 def collect_pairs(rows):
@@ -355,8 +333,104 @@
     return [rows, near, swap(rows, "dp", 1), swap(near, "dp", 1)]
 
 
-def after(values, *earlier):
-    return lax.optimization_barrier((values,) + earlier)[0]
+(
+    ACTIVATED,
+    ATTEND,
+    ATTEND_BACK,
+    ATTEND_SEND,
+    ATTN_BLOCKS,
+    ATTN_CORE,
+    ATTN_FAR,
+    ATTN_HALF,
+    ATTN_OWNER,
+    ATTN_PARTS,
+    ATTN_SHARD,
+    ATTN_SHARE,
+    BACK_SENT,
+    BLOCK_MOVED,
+    BLOCK_OUT,
+    FAR,
+    FEED,
+    FEED_SEND,
+    FF_BLOCKS,
+    FF_CORE,
+    FF_FAR,
+    FF_GOING,
+    FF_HALF,
+    FF_MIDDLE,
+    FF_MOVED,
+    FF_OWNER,
+    FF_SECOND,
+    FF_SHARE,
+    GRAD_SILU,
+    HIDDEN_BACK,
+    LINE,
+    LINE_FAR,
+    LINE_NEAR,
+    MOD_LINE,
+    MOD_PLACE,
+    MODULATION_BACK,
+    NEAR,
+    NORM_CROSSED,
+    OUT_SEND,
+    OUTPUT_NEAR,
+    OUTPUTS,
+    PACK,
+    PACKED_X,
+    PACKED_Y,
+    PARTIAL_CORE,
+    RESIDUAL,
+    TABLE,
+    TOKENS_HALF,
+    TOKENS_SENT,
+    UPSTREAM_HALF,
+    UPSTREAM_SENT,
+) = range(51)
+
+HOLDS = {
+    TOKENS_SENT: (ATTN_SHARD,),
+    PARTIAL_CORE: (ATTN_FAR, ATTN_SHARE, TOKENS_HALF,),
+    MOD_PLACE: (ATTN_PARTS,),
+    FF_FAR: (MOD_LINE,),
+    UPSTREAM_SENT: (FF_FAR, FF_SHARE,),
+    ATTEND: (FF_SHARE,),
+    FF_SECOND: (ATTEND_SEND,),
+    RESIDUAL: (UPSTREAM_HALF,),
+    FF_BLOCKS: (FEED_SEND,),
+    ACTIVATED: (FEED,),
+    HIDDEN_BACK: (OUT_SEND,),
+    FF_MIDDLE: (BLOCK_OUT, OUTPUT_NEAR,),
+    ATTEND_BACK: (BLOCK_OUT, FF_GOING,),
+    BLOCK_MOVED: (OUTPUT_NEAR,),
+    PACK: (FF_CORE,),
+    ATTN_BLOCKS: (PACK,),
+    LINE_NEAR: (FF_CORE,),
+    LINE: (FF_HALF,),
+    LINE_FAR: (ATTN_BLOCKS, FF_HALF,),
+    FF_CORE: (NORM_CROSSED,),
+    BACK_SENT: (FAR,),
+    PACKED_X: (FF_CORE, FF_HALF,),
+    PACKED_Y: (FF_MOVED,),
+    MODULATION_BACK: (ATTN_CORE,),
+    ATTN_HALF: (MODULATION_BACK,),
+    GRAD_SILU: (FF_MOVED,),
+    FF_OWNER: (NEAR,),
+    ATTN_OWNER: (TABLE,),
+    OUTPUTS: (MODULATION_BACK,),
+}
+
+
+class Order:
+    def __init__(self):
+        self.marks = {}
+
+    def mark(self, name, values):
+        self.marks[name] = values
+        return values
+
+    def hold(self, name, values):
+        earlier = [self.marks[mark] for mark in HOLDS.get(name, ())]
+        return lax.optimization_barrier((values, earlier))[0] if earlier else values
 
 
 def near_weight(shard, far, is_own, core):
@@ -368,12 +442,15 @@
     )
 
 
-def chip_rows(share):
+def chip_first(share):
     count = share.shape[0] // 2
-    first, second = share[:count], share[count:]
-    first_x, second_y = swap(first, "dp", 2), swap(second, "dp", 4)
-    first_y = swap(jnp.concatenate([first, first_x]), "dp", 4)
-    second_x = swap(jnp.concatenate([second, second_y]), "dp", 2)
+    return swap(share[:count], "dp", 2), swap(share[count:], "dp", 4)
+
+
+def chip_second(share, first_x, second_y):
+    count = share.shape[0] // 2
+    first_y = swap(jnp.concatenate([share[:count], first_x]), "dp", 4)
+    second_x = swap(jnp.concatenate([share[count:], second_y]), "dp", 2)
     return [share, first_x, second_y, first_y, second_x]
 
 
@@ -661,26 +738,140 @@
     return kernel_call(half_body, "half_step", outs, operands, [], 12, 0)
 
 
-def pack_body(norm, got, gate_a, shift_m, scale_m, gate_m, out_b, red_b, expand, bias, packed):
-    wide = gate_a.shape[1]
+def mod_sum_body(partial, crossed, mod_bias, attend_bias, expand_bias, out):
+    heads = attend_bias.shape[1]
+    out[...] = jnp.zeros_like(out)
+    out[0:2, :] = partial[0:2, :] + crossed[2:4, :] + mod_bias[...]
+    out[2:4, :] = partial[2:4, :] + crossed[0:2, :] + mod_bias[...]
+    out[4:5, :heads] = attend_bias[0:1, :]
+    out[4:5, heads : 2 * heads] = attend_bias[1:2, :]
+    out[4:5, 2 * heads :] = expand_bias[...]
+
+
+def mod_place_body(place_ref, own, near, far, mod, qkv_bias, expand_bias, *pieces):
+    z, half, is_own = place_ref[0], place_ref[1], place_ref[2]
+    width = own.shape[1]
+    for r, (source, start) in enumerate(((own, 0), (near, 0), (far, 0), (far, 8))):
+        cols = pl.ds(pl.multiple_of((z ^ r) * width, 128), width)
+        mod[0:1, cols] = source[pl.ds(start + half, 1), :]
+        mod[1:2, cols] = source[pl.ds(start + 2 + half, 1), :]
+    wide = expand_bias.shape[1]
+    for k, piece in enumerate(pieces):
+        piece[...] = mod[0:1, k * wide : (k + 1) * wide]
+    bias = jnp.where(is_own == 1, own[4:5, :], far[4:5, :])
+    heads = qkv_bias.shape[1] // 3
+    qkv_bias[:, :heads] = bias[:, :heads]
+    qkv_bias[:, heads : 2 * heads] = jnp.zeros_like(qkv_bias[:, heads : 2 * heads])
+    qkv_bias[:, 2 * heads :] = bias[:, heads : 2 * heads]
+    expand_bias[...] = bias[:, 2 * heads :]
+
+
+def halve_body(own, got, keep, send):
+    count = keep.shape[0]
+    keep[...] = own[:count, :] + got[:count, :]
+    send[...] = (own[count:, :] + got[count:, :]).astype(jnp.bfloat16)
+
+
+def halve(own, got):
+    shape = (own.shape[0] // 2, own.shape[1])
+    outs = [(shape, jnp.float32), (shape, jnp.bfloat16)]
+    return kernel_call(halve_body, "halve", outs, [own, got], [], 8, 0)
+
+
+def column_sums(values):
+    return jnp.sum(values, axis=0, keepdims=True)
+
+
+def residual_body(keep, got, tokens, out_bias, gate, shift, gain, attend_out, residual, low):
+    attend_out[...] = keep[...] + got[...].astype(jnp.float32) + out_bias[...]
+    residual[...] = tokens[...].astype(jnp.float32) + gate[...] * attend_out[...]
+    normed, _ = normalize(residual[...])
+    low[...] = (normed * (1.0 + gain[...]) + shift[...]).astype(jnp.bfloat16)
+
+
+def hidden_back_body(
+    keep, got, residual, attend_out, upstream, gate_a, gain, gate_m, low, grad_residual, sums
+):
+    grad = keep[...] + got[...].astype(jnp.float32)
+    normed, inverse = normalize(residual[...])
+    up = upstream[...].astype(jnp.float32)
+    total = up + norm_back(grad * (1.0 + gain[...]), normed, inverse)
+    grad_residual[...] = total
+    term = total * gate_a[...]
+    low[...] = term.astype(jnp.bfloat16)
+    sums[0:1, :] = column_sums(total * attend_out[...])
+    sums[1:2, :] = column_sums(grad)
+    sums[2:3, :] = column_sums(grad * normed)
+    sums[3:4, :] = column_sums(term)
+    sums[4:5, :] = column_sums(up * gate_m[...])
+    sums[5:8, :] = jnp.zeros_like(sums[5:8, :])
+
+
+def block_out_body(keep, got, residual, upstream, reduce_bias, gate, block, gate_sum):
+    hidden_out = keep[...] + got[...].astype(jnp.float32) + reduce_bias[...]
+    block[...] = (residual[...] + gate[...] * hidden_out).astype(jnp.bfloat16)
+    gate_sum[...] = column_sums(upstream[...].astype(jnp.float32) * hidden_out)
+
+
+def tokens_back_body(keep, got, tokens, grad_residual, gain, kept, send):
+    count = kept.shape[0]
+    grad = keep[...] + got[...].astype(jnp.float32)
+    normed, inverse = normalize(tokens[...].astype(jnp.float32))
+    total = grad_residual[...] + norm_back(grad * (1.0 + gain[...]), normed, inverse)
+    kept[...] = total[:count, :]
+    send[...] = total[count:, :].astype(jnp.bfloat16)
+
+
+def outputs_body(half_ref, block, block_moved, kept, moved, block_out, tokens_grad):
+    half, count = half_ref[0], kept.shape[0]
+    block_out[half] = block[:count, :]
+    block_out[1 - half] = block_moved[...]
+    tokens_grad[half] = kept[...]
+    tokens_grad[1 - half] = moved[...].astype(jnp.float32)
+
+
+def owner_body(kept, moved, *outs):
+    start = 0
+    for out in outs:
+        stop = start + out.shape[1]
+        out[...] = kept[:, start:stop] + moved[:, start:stop].astype(jnp.float32)
+        start = stop
+
+
+def owner_sum(kept, moved, widths):
+    outs = [((kept.shape[0], width), jnp.float32) for width in widths]
+    return kernel_call(owner_body, "owner_sum", outs, [kept, moved], [], 8, 0)
+
+
+def pack_body(norm, got, sums, gate_m, expand, bias, packed):
+    wide = gate_m.shape[1]
     part = packed.shape[1] - wide
-    packed[...] = jnp.zeros_like(packed)
     both = norm[0:1, :] + got[...]
     packed[0:1, :wide] = both[:, :wide]
     packed[0:1, wide:] = both[:, wide : wide + part]
     packed[1:2, : wide - part] = both[:, wide + part :]
-    packed[1:2, wide - part :] = gate_a[...]
-    packed[2:3, :wide] = shift_m[...]
-    packed[2:3, wide:] = scale_m[:, :part]
-    packed[3:4, : wide - part] = scale_m[:, part:]
+    packed[1:2, wide - part :] = sums[0:1, :]
+    packed[2:3, :wide] = sums[1:2, :]
+    packed[2:3, wide:] = sums[2:3, :part]
+    packed[3:4, : wide - part] = sums[2:3, part:]
     packed[3:4, wide - part :] = gate_m[...]
-    packed[4:5, :wide] = out_b[...]
-    packed[4:5, wide:] = red_b[:, :part]
-    packed[5:6, : wide - part] = red_b[:, part:]
+    packed[4:5, :wide] = sums[3:4, :]
+    packed[4:5, wide:] = sums[4:5, :part]
+    packed[5:6, : wide - part] = sums[4:5, part:]
+    packed[5:6, wide - part :] = jnp.zeros_like(packed[5:6, wide - part :])
     heads = bias.shape[1] // 3
     packed[6:7, :wide] = expand[...]
     packed[6:7, wide : wide + heads] = bias[:, :heads]
-    packed[6:7, wide + heads : wide + 2 * heads] = bias[:, 2 * heads :]
+    packed[6:7, wide + heads :] = bias[:, 2 * heads :]
+    packed[7:8, :] = jnp.zeros_like(packed[7:8, :])
+
+
+def attend_owner_body(kept, moved, attend_grad, output_grad):
+    width = output_grad.shape[1]
+    for j in range(3):
+        cols = slice(j * width, (j + 1) * width)
+        attend_grad[j] = kept[:, cols] + moved[:, cols].astype(jnp.float32)
+    output_grad[...] = kept[:, 3 * width :] + moved[:, 3 * width :].astype(jnp.float32)
 
 
 def choose_body(place_ref, line, far, packed):
@@ -689,10 +880,11 @@
     packed[pl.ds(1 - half, 1), :] = far[pl.ds(z, 1), :]
     packed[2:3, :] = jnp.where(own == 1, line[6:7, :] + far[6:7, :], 0.0)
     packed[3:5, :] = line[4:6, :] + far[4:6, :]
+    packed[5:8, :] = jnp.zeros_like(packed[5:8, :])
 
 
 def modulation_back_body(gathered, silu, weight, weight_grad, grad_silu, bias_grad, rest, rows):
-    parts = [gathered[m] for m in range(gathered.shape[0])]
+    parts = [gathered[start : start + 8, :] for start in range(0, gathered.shape[0], 8)]
     for m, part in enumerate(parts):
         rows[2 * m : 2 * m + 2, :] = part[0:2, :]
     low = rows[...].astype(jnp.bfloat16)
@@ -704,14 +896,27 @@
     rest[...] = parts[0][2:5, :]
 
 
-def table_body(labels, cond, near, far, table):
+def table_body(labels, cond, near, far, table, chosen):
     value = cond[...]
     share = 1.0 / (1.0 + jnp.exp(-value))
     grad = (near[...] + far[...]) * share * (1.0 + value * (1.0 - share))
-    table[...] = jnp.zeros_like(table)
-    for row in range(grad.shape[0]):
-        place = pl.ds(labels[row], 1)
-        table[place, :] = table[place, :] + grad[row : row + 1, :]
+    place = lax.broadcasted_iota(jnp.int32, (1, chosen.shape[1]), 1)
+    for row in range(chosen.shape[0]):
+        chosen[row : row + 1, :] = jnp.where(place == labels[row], 1.0, 0.0)
+    table[...] = lax.dot_general(
+        grad,
+        chosen[...],
+        (((0,), (0,)), ((), ())),
+        precision=lax.Precision.HIGHEST,
+        preferred_element_type=jnp.float32,
+    )
+
+
+def join_body(attend, output, joined):
+    width = output.shape[1]
+    for j in range(3):
+        joined[:, j * width : (j + 1) * width] = attend[j]
+    joined[:, 3 * width :] = output[...]
 
 
 def attend_back_body(heads, scale, *refs):
@@ -810,6 +1015,28 @@
     classes_total = class_table.shape[0]
     score_scale = 1.0 / math.sqrt(HD)
 
+    count = tokens.shape[1]
+    place = jnp.stack([tensor_index, half, is_own.astype(jnp.int32)])
+
+    order = Order()
+    mark, hold = order.mark, order.hold
+
+    attn_shard = kernel_call(
+        join_body,
+        "join_weights",
+        [((row_share, 4 * head_width), jnp.bfloat16)],
+        [jnp.transpose(attend_weight, (1, 0, 2)), output_weight],
+        [],
+        4,
+        0,
+    )[0]
+    mark(ATTN_SHARD, attn_shard)
+    attn_far = mark(ATTN_FAR, swap(attn_shard, "tensor", 2))
+    tokens_sent = pick(hold(TOKENS_SENT, tokens), 1 - half)
+    tokens_half = jnp.concatenate([pick(tokens, half), swap(tokens_sent, "tensor", 2)])
+    mark(TOKENS_HALF, tokens_half)
+    labels, timesteps = (labels, timesteps)
+
     slot = jnp.arange(latent_total, dtype=jnp.int32)
     latent_ids = ((slot >> 1) ^ data_index) * 2 + (slot & 1)
     chosen = latent_ids[:, None] == slot[None, :]
@@ -821,58 +1048,64 @@
     halfway = model_width // 2
     column = data_index * row_share + jnp.arange(row_share, dtype=jnp.int32)
     is_cos = column < halfway
-    place = jnp.where(is_cos, column, column - halfway).astype(jnp.float32)
-    frequency = jnp.exp(-math.log(10000.0) * place / halfway)
+    position = jnp.where(is_cos, column, column - halfway).astype(jnp.float32)
+    frequency = jnp.exp(-math.log(10000.0) * position / halfway)
     angles = steps_rel.astype(jnp.float32)[:, None] * frequency[None, :]
     cond = looked + jnp.where(is_cos[None, :], jnp.cos(angles), jnp.sin(angles))
     silu_act = jax.nn.silu(cond).astype(jnp.bfloat16)
     partial = jnp.dot(silu_act, modulation_weight, preferred_element_type=jnp.float32)
-    attn_shard = jnp.concatenate([attend_weight.reshape(row_share, -1), output_weight], axis=1)
-    attn_far = swap(attn_shard, "tensor", 2)
+    partial = partial[:8] + swap(partial[8:], "dp", 4)
     attn_share = near_weight(attn_shard, attn_far, is_own, core)
-    partial = partial[:8] + swap(partial[8:], "dp", 4)
-    partial = partial[:4] + swap(after(partial, attn_far)[4:], "dp", 2)
-    crossed = swap(after(partial, attn_share), "dp", 1)
-    bias_vec = jnp.concatenate([attend_bias.reshape(-1), expand_bias])
-    mod_cols = jnp.concatenate(
+    mark(ATTN_SHARE, attn_share)
+    partial = partial[:4] + swap(partial[4:], "dp", 2)
+    partial = hold(PARTIAL_CORE, partial)
+    ff_shard = jnp.concatenate([expand_weight, reduce_weight], axis=1)
+    tokens_near = swap(tokens_half, "tensor", 1)
+    mod_cols = kernel_call(
+        mod_sum_body,
+        "mod_sum",
+        [((8, mod_width), jnp.float32)],
         [
-            partial + jnp.concatenate([crossed[2:], crossed[:2]]) + modulation_bias,
-            bias_vec[None],
+            partial,
+            swap(partial, "dp", 1),
+            modulation_bias[None],
+            attend_bias,
+            expand_bias[None],
+        ],
+        [],
+        4,
+        0,
+    )[0]
+    attn_first = chip_first(attn_share)
+    attn_parts = chip_second(attn_share, *attn_first)
+    mark(ATTN_PARTS, attn_parts)
+    mod_near = swap(mod_cols, "tensor", 1)
+    mod_line = jnp.concatenate([mod_cols, mod_near])
+    mark(MOD_LINE, mod_line)
+    mod_far = swap(mod_line, "tensor", 2)
+    ff_far = mark(FF_FAR, swap(ff_shard, "tensor", 2))
+    tokens_across = swap(jnp.concatenate([tokens_half, tokens_near]), "dp", 1)
+    row = ((1, model_width), jnp.float32)
+    mod_full, qkv_bias, expand_row, _, gain_a, gate_a, shift_m, gain_m, gate_m = kernel_call(
+        mod_place_body,
+        "mod_place",
+        [
+            ((2, 6 * model_width), jnp.float32),
+            ((1, 3 * head_width), jnp.float32),
+            ((1, ff_width), jnp.float32),
         ]
-    )
-    mod_near = jnp.stack([mod_cols, swap(mod_cols, "tensor", 1)])
-    mod_far = swap(mod_near, "tensor", 2)
-    mod_parts = [mod_near[0], mod_near[1], mod_far[0], mod_far[1]]
-    mod_full = jnp.concatenate(
-        unxor([jnp.where(half == 0, m[0:4:2], m[1:4:2]) for m in mod_parts], tensor_index), axis=1
-    )
-    bias_vec = jnp.where(is_own, bias_vec, mod_parts[2][4])
-    pieces = mod_full.reshape(2, 6, 1, model_width)
-    own_pieces = pieces[0]
-
-    tokens_half = exchange_latents(after(tokens, attn_shard), half)
-    own_rows = tokens_half.shape[0]
-    tokens_near = swap(tokens_half, "tensor", 1)
-    tokens_across = swap(jnp.concatenate([tokens_half, tokens_near]), "dp", 1)
-    tokens_own = tokens_half.astype(jnp.float32)
-
-    attn_parts = chip_rows(attn_share)
-    ff_shard = after(
-        jnp.concatenate([expand_weight, reduce_weight], axis=1), attn_far, tokens_half
-    )
-    ff_far = swap(ff_shard, "tensor", 2)
-    ff_share = near_weight(ff_shard, ff_far, is_own, core)
-    ff_parts = chip_rows(after(ff_share, *attn_parts))
-
-    upstream_half = exchange_latents(after(cotangent, mod_far), half)
-    upstream_near = swap(upstream_half, "tensor", 1)
-    upstream_across = swap(jnp.concatenate([upstream_half, upstream_near]), "dp", 1)
-    upstream = upstream_half.astype(jnp.float32)
-    query_bias = bias_vec[:head_width]
-    value_bias = bias_vec[head_width : 2 * head_width]
-    expand_bias_q = bias_vec[2 * head_width :]
-
-    bias_rows = jnp.concatenate([query_bias, jnp.zeros_like(query_bias), value_bias])[None]
+        + [row] * 6,
+        [place, mod_cols, mod_near, hold(MOD_PLACE, mod_far)],
+        [],
+        4,
+        0,
+    )
+    ff_share = near_weight(ff_shard, hold(FF_FAR, ff_far), is_own, core)
+    mark(FF_SHARE, ff_share)
+    upstream_sent = hold(UPSTREAM_SENT, pick(cotangent, 1 - half))
+    upstream_far = swap(upstream_sent, "tensor", 2)
+    ff_first = chip_first(ff_share)
+
     (
         attend_rows,
         normed_all,
@@ -884,19 +1117,41 @@
         other_partial,
     ) = attend_forward(
         chip,
-        [tokens_half, tokens_near, tokens_across],
+        [tokens_half, tokens_near, hold(ATTEND, tokens_across)],
         mod_full,
-        bias_rows,
+        qkv_bias,
         attn_parts,
         head_count,
         score_scale,
     )
-    attend_out = spread_pairs(own_partial, other_partial) + output_bias
-    normed_first, inverse_first = normalize(tokens_own)
-    residual = tokens_own + own_pieces[2] * attend_out
-    normed_second, inverse_second = normalize(residual)
-    hidden_in = (normed_second * (1.0 + own_pieces[4]) + own_pieces[3]).astype(jnp.bfloat16)
+    keep, send = halve(own_partial, swap(other_partial, "dp", 1))
+    mark(ATTEND_SEND, send)
+    upstream_half = jnp.concatenate([pick(cotangent, half), upstream_far])
+    mark(UPSTREAM_HALF, upstream_half)
+    ff_first = hold(FF_SECOND, ff_first)
+    ff_parts = chip_second(ff_share, *ff_first)
+    got = swap(send, "tensor", 1)
+    upstream_near = swap(upstream_half, "tensor", 1)
+    attend_out, residual, hidden_in = kernel_call(
+        residual_body,
+        "residual",
+        [(keep.shape, jnp.float32), (keep.shape, jnp.float32), (keep.shape, jnp.bfloat16)],
+        [
+            keep,
+            hold(RESIDUAL, got),
+            tokens_half,
+            output_bias[None],
+            gate_a,
+            shift_m,
+            gain_m,
+        ],
+        [],
+        8,
+        0,
+    )
     hidden_pieces = collect_pairs(hidden_in)
+    upstream_line = jnp.concatenate([upstream_half, upstream_near])
+    upstream_across = swap(upstream_line, "dp", 1)
 
     (
         activated,
@@ -910,35 +1165,66 @@
         hidden_pieces,
         [upstream_half, upstream_near, upstream_across],
         mod_full,
-        expand_bias_q[None],
+        expand_row,
         ff_parts,
     )
-    ff_first = first_step(ff_blocks[2:])
-    grad_reduce_bias = jnp.sum(upstream * own_pieces[5], axis=0, keepdims=True)
+    mark(FEED, own_partial)
+    keep, send = halve(own_partial, swap(other_partial, "dp", 1))
+    mark(FEED_SEND, send)
+    got = swap(send, "tensor", 1)
+    ff_first = first_step(hold(FF_BLOCKS, ff_blocks[2:]))
     seq_len = tokens_across.shape[0]
-    hidden_sum = own_partial + swap(other_partial, "dp", 1)
-    grad_hidden_in = spread_rows(hidden_sum)
-    act_later = after(activated, own_partial)
+    act_later = hold(ACTIVATED, activated)
     other_out, own_out = (
         jnp.einsum("sf,of->so", act_half, reduce_full, preferred_element_type=jnp.float32)
         for act_half in (act_later[seq_len:], act_later[:seq_len])
     )
-    out_sum = own_out + swap(other_out, "dp", 1)
-
-    grad_shift_hidden = jnp.sum(grad_hidden_in, axis=0, keepdims=True)
-    grad_scale_hidden = jnp.sum(grad_hidden_in * normed_second, axis=0, keepdims=True)
-    grad_residual = upstream + norm_back(
-        grad_hidden_in * (1.0 + own_pieces[4]), normed_second, inverse_second
-    )
-    grad_gate_attend = jnp.sum(grad_residual * attend_out, axis=0, keepdims=True)
-    output_term = grad_residual * own_pieces[2]
-    grad_output_bias = jnp.sum(output_term, axis=0, keepdims=True)
-    output_pieces = collect_pairs(output_term.astype(jnp.bfloat16))
-    *ff_bases, ff_going, ff_going_second = middle_step(ff_blocks[:2], after(ff_first, output_term))
-    ff_second = second_step([ff_going, ff_going_second])
-    hidden_out = spread_rows(after(out_sum, output_term)) + reduce_bias
-    block_own = (residual + own_pieces[5] * hidden_out).astype(jnp.bfloat16)
-    grad_gate_hidden = jnp.sum(upstream * hidden_out, axis=0, keepdims=True)
+    out_keep, out_send = halve(own_out, swap(other_out, "dp", 1))
+    mark(OUT_SEND, out_send)
+    output_low, grad_residual, row_sums = kernel_call(
+        hidden_back_body,
+        "hidden_back",
+        [(keep.shape, jnp.bfloat16), (keep.shape, jnp.float32), ((8, model_width), jnp.float32)],
+        [
+            keep,
+            hold(HIDDEN_BACK, got),
+            residual,
+            attend_out,
+            upstream_half,
+            gate_a,
+            gain_m,
+            gate_m,
+        ],
+        [],
+        8,
+        0,
+    )
+    output_pieces = collect_pairs(output_low)
+    mark(OUTPUT_NEAR, output_pieces[1])
+    block_own, gate_sum = kernel_call(
+        block_out_body,
+        "block_out",
+        [(keep.shape, jnp.bfloat16), row],
+        [
+            out_keep,
+            swap(out_send, "tensor", 1),
+            residual,
+            upstream_half,
+            reduce_bias[None],
+            gate_m,
+        ],
+        [],
+        8,
+        0,
+    )
+    mark(BLOCK_OUT, block_own)
+
+    def ff_middle():
+        *bases, going, going_second = middle_step(ff_blocks[:2], hold(FF_MIDDLE, ff_first))
+        mark(FF_GOING, going)
+        return bases, second_step([going, going_second])
+
+    ff_bases, ff_second = ff_middle()
 
     (
         output_rows,
@@ -948,7 +1234,7 @@
         own_partial,
         other_partial,
     ) = attend_back(
-        after(output_pieces, out_sum, ff_going),
+        hold(ATTEND_BACK, output_pieces),
         output_full,
         projected,
         mixed_rows,
@@ -957,30 +1243,12 @@
         head_count,
         score_scale,
     )
-    attend_sum = own_partial + swap(other_partial, "dp", 1)
-    norm_crossed = swap(norm_sums[1:], "dp", 1)
-    grad_attend_in = spread_rows(attend_sum)
-    attn_blocks = grad_blocks(
-        [(attend_rows, after(projected_low, norm_crossed)), (output_rows, mixed_rows)], chip
-    )
-    attn_first = first_step(attn_blocks[2:])
-    tokens_grad_own = grad_residual + norm_back(
-        grad_attend_in * (1.0 + own_pieces[1]), normed_first, inverse_first
-    )
-
-    count = tokens_grad_own.shape[0] // 2
-    far = swap(
-        jnp.concatenate([block_own[count:], tokens_grad_own[count:].astype(jnp.bfloat16)]),
-        "tensor",
-        2,
-    )
-    block_output, tokens_grad = (
-        jnp.where(half == 0, jnp.stack([own, moved]), jnp.stack([moved, own]))
-        for own, moved in (
-            (block_own[:count], far[:count]),
-            (tokens_grad_own[:count], far[count:].astype(jnp.float32)),
-        )
-    )
+    block_moved = swap(hold(BLOCK_MOVED, block_own[count:]), "tensor", 2)
+    norm_crossed = mark(NORM_CROSSED, swap(norm_sums[1:], "dp", 1))
+    ff_mine, ff_other = core_step(core, ff_bases, hold(FF_CORE, ff_second))
+    mark(FF_CORE, ff_mine)
+    ff_kept, ff_sent = half_step(is_own, ff_mine, swap(ff_other, "dp", 1))
+    mark(FF_HALF, ff_sent)
 
     line = kernel_call(
         pack_body,
@@ -988,13 +1256,9 @@
         [((8, mod_width), jnp.float32)],
         [
             norm_sums,
-            norm_crossed,
-            grad_gate_attend,
-            grad_shift_hidden,
-            grad_scale_hidden,
-            grad_gate_hidden,
-            grad_output_bias,
-            grad_reduce_bias,
+            hold(PACK, norm_crossed),
+            row_sums,
+            gate_sum,
             grad_expand_bias,
             bias_sums,
         ],
@@ -1002,22 +1266,47 @@
         4,
         0,
     )[0]
+    mark(PACK, line)
+    keep, send = halve(own_partial, swap(other_partial, "dp", 1))
+    grad_got = swap(send, "tensor", 1)
+    attn_blocks = grad_blocks(
+        [(attend_rows, hold(ATTN_BLOCKS, projected_low)), (output_rows, mixed_rows)], chip
+    )
+    mark(ATTN_BLOCKS, attn_blocks[2])
+    attn_first = first_step(attn_blocks[2:])
     summed = lax.broadcasted_iota(jnp.int32, line.shape, 0) < 6
-    line = line + jnp.where(summed, swap(line, "tensor", 1), 0.0)
-    far = swap(line, "tensor", 2)
-    ff_mine, ff_other = core_step(core, ff_bases, ff_second)
-    ff_kept, ff_sent = half_step(is_own, ff_mine, swap(ff_other, "dp", 1))
-    ff_moved = swap(after(ff_sent, far), "tensor", 2)
-    place = jnp.stack([tensor_index, half, is_own.astype(jnp.int32)])
+    near = hold(LINE, swap(hold(LINE_NEAR, line), "tensor", 1))
+    line = line + jnp.where(summed, near, 0.0)
+    far = mark(FAR, swap(hold(LINE_FAR, line), "tensor", 2))
     packed = kernel_call(
-        choose_body, "choose", [((5, mod_width), jnp.float32)], [place, line, far], [], 4, 0
-    )[0][None]
-    packed = jnp.concatenate([packed, swap(packed, "dp", 1)], axis=0)
-    *attn_bases, attn_going, attn_going_second = middle_step(attn_blocks[:2], attn_first)
-    packed = after(packed, attn_going, grad_attend_in, ff_sent)
-    packed = jnp.concatenate([packed, swap(packed, "dp", 2)], axis=0)
+        choose_body,
+        "choose",
+        [((8, mod_width), jnp.float32)],
+        [place, line, far],
+        [],
+        4,
+        0,
+    )[0]
+    ff_moved = mark(FF_MOVED, swap(ff_sent, "tensor", 2))
+    tokens_kept, back_sent = kernel_call(
+        tokens_back_body,
+        "tokens_back",
+        [((count, model_width), jnp.float32), ((count, model_width), jnp.bfloat16)],
+        [keep, grad_got, tokens_half, grad_residual, gain_a],
+        [],
+        8,
+        0,
+    )
+    tokens_moved = swap(hold(BACK_SENT, back_sent), "tensor", 2)
+    *attn_bases, attn_going, attn_going_second = middle_step(
+        attn_blocks[:2], attn_first
+    )
     attn_second = second_step([attn_going, attn_going_second])
-    packed = jnp.concatenate([packed, swap(packed, "dp", 4)], axis=0)
+    packed = jnp.concatenate([packed, swap(packed, "dp", 1)])
+    packed = jnp.concatenate([packed, swap(hold(PACKED_X, packed), "dp", 2)])
+    attn_mine, attn_other = core_step(core, attn_bases, attn_second)
+    mark(ATTN_CORE, attn_mine)
+    packed = jnp.concatenate([packed, swap(hold(PACKED_Y, packed), "dp", 4)])
     modulation_weight_grad, grad_silu, modulation_bias_grad, rest = kernel_call(
         modulation_back_body,
         "modulation_back",
@@ -1027,40 +1316,61 @@
             ((1, mod_width), jnp.float32),
             ((3, mod_width), jnp.float32),
         ],
-        [packed, silu_act, modulation_weight],
+        [hold(MODULATION_BACK, packed), silu_act, modulation_weight],
         [pltpu.VMEM((latent_total, mod_width), jnp.float32)],
         8,
         4 * latent_total * row_share * mod_width,
     )
-    attn_mine, attn_other = core_step(core, attn_bases, attn_second)
-    grad_silu = after(grad_silu, attn_mine, tokens_grad_own)
-    near = grad_silu + swap(grad_silu, "tensor", 1)
-    attn_kept, attn_sent = half_step(is_own, attn_mine, swap(attn_other, "dp", 1))
-    attn_grad = attn_kept + swap(attn_sent, "tensor", 2).astype(jnp.float32)
-    ff_grad = ff_kept + after(ff_moved, near).astype(jnp.float32)
+    mark(MODULATION_BACK, grad_silu)
+    attn_kept, attn_sent = half_step(is_own, attn_mine, hold(ATTN_HALF, swap(attn_other, "dp", 1)))
+    attn_moved = swap(attn_sent, "tensor", 2)
+    near = grad_silu + swap(hold(GRAD_SILU, grad_silu), "tensor", 1)
+    mark(NEAR, near)
     table_grad = kernel_call(
         table_body,
         "table",
-        [((classes_total, row_share), jnp.float32)],
+        [((row_share, classes_total), jnp.float32)],
         [labels_rel, cond, near, swap(near, "tensor", 2)],
-        [],
+        [pltpu.VMEM((latent_total, classes_total), jnp.float32)],
         4,
         0,
     )[0]
+    mark(TABLE, table_grad)
+    expand_grad, reduce_grad = owner_sum(
+        ff_kept, hold(FF_OWNER, ff_moved), [ff_width, ff_width]
+    )
+    attend_grad, output_grad = kernel_call(
+        attend_owner_body,
+        "owner_sum",
+        [((3, row_share, head_width), jnp.float32), (output_weight.shape, jnp.float32)],
+        [attn_kept, hold(ATTN_OWNER, attn_moved)],
+        [],
+        8,
+        0,
+    )
+    block_output, tokens_grad = kernel_call(
+        outputs_body,
+        "outputs",
+        [(tokens.shape, jnp.bfloat16), (tokens.shape, jnp.float32)],
+        [half.reshape(1), block_own, block_moved, tokens_kept, hold(OUTPUTS, tokens_moved)],
+        [],
+        8,
+        0,
+    )
     wide = model_width
     return (
         block_output,
         tokens_grad,
-        table_grad,
+        table_grad.T,
         modulation_weight_grad,
         modulation_bias_grad[0],
-        attn_grad[:, : 3 * head_width].reshape(row_share, 3, head_width),
+        jnp.transpose(attend_grad, (1, 0, 2)),
         rest[0, wide:].reshape(2, head_width),
-        attn_grad[:, 3 * head_width :],
+        output_grad,
         rest[1, :wide],
-        ff_grad[:, :ff_width],
+        expand_grad,
         rest[0, :wide],
-        ff_grad[:, ff_width:],
+        reduce_grad,
         jnp.concatenate([rest[1, wide:], rest[2, : 2 * wide - mod_width]]),
     )
 

time: 211 us -> 166 us (0.79)
  waiting for transfers between devices: 93.9 us -> 59.8 us
  local copies, waits for them, and re-layouts: 26.9 us -> 5.41 us
  starting transfers between devices: 48 us -> 65.9 us
  other arithmetic: 18 us -> 7.34 us
  Pallas kernels: 18 us -> 24.1 us
    ppermute x58 -> x59, waiting for transfers between devices: 93.9 us -> 59.8 us  [swap(): lax.ppermute(values, axis, [(place, place ^ mask) for place in range(coun...]
    ppermute x58 -> x59, starting transfers between devices: 48 us -> 65.9 us  [swap(): lax.ppermute(values, axis, [(place, place ^ mask) for place in range(coun...]
    slice x24 -> x3, local copies, waits for them, and re-layouts: 11.8 us -> 0.66 us  [the longest x1 0.65 us: on_paired_device(): block_moved = swap(hold(BLOCK_MOVED, block_own[count:]), 'tensor', 2)]
    pallas_call x14 -> x28, Pallas kernels: 18 us -> 24.1 us  [kernel_call(): pl.pallas_call(body, out_shape=shapes, in_specs=specs, out_specs=[pl.Bloc...]
    unnamed x102 -> x31, local copies, waits for them, and re-layouts: 7.87 us -> 1.9 us
    select_n x6 -> x0, other arithmetic: 4.04 us -> none  [the longest x2 1.47 us: on_paired_device(): jnp.where(half == 0, jnp.stack([own, moved]), jnp.stack([moved, own]))]
    reduce_sum x8 -> x0, other arithmetic: 4.03 us -> none  [the longest x1 1.56 us: on_paired_device(): grad_output_bias = jnp.sum(output_term, axis=0, keepdims=True)]
  transfers between devices with their start and end apart: 58 -> 59, of which waited for: 27 -> 24; matrix products, arithmetic and copies ran while one was open for 18% -> 8% of each run, Pallas kernels for 4% -> 9%
where the time goes in v3:
time: 166 us
  starting transfers between devices  65.9 us (40%)
  waiting for transfers between devices  59.8 us (36%)
  Pallas kernels  24.1 us (15%)
  other arithmetic  7.34 us (4%)
  local copies, waits for them, and re-layouts  5.41 us (3%)
  matrix products  2.09 us (1%)
    ppermute x59, starting transfers between devices, swap(): lax.ppermute(values, axis, [(place, place ^ mask) for place in range(coun...  65.9 us
    ppermute x59, waiting for transfers between devices, swap(): lax.ppermute(values, axis, [(place, place ^ mask) for place in range(coun...  59.8 us
    pallas_call x28, Pallas kernels, kernel_call(): pl.pallas_call(body, out_shape=shapes, in_specs=specs, out_specs=[pl.Bloc...  24.1 us
  transfers between devices with their start and end apart: 59, of which 24 were waited for; matrix products, arithmetic and copies ran while one was open for 8% of the time, Pallas kernels for 9%

profile of v3, /device:TPU:0, one launch (start us, length us, event | category | flops | bytes accessed | tf_op | source)
XLA Modules:
  0.0 165.8 jit_solution(13727522190415222323)
XLA Ops:
  2.6 4.1 %collective-permute-start.6 = (bf16[96,768]{1,0:T(8,128)(2,1)S(1)}, bf16[96,768]{1,0:T(8,128)(2,1)S(1)}, u32[]{:S(2)}, u32[]{:S(2)}) collective-permute-start(bf16[96,768]{1,0:T(8,128)(2,1)S(1)} %join_weights.1), channel_id=1, source_target_pairs={{0,2},{1,3},{2,0},{3,1},{4,6},{5,7},{6,4},{7,5},{8,10},{9,11},{10,... | collective-permute-start | bytes 442376 | tf_op jit(solution)/shard_map/ppermute | solution.py:324
  9.5 1.6 collective-permute-start.4
  12.3 2.7 %collective-permute-start.3 = (bf16[96,1536]{1,0:T(8,128)(2,1)S(1)}, bf16[96,1536]{1,0:T(8,128)(2,1)}, u32[]{:S(2)}, u32[]{:S(2)}) collective-permute-start(bf16[96,1536]{1,0:T(8,128)(2,1)S(1)} %constant_dynamic-update-slice_fusion), channel_id=1, source_target_pairs={{0,2},{1,3},{2,0},{3,1},{4,6},{5,7},{6,4},{7,5},{8,10},{9,11},{10,... | collective-permute-start | bytes 884744 | tf_op jit(solution)/shard_map/ppermute | solution.py:324
  15.2 1.6 collective-permute-start.5
  16.8 1.3 collective-permute-start.12
  19.0 7.4 %collective-permute-done = bf16[64,768]{1,0:T(8,128)(2,1)S(1)} collective-permute-done((bf16[64,768]{1,0:T(8,128)(2,1)S(1)}, bf16[64,768]{1,0:T(8,128)(2,1)S(1)}, u32[]{:S(2)}, u32[]{:S(2)}) %collective-permute-start) | collective-permute-done | bytes 98336 | tf_op jit(solution)/shard_map/ppermute | solution.py:324
  28.6 5.1 %collective-permute-start.9 = (f32[8,1152]{1,0:T(8,128)S(1)}, f32[8,1152]{1,0:T(8,128)S(1)}, u32[]{:S(2)}, u32[]{:S(2)}) collective-permute-start(f32[8,1152]{1,0:T(8,128)S(1)} %mod_sum.1.own), channel_id=1, source_target_pairs={{0,1},{1,0},{2,3},{3,2},{4,5},{5,4},{6,7},{7,6},{8,9},{9,8},{10,11... | collective-permute-start | bytes 110600 | tf_op jit(solution)/shard_map/ppermute | solution.py:324
  33.8 1.6 collective-permute-start.14
  36.3 1.7 %broadcast_select_fusion = bf16[96,1536]{1,0:T(8,128)(2,1)} fusion(bf16[96,1536]{1,0:T(8,128)(2,1)} %collective-permute-done.3, bf16[96,1536]{1,0:T(8,128)(2,1)S(1)} %constant_dynamic-update-slice_fusion, pred[]{:T(512)S(6)} %eq.21), kind=kLoop, calls=%fused_computation.14 | loop fusion | flops 147456 | bytes 884737 | tf_op jit(solution)/shard_map/jit(_where)/select_n | solution.py:438
  38.1 2.7 %collective-permute-start.11 = (f32[16,1152]{1,0:T(8,128)S(1)}, f32[16,1152]{1,0:T(8,128)S(1)}, u32[]{:S(2)}, u32[]{:S(2)}) collective-permute-start(f32[16,1152]{1,0:T(8,128)S(1)} %pad_maximum_fusion.12), channel_id=1, source_target_pairs={{0,2},{1,3},{2,0},{3,1},{4,6},{5,7},{6,4},{7,5},{8,10},{9,11},{10,... | collective-permute-start | bytes 221192 | tf_op jit(solution)/shard_map/ppermute | solution.py:324
  41.8 3.5 %collective-permute-done.11.far = f32[16,1152]{1,0:T(8,128)S(1)} collective-permute-done((f32[16,1152]{1,0:T(8,128)S(1)}, f32[16,1152]{1,0:T(8,128)S(1)}, u32[]{:S(2)}, u32[]{:S(2)}) %collective-permute-start.11) | collective-permute-done | bytes 73760 | tf_op jit(solution)/shard_map/ppermute | solution.py:324
  47.6 4.0 %attend_forward.1 = (bf16[512,768]{1,0:T(8,128)(2,1)S(1)}, f32[512,768]{1,0:T(8,128)S(1)}, bf16[512,576]{1,0:T(8,128)(2,1)S(1)}, bf16[512,192]{1,0:T(8,128)(2,1)...) custom-call(s32[1]{0:T(128)} %bitcast.1.chip_ref, ...), custom_call_target="tpu_custom_call" | custom-call | flops 704643072 | bytes 7903492 | tf_op jit(solution)/shard_map/attend_forward/pallas_call | solution.py:537
  51.7 1.2 collective-permute-start.24
  52.9 2.6 %collective-permute-start.18 = (bf16[64,768]{1,0:T(8,128)(2,1)S(1)}, bf16[64,768]{1,0:T(8,128)(2,1)S(1)}, u32[]{:S(2)}, u32[]{:S(2)}) collective-permute-start(bf16[64,768]{1,0:T(8,128)(2,1)S(1)} %get-tuple-element.139), channel_id=1, source_target_pairs={{0,2},{1,3},{2,0},{3,1},{4,6},{5,7},{6,4},{7,5},{8,10},{9,11},{10,... | collective-permute-start | bytes 294920 | tf_op jit(solution)/shard_map/ppermute | solution.py:324
  55.5 5.3 %collective-permute-done.18 = bf16[64,768]{1,0:T(8,128)(2,1)S(1)} collective-permute-done((bf16[64,768]{1,0:T(8,128)(2,1)S(1)}, bf16[64,768]{1,0:T(8,128)(2,1)S(1)}, u32[]{:S(2)}, u32[]{:S(2)}) %collective-permute-start.18) | collective-permute-done | bytes 98336 | tf_op jit(solution)/shard_map/ppermute | solution.py:324
  61.4 1.7 %collective-permute-start.17 = (bf16[128,768]{1,0:T(8,128)(2,1)S(1)}, bf16[128,768]{1,0:T(8,128)(2,1)S(1)}, u32[]{:S(2)}, u32[]{:S(2)}) collective-permute-start(bf16[128,768]{1,0:T(8,128)(2,1)S(1)} %get-tuple-element.138), channel_id=1, source_target_pairs={{0,1},{1,0},{2,3},{3,2},{4,5},{5,4},{6,7},{7,6},{8,9},{9,8},{10,11... | collective-permute-start | bytes 589832 | tf_op jit(solution)/shard_map/ppermute | solution.py:324
  64.2 1.8 %collective-permute-start.26 = (bf16[192,1536]{1,0:T(8,128)(2,1)S(1)}, bf16[192,1536]{1,0:T(8,128)(2,1)S(1)}, u32[]{:S(2)}, u32[]{:S(2)}) collective-permute-start(bf16[192,1536]{1,0:T(8,128)(2,1)S(1)} %pad_maximum_fusion), channel_id=1, source_target_pairs={{0,16},{4,20},{8,24},{12,28},{16,0},{20,4},{24,8},{28,12},{1,17},{... | collective-permute-start | bytes 1769480 | tf_op jit(solution)/shard_map/ppermute | solution.py:324
  66.0 2.7 %collective-permute-done.22.refs_5_ = bf16[128,768]{1,0:T(8,128)(2,1)S(1)} collective-permute-done((bf16[128,768]{1,0:T(8,128)(2,1)S(1)}, bf16[128,768]{1,0:T(8,128)(2,1)S(1)}, u32[]{:S(2)}, u32[]{:S(2)}) %collective-permute-start.22) | collective-permute-done | bytes 196640 | tf_op jit(solution)/shard_map/ppermute | solution.py:324
  68.9 2.4 %collective-permute-done.17.got = bf16[128,768]{1,0:T(8,128)(2,1)S(1)} collective-permute-done((bf16[128,768]{1,0:T(8,128)(2,1)S(1)}, bf16[128,768]{1,0:T(8,128)(2,1)S(1)}, u32[]{:S(2)}, u32[]{:S(2)}) %collective-permute-start.17) | collective-permute-done | bytes 196640 | tf_op jit(solution)/shard_map/ppermute | solution.py:324
  72.7 4.6 %collective-permute-done.19.refs_1_ = bf16[128,768]{1,0:T(8,128)(2,1)S(1)} collective-permute-done((bf16[128,768]{1,0:T(8,128)(2,1)S(1)}, bf16[128,768]{1,0:T(8,128)(2,1)S(1)}, u32[]{:S(2)}, u32[]{:S(2)}) %collective-permute-start.19) | collective-permute-done | bytes 196640 | tf_op jit(solution)/shard_map/ppermute | solution.py:324
  78.7 4.2 %feed_forward.1 = (bf16[512,768]{1,0:T(8,128)(2,1)S(1)}, f32[1,768]{1,0:T(1,128)S(1)}, bf16[768,768]{1,0:T(8,128)(2,1)S(1)}, f32[256,768]{1,0:T(8,128)S(1)}, f32...) custom-call(s32[1]{0:T(128)} %bitcast.1.chip_ref, ...), custom_call_target="tpu_custom_call" | custom-call | flops 3019898880 | bytes 11053060 | tf_op jit(solution)/shard_map/feed_forward/pallas_call | solution.py:537
  84.0 1.2 collective-permute-done.30.got
  86.1 1.7 %collective-permute-start.37 = (bf16[192,1536]{1,0:T(8,128)(2,1)S(1)}, bf16[192,1536]{1,0:T(8,128)(2,1)S(1)}, u32[]{:S(2)}, u32[]{:S(2)}) collective-permute-start(bf16[192,1536]{1,0:T(8,128)(2,1)S(1)} %get-tuple-element.169), channel_id=1, source_target_pairs={{0,16},{4,20},{8,24},{12,28},{16,0},{20,4},{24,8},{28,12},{1,17},{... | collective-permute-start | bytes 1769480 | tf_op jit(solution)/shard_map/ppermute | solution.py:324
  87.9 1.6 collective-permute-start.31
  90.6 5.1 %collective-permute-done.31.got = bf16[128,768]{1,0:T(8,128)(2,1)S(1)} collective-permute-done((bf16[128,768]{1,0:T(8,128)(2,1)S(1)}, bf16[128,768]{1,0:T(8,128)(2,1)S(1)}, u32[]{:S(2)}, u32[]{:S(2)}) %collective-permute-start.31) | collective-permute-done | bytes 196640 | tf_op jit(solution)/shard_map/ppermute | solution.py:324
  96.4 1.6 collective-permute-start.32
  98.0 1.9 %collective-permute-done.29.got = bf16[128,768]{1,0:T(8,128)(2,1)S(1)} collective-permute-done((bf16[128,768]{1,0:T(8,128)(2,1)S(1)}, bf16[128,768]{1,0:T(8,128)(2,1)S(1)}, u32[]{:S(2)}, u32[]{:S(2)}) %collective-permute-start.29) | collective-permute-done | bytes 196640 | tf_op jit(solution)/shard_map/ppermute | solution.py:324
  100.0 2.6 %collective-permute-done.32.refs_1_ = bf16[128,768]{1,0:T(8,128)(2,1)S(1)} collective-permute-done((bf16[128,768]{1,0:T(8,128)(2,1)S(1)}, bf16[128,768]{1,0:T(8,128)(2,1)S(1)}, u32[]{:S(2)}, u32[]{:S(2)}) %collective-permute-start.32) | collective-permute-done | bytes 196640 | tf_op jit(solution)/shard_map/ppermute | solution.py:324
  103.3 1.3 collective-permute-start.42
  106.2 4.2 %attend_back.1 = (bf16[512,768]{1,0:T(8,128)(2,1)S(1)}, bf16[512,576]{1,0:T(8,128)(2,1)S(1)}, f32[1,576]{1,0:T(1,128)S(1)}, f32[2,1536]{1,0:T(2,128)S(1)}, f32[2...) custom-call(bf16[128,768]{1,0:T(8,128)(2,1)S(1)} %get-tuple-element.173.refs_0_, ...), custom_call_target="tpu_custom_call" | custom-call | flops 855638016 | bytes 7289088 | tf_op jit(solution)/shard_map/attend_back/pallas_call | solution.py:537
  112.6 1.4 collective-permute-start.43
  113.9 1.2 grad_blocks.1
  115.3 1.2 collective-permute-done.43
  116.6 3.3 %collective-permute-start.45 = (f32[8,1152]{1,0:T(8,128)S(1)}, f32[8,1152]{1,0:T(8,128)S(1)}, u32[]{:S(2)}, u32[]{:S(2)}) collective-permute-start(f32[8,1152]{1,0:T(8,128)S(1)} %select_add_fusion.line), channel_id=1, source_target_pairs={{0,2},{1,3},{2,0},{3,1},{4,6},{5,7},{6,4},{7,5},{8,10},{9,11},{10,... | collective-permute-start | bytes 110600 | tf_op jit(solution)/shard_map/ppermute | solution.py:324
  119.9 1.9 %collective-permute-done.45.far = f32[8,1152]{1,0:T(8,128)S(1)} collective-permute-done((f32[8,1152]{1,0:T(8,128)S(1)}, f32[8,1152]{1,0:T(8,128)S(1)}, u32[]{:S(2)}, u32[]{:S(2)}) %collective-permute-start.45) | collective-permute-done | bytes 36896 | tf_op jit(solution)/shard_map/ppermute | solution.py:324
  122.5 1.2 collective-permute-start.51
  123.7 1.5 collective-permute-start.52
  126.2 3.0 %collective-permute-start.49 = (bf16[96,1536]{1,0:T(8,128)(2,1)S(1)}, bf16[96,1536]{1,0:T(8,128)(2,1)S(1)}, u32[]{:S(2)}, u32[]{:S(2)}) collective-permute-start(bf16[96,1536]{1,0:T(8,128)(2,1)S(1)} %get-tuple-element.204), channel_id=1, source_target_pairs={{0,2},{1,3},{2,0},{3,1},{4,6},{5,7},{6,4},{7,5},{8,10},{9,11},{10,... | collective-permute-start | bytes 884744 | tf_op jit(solution)/shard_map/ppermute | solution.py:324
  129.2 3.2 %collective-permute-done.51.got_first = bf16[192,768]{1,0:T(8,128)(2,1)S(1)} collective-permute-done((bf16[192,768]{1,0:T(8,128)(2,1)S(1)}, bf16[192,768]{1,0:T(8,128)(2,1)S(1)}, u32[]{:S(2)}, u32[]{:S(2)}) %collective-permute-start.51) | collective-permute-done | bytes 294944 | tf_op jit(solution)/shard_map/ppermute | solution.py:324
  132.9 1.6 collective-permute-start.53
  135.5 1.5 collective-permute-start.39
  137.0 5.4 %collective-permute-done.49.moved = bf16[96,1536]{1,0:T(8,128)(2,1)S(1)} collective-permute-done((bf16[96,1536]{1,0:T(8,128)(2,1)S(1)}, bf16[96,1536]{1,0:T(8,128)(2,1)S(1)}, u32[]{:S(2)}, u32[]{:S(2)}) %collective-permute-start.49) | collective-permute-done | bytes 294944 | tf_op jit(solution)/shard_map/ppermute | solution.py:324
  143.8 2.4 %collective-permute-done.39.got = bf16[128,768]{1,0:T(8,128)(2,1)S(1)} collective-permute-done((bf16[128,768]{1,0:T(8,128)(2,1)S(1)}, bf16[128,768]{1,0:T(8,128)(2,1)S(1)}, u32[]{:S(2)}, u32[]{:S(2)}) %collective-permute-start.39) | collective-permute-done | bytes 196640 | tf_op jit(solution)/shard_map/ppermute | solution.py:324
  146.6 2.0 %collective-permute-start.46 = (bf16[64,768]{1,0:T(8,128)(2,1)S(1)}, bf16[64,768]{1,0:T(8,128)(2,1)S(1)}, u32[]{:S(2)}, u32[]{:S(2)}) collective-permute-start(bf16[64,768]{1,0:T(8,128)(2,1)S(1)} %get-tuple-element.212), channel_id=1, source_target_pairs={{0,2},{1,3},{2,0},{3,1},{4,6},{5,7},{6,4},{7,5},{8,10},{9,11},{10,... | collective-permute-start | bytes 294920 | tf_op jit(solution)/shard_map/ppermute | solution.py:324
  149.6 2.5 %collective-permute-start.55 = (f32[16,96]{1,0:T(8,128)S(1)}, f32[16,96]{1,0:T(8,128)S(1)}, u32[]{:S(2)}, u32[]{:S(2)}) collective-permute-start(f32[16,96]{1,0:T(8,128)S(1)} %get-tuple-element.228), channel_id=1, source_target_pairs={{0,1},{1,0},{2,3},{3,2},{4,5},{5,4},{6,7},{7,6},{8,9},{9,8},{10,11... | collective-permute-start | bytes 18440 | tf_op jit(solution)/shard_map/ppermute | solution.py:324
  154.7 1.8 %collective-permute-start.56 = (f32[16,96]{1,0:T(8,128)S(1)}, f32[16,96]{1,0:T(8,128)S(1)}, u32[]{:S(2)}, u32[]{:S(2)}) collective-permute-start(f32[16,96]{1,0:T(8,128)S(1)} %add.85.near), channel_id=1, source_target_pairs={{0,2},{1,3},{2,0},{3,1},{4,6},{5,7},{6,4},{7,5},{8,10},{9,11},{10,... | collective-permute-start | bytes 18440 | tf_op jit(solution)/shard_map/ppermute | solution.py:324
  157.1 3.1 %collective-permute-done.46.moved = bf16[64,768]{1,0:T(8,128)(2,1)S(1)} collective-permute-done((bf16[64,768]{1,0:T(8,128)(2,1)S(1)}, bf16[64,768]{1,0:T(8,128)(2,1)S(1)}, u32[]{:S(2)}, u32[]{:S(2)}) %collective-permute-start.46) | collective-permute-done | bytes 98336 | tf_op jit(solution)/shard_map/ppermute | solution.py:324
  163.2 1.8 %table.1 = f32[96,1000]{1,0:T(8,128)} custom-call(s32[16]{0:T(128)S(1)} %get-tuple-element.249.labels, f32[16,96]{1,0:T(8,128)S(1)} %get-tuple-element.251.cond, f32[16,96]{1,0:T(8,128)S(1)} %add.85.near, f32[16,96]{1,0:T(8,128)S(1)} %collective-permute-done.56.far), custom_call_target="tpu_custom_call" | custom-call | bytes 402496 | tf_op jit(solution)/shard_map/table/pallas_call | solution.py:537
  (181 shorter events, 39.4 us)
Async XLA Ops:
  2.6 12.4 %collective-permute-start.6 = (bf16[96,768]{1,0:T(8,128)(2,1)S(1)}, bf16[96,768]{1,0:T(8,128)(2,1)S(1)}, u32[]{:S(2)}, u32[]{:S(2)}) collective-permute-start(bf16[96,768]{1,0:T(8,128)(2,1)S(1)} %join_weights.1), channel_id=1, source_target_pairs={{0,2},{1,3},{2,0},{3,1},{4,6},{5,7},{6,4},{7,5},{8,10},{9,11},{10,... | collective-permute-start | bytes 442376 | tf_op jit(solution)/shard_map/ppermute | solution.py:324
  9.5 5.7 %collective-permute-start.4 = (f32[8,1152]{1,0:T(8,128)S(1)}, f32[8,1152]{1,0:T(8,128)S(1)}, u32[]{:S(2)}, u32[]{:S(2)}) collective-permute-start(f32[8,1152]{1,0:T(8,128)S(1)} %slice.55), channel_id=1, source_target_pairs={{0,16},{4,20},{8,24},{12,28},{16,0},{20,4},{24,8},{28,12},{1,17},{... | collective-permute-start | bytes 110600 | tf_op jit(solution)/shard_map/ppermute | solution.py:324
  11.9 14.5 %collective-permute-start = (bf16[64,768]{1,0:T(8,128)(2,1)S(1)}, bf16[64,768]{1,0:T(8,128)(2,1)S(1)}, u32[]{:S(2)}, u32[]{:S(2)}) collective-permute-start(bf16[64,768]{1,0:T(8,128)(2,1)S(1)} %dynamic-slice_bitcast_fusion.2), channel_id=1, source_target_pairs={{0,2},{1,3},{2,0},{3,1},{4,6},{5,7},{6,4},{7,5},{8,10},{9,11},{10,... | collective-permute-start | bytes 294920 | tf_op jit(solution)/shard_map/ppermute | solution.py:324
  12.3 23.9 %collective-permute-start.3 = (bf16[96,1536]{1,0:T(8,128)(2,1)S(1)}, bf16[96,1536]{1,0:T(8,128)(2,1)}, u32[]{:S(2)}, u32[]{:S(2)}) collective-permute-start(bf16[96,1536]{1,0:T(8,128)(2,1)S(1)} %constant_dynamic-update-slice_fusion), channel_id=1, source_target_pairs={{0,2},{1,3},{2,0},{3,1},{4,6},{5,7},{6,4},{7,5},{8,10},{9,11},{10,... | collective-permute-start | bytes 884744 | tf_op jit(solution)/shard_map/ppermute | solution.py:324
  16.8 9.6 %collective-permute-start.12 = (bf16[96,768]{1,0:T(8,128)(2,1)S(1)}, bf16[96,768]{1,0:T(8,128)(2,1)S(1)}, u32[]{:S(2)}, u32[]{:S(2)}) collective-permute-start(bf16[96,768]{1,0:T(8,128)(2,1)S(1)} %get-tuple-element.255), channel_id=1, source_target_pairs={{0,8},{4,12},{8,0},{12,4},{16,24},{20,28},{24,16},{28,20},{1,9},{5... | collective-permute-start | bytes 442376 | tf_op jit(solution)/shard_map/ppermute | solution.py:324
  18.1 8.4 %collective-permute-start.13 = (bf16[96,768]{1,0:T(8,128)(2,1)S(1)}, bf16[96,768]{1,0:T(8,128)(2,1)S(1)}, u32[]{:S(2)}, u32[]{:S(2)}) collective-permute-start(bf16[96,768]{1,0:T(8,128)(2,1)S(1)} %get-tuple-element.254), channel_id=1, source_target_pairs={{0,16},{4,20},{8,24},{12,28},{16,0},{20,4},{24,8},{28,12},{1,17},{... | collective-permute-start | bytes 442376 | tf_op jit(solution)/shard_map/ppermute | solution.py:324
  28.6 7.6 %collective-permute-start.9 = (f32[8,1152]{1,0:T(8,128)S(1)}, f32[8,1152]{1,0:T(8,128)S(1)}, u32[]{:S(2)}, u32[]{:S(2)}) collective-permute-start(f32[8,1152]{1,0:T(8,128)S(1)} %mod_sum.1.own), channel_id=1, source_target_pairs={{0,1},{1,0},{2,3},{3,2},{4,5},{5,4},{6,7},{7,6},{8,9},{9,8},{10,11... | collective-permute-start | bytes 110600 | tf_op jit(solution)/shard_map/ppermute | solution.py:324
  33.7 7.1 %collective-permute-start.1 = (bf16[128,768]{1,0:T(8,128)(2,1)S(1)}, bf16[128,768]{1,0:T(8,128)(2,1)S(1)}, u32[]{:S(2)}, u32[]{:S(2)}) collective-permute-start(bf16[128,768]{1,0:T(8,128)(2,1)S(1)} %pad_maximum_fusion.9.refs_0_.tokens), channel_id=1, source_target_pairs={{0,1},{1,0},{2,3},{3,2},{4,5},{5,4},{6,7},{7,6},{8,9},{9,8},{10,11... | collective-permute-start | bytes 589832 | tf_op jit(solution)/shard_map/ppermute | solution.py:324
  33.8 11.4 %collective-permute-start.14 = (bf16[192,768]{1,0:T(8,128)(2,1)}, bf16[192,768]{1,0:T(8,128)(2,1)S(1)}, u32[]{:S(2)}, u32[]{:S(2)}) collective-permute-start(bf16[192,768]{1,0:T(8,128)(2,1)} %get-tuple-element.260), channel_id=1, source_target_pairs={{0,16},{4,20},{8,24},{12,28},{16,0},{20,4},{24,8},{28,12},{1,17},{... | collective-permute-start | bytes 884744 | tf_op jit(solution)/shard_map/ppermute | solution.py:324
  35.4 9.9 %collective-permute-start.15 = (bf16[192,768]{1,0:T(8,128)(2,1)}, bf16[192,768]{1,0:T(8,128)(2,1)}, u32[]{:S(2)}, u32[]{:S(2)}) collective-permute-start(bf16[192,768]{1,0:T(8,128)(2,1)} %get-tuple-element.258), channel_id=1, source_target_pairs={{0,8},{4,12},{8,0},{12,4},{16,24},{20,28},{24,16},{28,20},{1,9},{5... | collective-permute-start | bytes 884744 | tf_op jit(solution)/shard_map/ppermute | solution.py:324
  38.0 8.4 %collective-permute-start.10 = (bf16[96,1536]{1,0:T(8,128)(2,1)}, bf16[96,1536]{1,0:T(8,128)(2,1)}, u32[]{:S(2)}, u32[]{:S(2)}) collective-permute-start(bf16[96,1536]{1,0:T(8,128)(2,1)} %broadcast_select_fusion), channel_id=1, source_target_pairs={{0,4},{4,0},{8,12},{12,8},{16,20},{20,16},{24,28},{28,24},{1,5},{5... | collective-permute-start | bytes 884744 | tf_op jit(solution)/shard_map/ppermute | solution.py:324
  38.1 7.2 %collective-permute-start.11 = (f32[16,1152]{1,0:T(8,128)S(1)}, f32[16,1152]{1,0:T(8,128)S(1)}, u32[]{:S(2)}, u32[]{:S(2)}) collective-permute-start(f32[16,1152]{1,0:T(8,128)S(1)} %pad_maximum_fusion.12), channel_id=1, source_target_pairs={{0,2},{1,3},{2,0},{3,1},{4,6},{5,7},{6,4},{7,5},{8,10},{9,11},{10,... | collective-permute-start | bytes 221192 | tf_op jit(solution)/shard_map/ppermute | solution.py:324
  41.7 5.8 %collective-permute-start.2 = (bf16[256,768]{1,0:T(8,128)(2,1)S(1)}, bf16[256,768]{1,0:T(8,128)(2,1)S(1)}, u32[]{:S(2)}, u32[]{:S(2)}) collective-permute-start(bf16[256,768]{1,0:T(8,128)(2,1)S(1)} %pad_maximum_fusion.3), channel_id=1, source_target_pairs={{0,4},{4,0},{8,12},{12,8},{16,20},{20,16},{24,28},{28,24},{1,5},{5... | collective-permute-start | bytes 1179656 | tf_op jit(solution)/shard_map/ppermute | solution.py:324
  51.6 9.7 %collective-permute-start.16 = (f32[256,768]{1,0:T(8,128)S(1)}, f32[256,768]{1,0:T(8,128)S(1)}, u32[]{:S(2)}, u32[]{:S(2)}) collective-permute-start(f32[256,768]{1,0:T(8,128)S(1)} %get-tuple-element.136), channel_id=1, source_target_pairs={{0,4},{4,0},{8,12},{12,8},{16,20},{20,16},{24,28},{28,24},{1,5},{5... | collective-permute-start | bytes 2359304 | tf_op jit(solution)/shard_map/ppermute | solution.py:324
  51.7 11.5 %collective-permute-start.24 = (bf16[96,1536]{1,0:T(8,128)(2,1)S(1)}, bf16[96,1536]{1,0:T(8,128)(2,1)S(1)}, u32[]{:S(2)}, u32[]{:S(2)}) collective-permute-start(bf16[96,1536]{1,0:T(8,128)(2,1)S(1)} %get-tuple-element.253), channel_id=1, source_target_pairs={{0,8},{4,12},{8,0},{12,4},{16,24},{20,28},{24,16},{28,20},{1,9},{5... | collective-permute-start | bytes 884744 | tf_op jit(solution)/shard_map/ppermute | solution.py:324
  52.9 10.3 %collective-permute-start.25 = (bf16[96,1536]{1,0:T(8,128)(2,1)S(1)}, bf16[96,1536]{1,0:T(8,128)(2,1)S(1)}, u32[]{:S(2)}, u32[]{:S(2)}) collective-permute-start(bf16[96,1536]{1,0:T(8,128)(2,1)S(1)} %get-tuple-element.252), channel_id=1, source_target_pairs={{0,16},{4,20},{8,24},{12,28},{16,0},{20,4},{24,8},{28,12},{1,17},{... | collective-permute-start | bytes 884744 | tf_op jit(solution)/shard_map/ppermute | solution.py:324
  52.9 7.9 %collective-permute-start.18 = (bf16[64,768]{1,0:T(8,128)(2,1)S(1)}, bf16[64,768]{1,0:T(8,128)(2,1)S(1)}, u32[]{:S(2)}, u32[]{:S(2)}) collective-permute-start(bf16[64,768]{1,0:T(8,128)(2,1)S(1)} %get-tuple-element.139), channel_id=1, source_target_pairs={{0,2},{1,3},{2,0},{3,1},{4,6},{5,7},{6,4},{7,5},{8,10},{9,11},{10,... | collective-permute-start | bytes 294920 | tf_op jit(solution)/shard_map/ppermute | solution.py:324
  60.9 7.9 %collective-permute-start.22 = (bf16[128,768]{1,0:T(8,128)(2,1)S(1)}, bf16[128,768]{1,0:T(8,128)(2,1)S(1)}, u32[]{:S(2)}, u32[]{:S(2)}) collective-permute-start(bf16[128,768]{1,0:T(8,128)(2,1)S(1)} %pad_maximum_fusion.10.refs_4_.upstream), channel_id=1, source_target_pairs={{0,1},{1,0},{2,3},{3,2},{4,5},{5,4},{6,7},{7,6},{8,9},{9,8},{10,11... | collective-permute-start | bytes 589832 | tf_op jit(solution)/shard_map/ppermute | solution.py:324
  61.4 9.9 %collective-permute-start.17 = (bf16[128,768]{1,0:T(8,128)(2,1)S(1)}, bf16[128,768]{1,0:T(8,128)(2,1)S(1)}, u32[]{:S(2)}, u32[]{:S(2)}) collective-permute-start(bf16[128,768]{1,0:T(8,128)(2,1)S(1)} %get-tuple-element.138), channel_id=1, source_target_pairs={{0,1},{1,0},{2,3},{3,2},{4,5},{5,4},{6,7},{7,6},{8,9},{9,8},{10,11... | collective-permute-start | bytes 589832 | tf_op jit(solution)/shard_map/ppermute | solution.py:324
  63.2 14.1 %collective-permute-start.27 = (bf16[192,1536]{1,0:T(8,128)(2,1)S(1)}, bf16[192,1536]{1,0:T(8,128)(2,1)S(1)}, u32[]{:S(2)}, u32[]{:S(2)}) collective-permute-start(bf16[192,1536]{1,0:T(8,128)(2,1)S(1)} %pad_maximum_fusion.2), channel_id=1, source_target_pairs={{0,8},{4,12},{8,0},{12,4},{16,24},{20,28},{24,16},{28,20},{1,9},{5... | collective-permute-start | bytes 1769480 | tf_op jit(solution)/shard_map/ppermute | solution.py:324
  64.2 13.7 %collective-permute-start.26 = (bf16[192,1536]{1,0:T(8,128)(2,1)S(1)}, bf16[192,1536]{1,0:T(8,128)(2,1)S(1)}, u32[]{:S(2)}, u32[]{:S(2)}) collective-permute-start(bf16[192,1536]{1,0:T(8,128)(2,1)S(1)} %pad_maximum_fusion), channel_id=1, source_target_pairs={{0,16},{4,20},{8,24},{12,28},{16,0},{20,4},{24,8},{28,12},{1,17},{... | collective-permute-start | bytes 1769480 | tf_op jit(solution)/shard_map/ppermute | solution.py:324
  68.8 8.5 %collective-permute-start.23 = (bf16[256,768]{1,0:T(8,128)(2,1)S(1)}, bf16[256,768]{1,0:T(8,128)(2,1)S(1)}, u32[]{:S(2)}, u32[]{:S(2)}) collective-permute-start(bf16[256,768]{1,0:T(8,128)(2,1)S(1)} %pad_maximum_fusion.4), channel_id=1, source_target_pairs={{0,4},{4,0},{8,12},{12,8},{16,20},{20,16},{24,28},{28,24},{1,5},{5... | collective-permute-start | bytes 1179656 | tf_op jit(solution)/shard_map/ppermute | solution.py:324
  71.5 5.7 %collective-permute-start.19 = (bf16[128,768]{1,0:T(8,128)(2,1)S(1)}, bf16[128,768]{1,0:T(8,128)(2,1)S(1)}, u32[]{:S(2)}, u32[]{:S(2)}) collective-permute-start(bf16[128,768]{1,0:T(8,128)(2,1)S(1)} %get-tuple-element.144.refs_0_), channel_id=1, source_target_pairs={{0,1},{1,0},{2,3},{3,2},{4,5},{5,4},{6,7},{7,6},{8,9},{9,8},{10,11... | collective-permute-start | bytes 589832 | tf_op jit(solution)/shard_map/ppermute | solution.py:324
  72.7 4.6 %collective-permute-start.20 = (bf16[128,768]{1,0:T(8,128)(2,1)S(1)}, bf16[128,768]{1,0:T(8,128)(2,1)S(1)}, u32[]{:S(2)}, u32[]{:S(2)}) collective-permute-start(bf16[128,768]{1,0:T(8,128)(2,1)S(1)} %get-tuple-element.144.refs_0_), channel_id=1, source_target_pairs={{0,4},{4,0},{8,12},{12,8},{16,20},{20,16},{24,28},{28,24},{1,5},{5... | collective-permute-start | bytes 589832 | tf_op jit(solution)/shard_map/ppermute | solution.py:324
  83.6 6.3 %collective-permute-start.28 = (f32[256,768]{1,0:T(8,128)S(1)}, f32[256,768]{1,0:T(8,128)S(1)}, u32[]{:S(2)}, u32[]{:S(2)}) collective-permute-start(f32[256,768]{1,0:T(8,128)S(1)} %fusion), channel_id=1, source_target_pairs={{0,4},{4,0},{8,12},{12,8},{16,20},{20,16},{24,28},{28,24},{1,5},{5... | collective-permute-start | bytes 2359304 | tf_op jit(solution)/shard_map/ppermute | solution.py:324
  85.3 17.4 %collective-permute-start.36 = (bf16[192,1536]{1,0:T(8,128)(2,1)S(1)}, bf16[192,1536]{1,0:T(8,128)(2,1)S(1)}, u32[]{:S(2)}, u32[]{:S(2)}) collective-permute-start(bf16[192,1536]{1,0:T(8,128)(2,1)S(1)} %get-tuple-element.168), channel_id=1, source_target_pairs={{0,8},{4,12},{8,0},{12,4},{16,24},{20,28},{24,16},{28,20},{1,9},{5... | collective-permute-start | bytes 1769480 | tf_op jit(solution)/shard_map/ppermute | solution.py:324
  86.1 16.5 %collective-permute-start.37 = (bf16[192,1536]{1,0:T(8,128)(2,1)S(1)}, bf16[192,1536]{1,0:T(8,128)(2,1)S(1)}, u32[]{:S(2)}, u32[]{:S(2)}) collective-permute-start(bf16[192,1536]{1,0:T(8,128)(2,1)S(1)} %get-tuple-element.169), channel_id=1, source_target_pairs={{0,16},{4,20},{8,24},{12,28},{16,0},{20,4},{24,8},{28,12},{1,17},{... | collective-permute-start | bytes 1769480 | tf_op jit(solution)/shard_map/ppermute | solution.py:324
  87.9 7.8 %collective-permute-start.31 = (bf16[128,768]{1,0:T(8,128)(2,1)S(1)}, bf16[128,768]{1,0:T(8,128)(2,1)S(1)}, u32[]{:S(2)}, u32[]{:S(2)}) collective-permute-start(bf16[128,768]{1,0:T(8,128)(2,1)S(1)} %get-tuple-element.159), channel_id=1, source_target_pairs={{0,1},{1,0},{2,3},{3,2},{4,5},{5,4},{6,7},{7,6},{8,9},{9,8},{10,11... | collective-permute-start | bytes 589832 | tf_op jit(solution)/shard_map/ppermute | solution.py:324
  90.0 9.9 %collective-permute-start.29 = (bf16[128,768]{1,0:T(8,128)(2,1)S(1)}, bf16[128,768]{1,0:T(8,128)(2,1)S(1)}, u32[]{:S(2)}, u32[]{:S(2)}) collective-permute-start(bf16[128,768]{1,0:T(8,128)(2,1)S(1)} %get-tuple-element.153), channel_id=1, source_target_pairs={{0,1},{1,0},{2,3},{3,2},{4,5},{5,4},{6,7},{7,6},{8,9},{9,8},{10,11... | collective-permute-start | bytes 589832 | tf_op jit(solution)/shard_map/ppermute | solution.py:324
  96.4 6.3 %collective-permute-start.32 = (bf16[128,768]{1,0:T(8,128)(2,1)S(1)}, bf16[128,768]{1,0:T(8,128)(2,1)S(1)}, u32[]{:S(2)}, u32[]{:S(2)}) collective-permute-start(bf16[128,768]{1,0:T(8,128)(2,1)S(1)} %get-tuple-element.173.refs_0_), channel_id=1, source_target_pairs={{0,1},{1,0},{2,3},{3,2},{4,5},{5,4},{6,7},{7,6},{8,9},{9,8},{10,11... | collective-permute-start | bytes 589832 | tf_op jit(solution)/shard_map/ppermute | solution.py:324
  102.9 8.9 %collective-permute-start.41 = (bf16[96,1536]{1,0:T(8,128)(2,1)S(1)}, bf16[96,1536]{1,0:T(8,128)(2,1)S(1)}, u32[]{:S(2)}, u32[]{:S(2)}) collective-permute-start(bf16[96,1536]{1,0:T(8,128)(2,1)S(1)} %get-tuple-element.172), channel_id=1, source_target_pairs={{0,16},{4,20},{8,24},{12,28},{16,0},{20,4},{24,8},{28,12},{1,17},{... | collective-permute-start | bytes 884744 | tf_op jit(solution)/shard_map/ppermute | solution.py:324
  103.3 8.5 %collective-permute-start.42 = (bf16[96,1536]{1,0:T(8,128)(2,1)S(1)}, bf16[96,1536]{1,0:T(8,128)(2,1)S(1)}, u32[]{:S(2)}, u32[]{:S(2)}) collective-permute-start(bf16[96,1536]{1,0:T(8,128)(2,1)S(1)} %get-tuple-element.193), channel_id=1, source_target_pairs={{0,8},{4,12},{8,0},{12,4},{16,24},{20,28},{24,16},{28,20},{1,9},{5... | collective-permute-start | bytes 884744 | tf_op jit(solution)/shard_map/ppermute | solution.py:324
  112.2 23.2 %collective-permute-start.38 = (f32[256,768]{1,0:T(8,128)S(1)}, f32[256,768]{1,0:T(8,128)S(1)}, u32[]{:S(2)}, u32[]{:S(2)}) collective-permute-start(f32[256,768]{1,0:T(8,128)S(1)} %get-tuple-element.183), channel_id=1, source_target_pairs={{0,4},{4,0},{8,12},{12,8},{16,20},{20,16},{24,28},{28,24},{1,5},{5... | collective-permute-start | bytes 2359304 | tf_op jit(solution)/shard_map/ppermute | solution.py:324
  116.6 5.3 %collective-permute-start.45 = (f32[8,1152]{1,0:T(8,128)S(1)}, f32[8,1152]{1,0:T(8,128)S(1)}, u32[]{:S(2)}, u32[]{:S(2)}) collective-permute-start(f32[8,1152]{1,0:T(8,128)S(1)} %select_add_fusion.line), channel_id=1, source_target_pairs={{0,2},{1,3},{2,0},{3,1},{4,6},{5,7},{6,4},{7,5},{8,10},{9,11},{10,... | collective-permute-start | bytes 110600 | tf_op jit(solution)/shard_map/ppermute | solution.py:324
  122.5 9.9 %collective-permute-start.51 = (bf16[192,768]{1,0:T(8,128)(2,1)S(1)}, bf16[192,768]{1,0:T(8,128)(2,1)S(1)}, u32[]{:S(2)}, u32[]{:S(2)}) collective-permute-start(bf16[192,768]{1,0:T(8,128)(2,1)S(1)} %get-tuple-element.210), channel_id=1, source_target_pairs={{0,8},{4,12},{8,0},{12,4},{16,24},{20,28},{24,16},{28,20},{1,9},{5... | collective-permute-start | bytes 884744 | tf_op jit(solution)/shard_map/ppermute | solution.py:324
  123.7 9.1 %collective-permute-start.52 = (bf16[192,768]{1,0:T(8,128)(2,1)S(1)}, bf16[192,768]{1,0:T(8,128)(2,1)S(1)}, u32[]{:S(2)}, u32[]{:S(2)}) collective-permute-start(bf16[192,768]{1,0:T(8,128)(2,1)S(1)} %get-tuple-element.217), channel_id=1, source_target_pairs={{0,16},{4,20},{8,24},{12,28},{16,0},{20,4},{24,8},{28,12},{1,17},{... | collective-permute-start | bytes 884744 | tf_op jit(solution)/shard_map/ppermute | solution.py:324
  125.3 11.7 %collective-permute-start.48 = (f32[16,1152]{1,0:T(8,128)S(1)}, f32[16,1152]{1,0:T(8,128)S(1)}, u32[]{:S(2)}, u32[]{:S(2)}) collective-permute-start(f32[16,1152]{1,0:T(8,128)S(1)} %pad_maximum_fusion.13), channel_id=1, source_target_pairs={{0,8},{4,12},{8,0},{12,4},{16,24},{20,28},{24,16},{28,20},{1,9},{5... | collective-permute-start | bytes 221192 | tf_op jit(solution)/shard_map/ppermute | solution.py:324
  126.2 16.2 %collective-permute-start.49 = (bf16[96,1536]{1,0:T(8,128)(2,1)S(1)}, bf16[96,1536]{1,0:T(8,128)(2,1)S(1)}, u32[]{:S(2)}, u32[]{:S(2)}) collective-permute-start(bf16[96,1536]{1,0:T(8,128)(2,1)S(1)} %get-tuple-element.204), channel_id=1, source_target_pairs={{0,2},{1,3},{2,0},{3,1},{4,6},{5,7},{6,4},{7,5},{8,10},{9,11},{10,... | collective-permute-start | bytes 884744 | tf_op jit(solution)/shard_map/ppermute | solution.py:324
  132.9 10.0 %collective-permute-start.53 = (bf16[96,768]{1,0:T(8,128)(2,1)S(1)}, bf16[96,768]{1,0:T(8,128)(2,1)S(1)}, u32[]{:S(2)}, u32[]{:S(2)}) collective-permute-start(bf16[96,768]{1,0:T(8,128)(2,1)S(1)} %get-tuple-element.220), channel_id=1, source_target_pairs={{0,16},{4,20},{8,24},{12,28},{16,0},{20,4},{24,8},{28,12},{1,17},{... | collective-permute-start | bytes 442376 | tf_op jit(solution)/shard_map/ppermute | solution.py:324
  134.5 8.4 %collective-permute-start.54 = (bf16[96,768]{1,0:T(8,128)(2,1)S(1)}, bf16[96,768]{1,0:T(8,128)(2,1)S(1)}, u32[]{:S(2)}, u32[]{:S(2)}) collective-permute-start(bf16[96,768]{1,0:T(8,128)(2,1)S(1)} %get-tuple-element.221), channel_id=1, source_target_pairs={{0,8},{4,12},{8,0},{12,4},{16,24},{20,28},{24,16},{28,20},{1,9},{5... | collective-permute-start | bytes 442376 | tf_op jit(solution)/shard_map/ppermute | solution.py:324
  135.5 10.7 %collective-permute-start.39 = (bf16[128,768]{1,0:T(8,128)(2,1)S(1)}, bf16[128,768]{1,0:T(8,128)(2,1)S(1)}, u32[]{:S(2)}, u32[]{:S(2)}) collective-permute-start(bf16[128,768]{1,0:T(8,128)(2,1)S(1)} %get-tuple-element.185), channel_id=1, source_target_pairs={{0,1},{1,0},{2,3},{3,2},{4,5},{5,4},{6,7},{7,6},{8,9},{9,8},{10,11... | collective-permute-start | bytes 589832 | tf_op jit(solution)/shard_map/ppermute | solution.py:324
  142.4 6.1 %collective-permute-start.50 = (f32[32,1152]{1,0:T(8,128)S(1)}, f32[32,1152]{1,0:T(8,128)S(1)}, u32[]{:S(2)}, u32[]{:S(2)}) collective-permute-start(f32[32,1152]{1,0:T(8,128)S(1)} %pad_maximum_fusion.11), channel_id=1, source_target_pairs={{0,16},{4,20},{8,24},{12,28},{16,0},{20,4},{24,8},{28,12},{1,17},{... | collective-permute-start | bytes 442376 | tf_op jit(solution)/shard_map/ppermute | solution.py:324
  143.1 9.1 %collective-permute-start.57 = (f32[96,768]{1,0:T(8,128)S(1)}, f32[96,768]{1,0:T(8,128)S(1)}, u32[]{:S(2)}, u32[]{:S(2)}) collective-permute-start(f32[96,768]{1,0:T(8,128)S(1)} %get-tuple-element.231), channel_id=1, source_target_pairs={{0,4},{4,0},{8,12},{12,8},{16,20},{20,16},{24,28},{28,24},{1,5},{5... | collective-permute-start | bytes 884744 | tf_op jit(solution)/shard_map/ppermute | solution.py:324
  143.8 17.7 %collective-permute-start.33 = (bf16[64,768]{1,0:T(8,128)(2,1)}, bf16[64,768]{1,0:T(8,128)(2,1)S(1)}, u32[]{:S(2)}, u32[]{:S(2)}) collective-permute-start(bf16[64,768]{1,0:T(8,128)(2,1)} %slice.45), channel_id=1, source_target_pairs={{0,2},{1,3},{2,0},{3,1},{4,6},{5,7},{6,4},{7,5},{8,10},{9,11},{10,... | collective-permute-start | bytes 294920 | tf_op jit(solution)/shard_map/ppermute | solution.py:324
  146.6 13.6 %collective-permute-start.46 = (bf16[64,768]{1,0:T(8,128)(2,1)S(1)}, bf16[64,768]{1,0:T(8,128)(2,1)S(1)}, u32[]{:S(2)}, u32[]{:S(2)}) collective-permute-start(bf16[64,768]{1,0:T(8,128)(2,1)S(1)} %get-tuple-element.212), channel_id=1, source_target_pairs={{0,2},{1,3},{2,0},{3,1},{4,6},{5,7},{6,4},{7,5},{8,10},{9,11},{10,... | collective-permute-start | bytes 294920 | tf_op jit(solution)/shard_map/ppermute | solution.py:324
  149.6 5.0 %collective-permute-start.55 = (f32[16,96]{1,0:T(8,128)S(1)}, f32[16,96]{1,0:T(8,128)S(1)}, u32[]{:S(2)}, u32[]{:S(2)}) collective-permute-start(f32[16,96]{1,0:T(8,128)S(1)} %get-tuple-element.228), channel_id=1, source_target_pairs={{0,1},{1,0},{2,3},{3,2},{4,5},{5,4},{6,7},{7,6},{8,9},{9,8},{10,11... | collective-permute-start | bytes 18440 | tf_op jit(solution)/shard_map/ppermute | solution.py:324
  152.8 12.2 %collective-permute-start.58 = (bf16[96,768]{1,0:T(8,128)(2,1)}, bf16[96,768]{1,0:T(8,128)(2,1)S(1)}, u32[]{:S(2)}, u32[]{:S(2)}) collective-permute-start(bf16[96,768]{1,0:T(8,128)(2,1)} %get-tuple-element.234), channel_id=1, source_target_pairs={{0,2},{1,3},{2,0},{3,1},{4,6},{5,7},{6,4},{7,5},{8,10},{9,11},{10,... | collective-permute-start | bytes 442376 | tf_op jit(solution)/shard_map/ppermute | solution.py:324
  154.7 8.5 %collective-permute-start.56 = (f32[16,96]{1,0:T(8,128)S(1)}, f32[16,96]{1,0:T(8,128)S(1)}, u32[]{:S(2)}, u32[]{:S(2)}) collective-permute-start(f32[16,96]{1,0:T(8,128)S(1)} %add.85.near), channel_id=1, source_target_pairs={{0,2},{1,3},{2,0},{3,1},{4,6},{5,7},{6,4},{7,5},{8,10},{9,11},{10,... | collective-permute-start | bytes 18440 | tf_op jit(solution)/shard_map/ppermute | solution.py:324
  (26 other events, 154.8 us)

commit v4 on v3

--- a/solution.py
+++ b/solution.py
@@ -339,20 +339,17 @@
     ATTEND_BACK,
     ATTEND_SEND,
     ATTN_BLOCKS,
-    ATTN_CORE,
     ATTN_FAR,
     ATTN_HALF,
-    ATTN_OWNER,
     ATTN_PARTS,
+    ATTN_SENT,
     ATTN_SHARD,
     ATTN_SHARE,
     BACK_SENT,
-    BLOCK_MOVED,
     BLOCK_OUT,
     FAR,
     FEED,
-    FEED_SEND,
-    FF_BLOCKS,
+    FF_BACK_SECOND,
     FF_CORE,
     FF_FAR,
     FF_GOING,
@@ -361,12 +358,12 @@
     FF_MOVED,
     FF_OWNER,
     FF_SECOND,
+    FF_SHARD,
     FF_SHARE,
     GRAD_SILU,
     HIDDEN_BACK,
     LINE,
     LINE_FAR,
-    LINE_NEAR,
     MOD_LINE,
     MOD_PLACE,
     MODULATION_BACK,
@@ -376,7 +373,6 @@
     OUTPUT_NEAR,
     OUTPUTS,
     PACK,
-    PACKED_X,
     PACKED_Y,
     PARTIAL_CORE,
     RESIDUAL,
@@ -385,37 +381,34 @@
     TOKENS_SENT,
     UPSTREAM_HALF,
     UPSTREAM_SENT,
-) = range(51)
+) = range(47)
 
 HOLDS = {
     TOKENS_SENT: (ATTN_SHARD,),
-    PARTIAL_CORE: (ATTN_FAR, ATTN_SHARE, TOKENS_HALF,),
+    PARTIAL_CORE: (ATTN_SHARE,),
+    FF_SHARD: (ATTN_FAR, TOKENS_HALF,),
     MOD_PLACE: (ATTN_PARTS,),
     FF_FAR: (MOD_LINE,),
     UPSTREAM_SENT: (FF_FAR, FF_SHARE,),
     ATTEND: (FF_SHARE,),
     FF_SECOND: (ATTEND_SEND,),
     RESIDUAL: (UPSTREAM_HALF,),
-    FF_BLOCKS: (FEED_SEND,),
     ACTIVATED: (FEED,),
     HIDDEN_BACK: (OUT_SEND,),
     FF_MIDDLE: (BLOCK_OUT, OUTPUT_NEAR,),
     ATTEND_BACK: (BLOCK_OUT, FF_GOING,),
-    BLOCK_MOVED: (OUTPUT_NEAR,),
-    PACK: (FF_CORE,),
+    PACK: (FF_BACK_SECOND, FF_CORE,),
     ATTN_BLOCKS: (PACK,),
-    LINE_NEAR: (FF_CORE,),
     LINE: (FF_HALF,),
-    LINE_FAR: (ATTN_BLOCKS, FF_HALF,),
+    LINE_FAR: (ATTN_BLOCKS,),
     FF_CORE: (NORM_CROSSED,),
     BACK_SENT: (FAR,),
-    PACKED_X: (FF_CORE, FF_HALF,),
     PACKED_Y: (FF_MOVED,),
-    MODULATION_BACK: (ATTN_CORE,),
     ATTN_HALF: (MODULATION_BACK,),
+    ATTN_SENT: (FF_MOVED, MODULATION_BACK,),
     GRAD_SILU: (FF_MOVED,),
+    TABLE: (FF_MOVED,),
     FF_OWNER: (NEAR,),
-    ATTN_OWNER: (TABLE,),
     OUTPUTS: (MODULATION_BACK,),
 }
 
@@ -1083,7 +1076,7 @@
     mod_line = jnp.concatenate([mod_cols, mod_near])
     mark(MOD_LINE, mod_line)
     mod_far = swap(mod_line, "tensor", 2)
-    ff_far = mark(FF_FAR, swap(ff_shard, "tensor", 2))
+    ff_far = mark(FF_FAR, swap(hold(FF_SHARD, ff_shard), "tensor", 2))
     tokens_across = swap(jnp.concatenate([tokens_half, tokens_near]), "dp", 1)
     row = ((1, model_width), jnp.float32)
     mod_full, qkv_bias, expand_row, _, gain_a, gate_a, shift_m, gain_m, gate_m = kernel_call(
@@ -1170,9 +1163,8 @@
     )
     mark(FEED, own_partial)
     keep, send = halve(own_partial, swap(other_partial, "dp", 1))
-    mark(FEED_SEND, send)
     got = swap(send, "tensor", 1)
-    ff_first = first_step(hold(FF_BLOCKS, ff_blocks[2:]))
+    ff_first = first_step(ff_blocks[2:])
     seq_len = tokens_across.shape[0]
     act_later = hold(ACTIVATED, activated)
     other_out, own_out = (
@@ -1222,7 +1214,7 @@
     def ff_middle():
         *bases, going, going_second = middle_step(ff_blocks[:2], hold(FF_MIDDLE, ff_first))
         mark(FF_GOING, going)
-        return bases, second_step([going, going_second])
+        return bases, mark(FF_BACK_SECOND, second_step([going, going_second]))
 
     ff_bases, ff_second = ff_middle()
 
@@ -1243,7 +1235,7 @@
         head_count,
         score_scale,
     )
-    block_moved = swap(hold(BLOCK_MOVED, block_own[count:]), "tensor", 2)
+    block_moved = swap(block_own[count:], "tensor", 2)
     norm_crossed = mark(NORM_CROSSED, swap(norm_sums[1:], "dp", 1))
     ff_mine, ff_other = core_step(core, ff_bases, hold(FF_CORE, ff_second))
     mark(FF_CORE, ff_mine)
@@ -1275,7 +1267,7 @@
     mark(ATTN_BLOCKS, attn_blocks[2])
     attn_first = first_step(attn_blocks[2:])
     summed = lax.broadcasted_iota(jnp.int32, line.shape, 0) < 6
-    near = hold(LINE, swap(hold(LINE_NEAR, line), "tensor", 1))
+    near = hold(LINE, swap(line, "tensor", 1))
     line = line + jnp.where(summed, near, 0.0)
     far = mark(FAR, swap(hold(LINE_FAR, line), "tensor", 2))
     packed = kernel_call(
@@ -1303,9 +1295,8 @@
     )
     attn_second = second_step([attn_going, attn_going_second])
     packed = jnp.concatenate([packed, swap(packed, "dp", 1)])
-    packed = jnp.concatenate([packed, swap(hold(PACKED_X, packed), "dp", 2)])
+    packed = jnp.concatenate([packed, swap(packed, "dp", 2)])
     attn_mine, attn_other = core_step(core, attn_bases, attn_second)
-    mark(ATTN_CORE, attn_mine)
     packed = jnp.concatenate([packed, swap(hold(PACKED_Y, packed), "dp", 4)])
     modulation_weight_grad, grad_silu, modulation_bias_grad, rest = kernel_call(
         modulation_back_body,
@@ -1316,26 +1307,25 @@
             ((1, mod_width), jnp.float32),
             ((3, mod_width), jnp.float32),
         ],
-        [hold(MODULATION_BACK, packed), silu_act, modulation_weight],
+        [packed, silu_act, modulation_weight],
         [pltpu.VMEM((latent_total, mod_width), jnp.float32)],
         8,
         4 * latent_total * row_share * mod_width,
     )
     mark(MODULATION_BACK, grad_silu)
     attn_kept, attn_sent = half_step(is_own, attn_mine, hold(ATTN_HALF, swap(attn_other, "dp", 1)))
-    attn_moved = swap(attn_sent, "tensor", 2)
+    attn_moved = swap(hold(ATTN_SENT, attn_sent), "tensor", 2)
     near = grad_silu + swap(hold(GRAD_SILU, grad_silu), "tensor", 1)
     mark(NEAR, near)
     table_grad = kernel_call(
         table_body,
         "table",
         [((row_share, classes_total), jnp.float32)],
-        [labels_rel, cond, near, swap(near, "tensor", 2)],
+        [labels_rel, cond, near, hold(TABLE, swap(near, "tensor", 2))],
         [pltpu.VMEM((latent_total, classes_total), jnp.float32)],
         4,
         0,
     )[0]
-    mark(TABLE, table_grad)
     expand_grad, reduce_grad = owner_sum(
         ff_kept, hold(FF_OWNER, ff_moved), [ff_width, ff_width]
     )
@@ -1343,7 +1333,7 @@
         attend_owner_body,
         "owner_sum",
         [((3, row_share, head_width), jnp.float32), (output_weight.shape, jnp.float32)],
-        [attn_kept, hold(ATTN_OWNER, attn_moved)],
+        [attn_kept, attn_moved],
         [],
         8,
         0,

time: 166 us -> 161 us (0.970)
  starting transfers between devices: 65.9 us -> 44.8 us
  waiting for transfers between devices: 59.8 us -> 76.1 us
    ppermute x59, starting transfers between devices: 65.9 us -> 44.8 us  [swap(): lax.ppermute(values, axis, [(place, place ^ mask) for place in range(coun...]
    ppermute x59, waiting for transfers between devices: 59.8 us -> 76.1 us  [swap(): lax.ppermute(values, axis, [(place, place ^ mask) for place in range(coun...]
  transfers between devices with their start and end apart: 59 -> 59, of which waited for: 24 -> 29; matrix products, arithmetic and copies ran while one was open for 8% -> 8% of each run, Pallas kernels for 9% -> 9%
where the time goes in v4:
time: 161 us
  waiting for transfers between devices  76.1 us (47%)
  starting transfers between devices  44.8 us (28%)
  Pallas kernels  24.1 us (15%)
  other arithmetic  7.31 us (5%)
  local copies, waits for them, and re-layouts  5.41 us (3%)
  matrix products  2.1 us (1%)
    ppermute x59, waiting for transfers between devices, swap(): lax.ppermute(values, axis, [(place, place ^ mask) for place in range(coun...  76.1 us
    ppermute x59, starting transfers between devices, swap(): lax.ppermute(values, axis, [(place, place ^ mask) for place in range(coun...  44.8 us
    pallas_call x28, Pallas kernels, kernel_call(): pl.pallas_call(body, out_shape=shapes, in_specs=specs, out_specs=[pl.Bloc...  24.1 us
  transfers between devices with their start and end apart: 59, of which 29 were waited for; matrix products, arithmetic and copies ran while one was open for 8% of the time, Pallas kernels for 9%

profile of v4, /device:TPU:0, one launch (start us, length us, event | category | flops | bytes accessed | tf_op | source)
XLA Modules:
  0.0 161.1 jit_solution(14900307552507084715)
XLA Ops:
  2.6 4.1 %collective-permute-start.3 = (bf16[96,768]{1,0:T(8,128)(2,1)S(1)}, bf16[96,768]{1,0:T(8,128)(2,1)S(1)}, u32[]{:S(2)}, u32[]{:S(2)}) collective-permute-start(bf16[96,768]{1,0:T(8,128)(2,1)S(1)} %join_weights.1), channel_id=1, source_target_pairs={{0,2},{1,3},{2,0},{3,1},{4,6},{5,7},{6,4},{7,5},{8,10},{9,11},{10,... | collective-permute-start | bytes 442376 | tf_op jit(solution)/shard_map/ppermute | solution.py:324
  8.4 1.1 fusion.12
  9.5 1.6 collective-permute-start.5
  12.4 1.3 collective-permute-done.3
  13.9 1.6 collective-permute-start.6
  15.5 1.3 collective-permute-start.12
  16.8 1.5 collective-permute-start.13
  19.1 2.4 %collective-permute-done.12.refs_6_ = bf16[96,768]{1,0:T(8,128)(2,1)S(1)} collective-permute-done((bf16[96,768]{1,0:T(8,128)(2,1)S(1)}, bf16[96,768]{1,0:T(8,128)(2,1)S(1)}, u32[]{:S(2)}, u32[]{:S(2)}) %collective-permute-start.12) | collective-permute-done | bytes 147488 | tf_op jit(solution)/shard_map/ppermute | solution.py:324
  23.3 1.2 collective-permute-done.8.crossed
  24.6 2.8 %collective-permute-start.9 = (f32[8,1152]{1,0:T(8,128)S(1)}, f32[8,1152]{1,0:T(8,128)S(1)}, u32[]{:S(2)}, u32[]{:S(2)}) collective-permute-start(f32[8,1152]{1,0:T(8,128)S(1)} %mod_sum.1.own), channel_id=1, source_target_pairs={{0,1},{1,0},{2,3},{3,2},{4,5},{5,4},{6,7},{7,6},{8,9},{9,8},{10,11... | collective-permute-start | bytes 110600 | tf_op jit(solution)/shard_map/ppermute | solution.py:324
  27.5 1.6 collective-permute-start.14
  29.9 4.4 %collective-permute-done.4 = bf16[96,1536]{1,0:T(8,128)(2,1)} collective-permute-done((bf16[96,1536]{1,0:T(8,128)(2,1)S(1)}, bf16[96,1536]{1,0:T(8,128)(2,1)}, u32[]{:S(2)}, u32[]{:S(2)}) %collective-permute-start.4) | collective-permute-done | bytes 294944 | tf_op jit(solution)/shard_map/ppermute | solution.py:324
  34.4 1.7 %broadcast_select_fusion = bf16[96,1536]{1,0:T(8,128)(2,1)} fusion(bf16[96,1536]{1,0:T(8,128)(2,1)} %collective-permute-done.4, bf16[96,1536]{1,0:T(8,128)(2,1)S(1)} %constant_dynamic-update-slice_fusion, pred[]{:T(512)S(6)} %eq.21), kind=kLoop, calls=%fused_computation.14 | loop fusion | flops 147456 | bytes 884737 | tf_op jit(solution)/shard_map/jit(_where)/select_n | solution.py:431
  38.2 3.9 %collective-permute-done.11.far = f32[16,1152]{1,0:T(8,128)S(1)} collective-permute-done((f32[16,1152]{1,0:T(8,128)S(1)}, f32[16,1152]{1,0:T(8,128)S(1)}, u32[]{:S(2)}, u32[]{:S(2)}) %collective-permute-start.11) | collective-permute-done | bytes 73760 | tf_op jit(solution)/shard_map/ppermute | solution.py:324
  42.1 1.1 mod_place.1
  43.3 1.1 broadcast_select_fusion.2
  44.5 4.0 %attend_forward.1 = (bf16[512,768]{1,0:T(8,128)(2,1)S(1)}, f32[512,768]{1,0:T(8,128)S(1)}, bf16[512,576]{1,0:T(8,128)(2,1)S(1)}, bf16[512,192]{1,0:T(8,128)(2,1)...) custom-call(s32[1]{0:T(128)} %bitcast.1.chip_ref, ...), custom_call_target="tpu_custom_call" | custom-call | flops 704643072 | bytes 7903492 | tf_op jit(solution)/shard_map/attend_forward/pallas_call | solution.py:530
  48.6 1.5 collective-permute-start.24
  51.2 7.3 %collective-permute-done.18 = bf16[64,768]{1,0:T(8,128)(2,1)S(1)} collective-permute-done((bf16[64,768]{1,0:T(8,128)(2,1)S(1)}, bf16[64,768]{1,0:T(8,128)(2,1)S(1)}, u32[]{:S(2)}, u32[]{:S(2)}) %collective-permute-start.18) | collective-permute-done | bytes 98336 | tf_op jit(solution)/shard_map/ppermute | solution.py:324
  58.8 2.1 %collective-permute-start.17 = (bf16[128,768]{1,0:T(8,128)(2,1)S(1)}, bf16[128,768]{1,0:T(8,128)(2,1)S(1)}, u32[]{:S(2)}, u32[]{:S(2)}) collective-permute-start(bf16[128,768]{1,0:T(8,128)(2,1)S(1)} %get-tuple-element.135), channel_id=1, source_target_pairs={{0,1},{1,0},{2,3},{3,2},{4,5},{5,4},{6,7},{7,6},{8,9},{9,8},{10,11... | collective-permute-start | bytes 589832 | tf_op jit(solution)/shard_map/ppermute | solution.py:324
  61.5 1.1 collective-permute-start.26
  62.7 3.7 %collective-permute-done.22.refs_5_ = bf16[128,768]{1,0:T(8,128)(2,1)S(1)} collective-permute-done((bf16[128,768]{1,0:T(8,128)(2,1)S(1)}, bf16[128,768]{1,0:T(8,128)(2,1)S(1)}, u32[]{:S(2)}, u32[]{:S(2)}) %collective-permute-start.22) | collective-permute-done | bytes 196640 | tf_op jit(solution)/shard_map/ppermute | solution.py:324
  66.5 3.2 %collective-permute-done.17.got = bf16[128,768]{1,0:T(8,128)(2,1)S(1)} collective-permute-done((bf16[128,768]{1,0:T(8,128)(2,1)S(1)}, bf16[128,768]{1,0:T(8,128)(2,1)S(1)}, u32[]{:S(2)}, u32[]{:S(2)}) %collective-permute-start.17) | collective-permute-done | bytes 196640 | tf_op jit(solution)/shard_map/ppermute | solution.py:324
  70.3 5.7 %collective-permute-done.19.refs_1_ = bf16[128,768]{1,0:T(8,128)(2,1)S(1)} collective-permute-done((bf16[128,768]{1,0:T(8,128)(2,1)S(1)}, bf16[128,768]{1,0:T(8,128)(2,1)S(1)}, u32[]{:S(2)}, u32[]{:S(2)}) %collective-permute-start.19) | collective-permute-done | bytes 196640 | tf_op jit(solution)/shard_map/ppermute | solution.py:324
  76.0 1.4 collective-permute-done.21.refs_3_
  77.4 4.1 %feed_forward.1 = (bf16[512,768]{1,0:T(8,128)(2,1)S(1)}, f32[1,768]{1,0:T(1,128)S(1)}, bf16[768,768]{1,0:T(8,128)(2,1)S(1)}, f32[256,768]{1,0:T(8,128)S(1)}, f32...) custom-call(s32[1]{0:T(128)} %bitcast.1.chip_ref, ...), custom_call_target="tpu_custom_call" | custom-call | flops 3019898880 | bytes 11053060 | tf_op jit(solution)/shard_map/feed_forward/pallas_call | solution.py:530
  85.7 1.5 collective-permute-start.29
  87.2 5.1 %collective-permute-done.32.got = bf16[128,768]{1,0:T(8,128)(2,1)S(1)} collective-permute-done((bf16[128,768]{1,0:T(8,128)(2,1)S(1)}, bf16[128,768]{1,0:T(8,128)(2,1)S(1)}, u32[]{:S(2)}, u32[]{:S(2)}) %collective-permute-start.32) | collective-permute-done | bytes 196640 | tf_op jit(solution)/shard_map/ppermute | solution.py:324
  93.6 2.9 %collective-permute-done.29.got = bf16[128,768]{1,0:T(8,128)(2,1)S(1)} collective-permute-done((bf16[128,768]{1,0:T(8,128)(2,1)S(1)}, bf16[128,768]{1,0:T(8,128)(2,1)S(1)}, u32[]{:S(2)}, u32[]{:S(2)}) %collective-permute-start.29) | collective-permute-done | bytes 196640 | tf_op jit(solution)/shard_map/ppermute | solution.py:324
  96.6 1.5 collective-permute-done.36.got_first
  98.3 1.1 collective-permute-done.33.refs_1_
  100.5 1.5 collective-permute-start.42
  103.7 4.2 %attend_back.1 = (bf16[512,768]{1,0:T(8,128)(2,1)S(1)}, bf16[512,576]{1,0:T(8,128)(2,1)S(1)}, f32[1,576]{1,0:T(1,128)S(1)}, f32[2,1536]{1,0:T(2,128)S(1)}, f32[2...) custom-call(bf16[128,768]{1,0:T(8,128)(2,1)S(1)} %get-tuple-element.167.refs_0_, ...), custom_call_target="tpu_custom_call" | custom-call | flops 855638016 | bytes 7289088 | tf_op jit(solution)/shard_map/attend_back/pallas_call | solution.py:530
  110.7 1.2 grad_blocks.1
  112.0 2.0 %collective-permute-done.43 = f32[8,1152]{1,0:T(8,128)S(1)} collective-permute-done((f32[8,1152]{1,0:T(8,128)S(1)}, f32[8,1152]{1,0:T(8,128)S(1)}, u32[]{:S(2)}, u32[]{:S(2)}) %collective-permute-start.43) | collective-permute-done | bytes 36896 | tf_op jit(solution)/shard_map/ppermute | solution.py:324
  114.1 5.2 %collective-permute-done.45.far = f32[8,1152]{1,0:T(8,128)S(1)} collective-permute-done((f32[8,1152]{1,0:T(8,128)S(1)}, f32[8,1152]{1,0:T(8,128)S(1)}, u32[]{:S(2)}, u32[]{:S(2)}) %collective-permute-start.45) | collective-permute-done | bytes 36896 | tf_op jit(solution)/shard_map/ppermute | solution.py:324
  120.6 1.2 collective-permute-start.54
  123.5 6.4 %collective-permute-done.53.got_first = bf16[192,768]{1,0:T(8,128)(2,1)S(1)} collective-permute-done((bf16[192,768]{1,0:T(8,128)(2,1)S(1)}, bf16[192,768]{1,0:T(8,128)(2,1)S(1)}, u32[]{:S(2)}, u32[]{:S(2)}) %collective-permute-start.53) | collective-permute-done | bytes 294944 | tf_op jit(solution)/shard_map/ppermute | solution.py:324
  130.0 1.1 collective-permute-start.55
  132.4 5.9 %collective-permute-done.49.moved = bf16[96,1536]{1,0:T(8,128)(2,1)S(1)} collective-permute-done((bf16[96,1536]{1,0:T(8,128)(2,1)S(1)}, bf16[96,1536]{1,0:T(8,128)(2,1)S(1)}, u32[]{:S(2)}, u32[]{:S(2)}) %collective-permute-start.49) | collective-permute-done | bytes 294944 | tf_op jit(solution)/shard_map/ppermute | solution.py:324
  138.3 1.5 collective-permute-start.50
  140.6 1.8 %collective-permute-done.39.got = bf16[128,768]{1,0:T(8,128)(2,1)S(1)} collective-permute-done((bf16[128,768]{1,0:T(8,128)(2,1)S(1)}, bf16[128,768]{1,0:T(8,128)(2,1)S(1)}, u32[]{:S(2)}, u32[]{:S(2)}) %collective-permute-start.39) | collective-permute-done | bytes 196640 | tf_op jit(solution)/shard_map/ppermute | solution.py:324
  142.7 1.2 collective-permute-start.46
  145.0 1.3 collective-permute-start.51
  147.1 1.2 collective-permute-start.58
  149.5 1.2 collective-permute-start.52
  151.3 3.8 %collective-permute-done.46.moved = bf16[64,768]{1,0:T(8,128)(2,1)S(1)} collective-permute-done((bf16[64,768]{1,0:T(8,128)(2,1)S(1)}, bf16[64,768]{1,0:T(8,128)(2,1)S(1)}, u32[]{:S(2)}, u32[]{:S(2)}) %collective-permute-start.46) | collective-permute-done | bytes 98336 | tf_op jit(solution)/shard_map/ppermute | solution.py:324
  158.4 1.8 %table.1 = f32[96,1000]{1,0:T(8,128)} custom-call(s32[16]{0:T(128)S(1)} %get-tuple-element.241.labels, f32[16,96]{1,0:T(8,128)S(1)} %get-tuple-element.243.cond, f32[16,96]{1,0:T(8,128)S(1)} %add.85.near, f32[16,96]{1,0:T(8,128)S(1)} %collective-permute-done.52.far), custom_call_target="tpu_custom_call" | custom-call | bytes 402496 | tf_op jit(solution)/shard_map/table/pallas_call | solution.py:530
  (181 shorter events, 38.2 us)
Async XLA Ops:
  2.6 11.1 %collective-permute-start.3 = (bf16[96,768]{1,0:T(8,128)(2,1)S(1)}, bf16[96,768]{1,0:T(8,128)(2,1)S(1)}, u32[]{:S(2)}, u32[]{:S(2)}) collective-permute-start(bf16[96,768]{1,0:T(8,128)(2,1)S(1)} %join_weights.1), channel_id=1, source_target_pairs={{0,2},{1,3},{2,0},{3,1},{4,6},{5,7},{6,4},{7,5},{8,10},{9,11},{10,... | collective-permute-start | bytes 442376 | tf_op jit(solution)/shard_map/ppermute | solution.py:324
  9.5 4.4 %collective-permute-start.5 = (f32[8,1152]{1,0:T(8,128)S(1)}, f32[8,1152]{1,0:T(8,128)S(1)}, u32[]{:S(2)}, u32[]{:S(2)}) collective-permute-start(f32[8,1152]{1,0:T(8,128)S(1)} %slice.55), channel_id=1, source_target_pairs={{0,16},{4,20},{8,24},{12,28},{16,0},{20,4},{24,8},{28,12},{1,17},{... | collective-permute-start | bytes 110600 | tf_op jit(solution)/shard_map/ppermute | solution.py:324
  11.9 7.0 %collective-permute-start = (bf16[64,768]{1,0:T(8,128)(2,1)S(1)}, bf16[64,768]{1,0:T(8,128)(2,1)S(1)}, u32[]{:S(2)}, u32[]{:S(2)}) collective-permute-start(bf16[64,768]{1,0:T(8,128)(2,1)S(1)} %dynamic-slice_bitcast_fusion.2), channel_id=1, source_target_pairs={{0,2},{1,3},{2,0},{3,1},{4,6},{5,7},{6,4},{7,5},{8,10},{9,11},{10,... | collective-permute-start | bytes 294920 | tf_op jit(solution)/shard_map/ppermute | solution.py:324
  13.9 4.4 %collective-permute-start.6 = (f32[4,1152]{1,0:T(4,128)S(1)}, f32[4,1152]{1,0:T(4,128)S(1)}, u32[]{:S(2)}, u32[]{:S(2)}) collective-permute-start(f32[4,1152]{1,0:T(4,128)S(1)} %slice.57), channel_id=1, source_target_pairs={{0,8},{4,12},{8,0},{12,4},{16,24},{20,28},{24,16},{28,20},{1,9},{5... | collective-permute-start | bytes 55304 | tf_op jit(solution)/shard_map/ppermute | solution.py:324
  15.5 6.0 %collective-permute-start.12 = (bf16[96,768]{1,0:T(8,128)(2,1)S(1)}, bf16[96,768]{1,0:T(8,128)(2,1)S(1)}, u32[]{:S(2)}, u32[]{:S(2)}) collective-permute-start(bf16[96,768]{1,0:T(8,128)(2,1)S(1)} %get-tuple-element.247), channel_id=1, source_target_pairs={{0,8},{4,12},{8,0},{12,4},{16,24},{20,28},{24,16},{28,20},{1,9},{5... | collective-permute-start | bytes 442376 | tf_op jit(solution)/shard_map/ppermute | solution.py:324
  16.8 5.6 %collective-permute-start.13 = (bf16[96,768]{1,0:T(8,128)(2,1)S(1)}, bf16[96,768]{1,0:T(8,128)(2,1)S(1)}, u32[]{:S(2)}, u32[]{:S(2)}) collective-permute-start(bf16[96,768]{1,0:T(8,128)(2,1)S(1)} %get-tuple-element.246), channel_id=1, source_target_pairs={{0,16},{4,20},{8,24},{12,28},{16,0},{20,4},{24,8},{28,12},{1,17},{... | collective-permute-start | bytes 442376 | tf_op jit(solution)/shard_map/ppermute | solution.py:324
  18.9 15.4 %collective-permute-start.4 = (bf16[96,1536]{1,0:T(8,128)(2,1)S(1)}, bf16[96,1536]{1,0:T(8,128)(2,1)}, u32[]{:S(2)}, u32[]{:S(2)}) collective-permute-start(bf16[96,1536]{1,0:T(8,128)(2,1)S(1)} %constant_dynamic-update-slice_fusion), channel_id=1, source_target_pairs={{0,2},{1,3},{2,0},{3,1},{4,6},{5,7},{6,4},{7,5},{8,10},{9,11},{10,... | collective-permute-start | bytes 884744 | tf_op jit(solution)/shard_map/ppermute | solution.py:324
  24.6 5.4 %collective-permute-start.9 = (f32[8,1152]{1,0:T(8,128)S(1)}, f32[8,1152]{1,0:T(8,128)S(1)}, u32[]{:S(2)}, u32[]{:S(2)}) collective-permute-start(f32[8,1152]{1,0:T(8,128)S(1)} %mod_sum.1.own), channel_id=1, source_target_pairs={{0,1},{1,0},{2,3},{3,2},{4,5},{5,4},{6,7},{7,6},{8,9},{9,8},{10,11... | collective-permute-start | bytes 110600 | tf_op jit(solution)/shard_map/ppermute | solution.py:324
  27.4 9.9 %collective-permute-start.1 = (bf16[128,768]{1,0:T(8,128)(2,1)S(1)}, bf16[128,768]{1,0:T(8,128)(2,1)S(1)}, u32[]{:S(2)}, u32[]{:S(2)}) collective-permute-start(bf16[128,768]{1,0:T(8,128)(2,1)S(1)} %pad_maximum_fusion.9.refs_0_.tokens), channel_id=1, source_target_pairs={{0,1},{1,0},{2,3},{3,2},{4,5},{5,4},{6,7},{7,6},{8,9},{9,8},{10,11... | collective-permute-start | bytes 589832 | tf_op jit(solution)/shard_map/ppermute | solution.py:324
  27.5 14.7 %collective-permute-start.14 = (bf16[192,768]{1,0:T(8,128)(2,1)}, bf16[192,768]{1,0:T(8,128)(2,1)S(1)}, u32[]{:S(2)}, u32[]{:S(2)}) collective-permute-start(bf16[192,768]{1,0:T(8,128)(2,1)} %get-tuple-element.252), channel_id=1, source_target_pairs={{0,16},{4,20},{8,24},{12,28},{16,0},{20,4},{24,8},{28,12},{1,17},{... | collective-permute-start | bytes 884744 | tf_op jit(solution)/shard_map/ppermute | solution.py:324
  29.0 13.1 %collective-permute-start.15 = (bf16[192,768]{1,0:T(8,128)(2,1)}, bf16[192,768]{1,0:T(8,128)(2,1)}, u32[]{:S(2)}, u32[]{:S(2)}) collective-permute-start(bf16[192,768]{1,0:T(8,128)(2,1)} %get-tuple-element.250), channel_id=1, source_target_pairs={{0,8},{4,12},{8,0},{12,4},{16,24},{20,28},{24,16},{28,20},{1,9},{5... | collective-permute-start | bytes 884744 | tf_op jit(solution)/shard_map/ppermute | solution.py:324
  36.1 7.2 %collective-permute-start.10 = (bf16[96,1536]{1,0:T(8,128)(2,1)}, bf16[96,1536]{1,0:T(8,128)(2,1)}, u32[]{:S(2)}, u32[]{:S(2)}) collective-permute-start(bf16[96,1536]{1,0:T(8,128)(2,1)} %broadcast_select_fusion), channel_id=1, source_target_pairs={{0,4},{4,0},{8,12},{12,8},{16,20},{20,16},{24,28},{28,24},{1,5},{5... | collective-permute-start | bytes 884744 | tf_op jit(solution)/shard_map/ppermute | solution.py:324
  36.2 6.0 %collective-permute-start.11 = (f32[16,1152]{1,0:T(8,128)S(1)}, f32[16,1152]{1,0:T(8,128)S(1)}, u32[]{:S(2)}, u32[]{:S(2)}) collective-permute-start(f32[16,1152]{1,0:T(8,128)S(1)} %pad_maximum_fusion.12), channel_id=1, source_target_pairs={{0,2},{1,3},{2,0},{3,1},{4,6},{5,7},{6,4},{7,5},{8,10},{9,11},{10,... | collective-permute-start | bytes 221192 | tf_op jit(solution)/shard_map/ppermute | solution.py:324
  38.2 6.3 %collective-permute-start.2 = (bf16[256,768]{1,0:T(8,128)(2,1)S(1)}, bf16[256,768]{1,0:T(8,128)(2,1)S(1)}, u32[]{:S(2)}, u32[]{:S(2)}) collective-permute-start(bf16[256,768]{1,0:T(8,128)(2,1)S(1)} %pad_maximum_fusion.3), channel_id=1, source_target_pairs={{0,4},{4,0},{8,12},{12,8},{16,20},{20,16},{24,28},{28,24},{1,5},{5... | collective-permute-start | bytes 1179656 | tf_op jit(solution)/shard_map/ppermute | solution.py:324
  48.5 10.2 %collective-permute-start.16 = (f32[256,768]{1,0:T(8,128)S(1)}, f32[256,768]{1,0:T(8,128)S(1)}, u32[]{:S(2)}, u32[]{:S(2)}) collective-permute-start(f32[256,768]{1,0:T(8,128)S(1)} %get-tuple-element.133), channel_id=1, source_target_pairs={{0,4},{4,0},{8,12},{12,8},{16,20},{20,16},{24,28},{28,24},{1,5},{5... | collective-permute-start | bytes 2359304 | tf_op jit(solution)/shard_map/ppermute | solution.py:324
  48.6 12.3 %collective-permute-start.24 = (bf16[96,1536]{1,0:T(8,128)(2,1)S(1)}, bf16[96,1536]{1,0:T(8,128)(2,1)S(1)}, u32[]{:S(2)}, u32[]{:S(2)}) collective-permute-start(bf16[96,1536]{1,0:T(8,128)(2,1)S(1)} %get-tuple-element.245), channel_id=1, source_target_pairs={{0,8},{4,12},{8,0},{12,4},{16,24},{20,28},{24,16},{28,20},{1,9},{5... | collective-permute-start | bytes 884744 | tf_op jit(solution)/shard_map/ppermute | solution.py:324
  50.1 10.7 %collective-permute-start.25 = (bf16[96,1536]{1,0:T(8,128)(2,1)S(1)}, bf16[96,1536]{1,0:T(8,128)(2,1)S(1)}, u32[]{:S(2)}, u32[]{:S(2)}) collective-permute-start(bf16[96,1536]{1,0:T(8,128)(2,1)S(1)} %get-tuple-element.244), channel_id=1, source_target_pairs={{0,16},{4,20},{8,24},{12,28},{16,0},{20,4},{24,8},{28,12},{1,17},{... | collective-permute-start | bytes 884744 | tf_op jit(solution)/shard_map/ppermute | solution.py:324
  51.0 7.5 %collective-permute-start.18 = (bf16[64,768]{1,0:T(8,128)(2,1)S(1)}, bf16[64,768]{1,0:T(8,128)(2,1)S(1)}, u32[]{:S(2)}, u32[]{:S(2)}) collective-permute-start(bf16[64,768]{1,0:T(8,128)(2,1)S(1)} %get-tuple-element.136), channel_id=1, source_target_pairs={{0,2},{1,3},{2,0},{3,1},{4,6},{5,7},{6,4},{7,5},{8,10},{9,11},{10,... | collective-permute-start | bytes 294920 | tf_op jit(solution)/shard_map/ppermute | solution.py:324
  58.6 7.8 %collective-permute-start.22 = (bf16[128,768]{1,0:T(8,128)(2,1)S(1)}, bf16[128,768]{1,0:T(8,128)(2,1)S(1)}, u32[]{:S(2)}, u32[]{:S(2)}) collective-permute-start(bf16[128,768]{1,0:T(8,128)(2,1)S(1)} %pad_maximum_fusion.10.refs_4_.upstream), channel_id=1, source_target_pairs={{0,1},{1,0},{2,3},{3,2},{4,5},{5,4},{6,7},{7,6},{8,9},{9,8},{10,11... | collective-permute-start | bytes 589832 | tf_op jit(solution)/shard_map/ppermute | solution.py:324
  58.8 10.9 %collective-permute-start.17 = (bf16[128,768]{1,0:T(8,128)(2,1)S(1)}, bf16[128,768]{1,0:T(8,128)(2,1)S(1)}, u32[]{:S(2)}, u32[]{:S(2)}) collective-permute-start(bf16[128,768]{1,0:T(8,128)(2,1)S(1)} %get-tuple-element.135), channel_id=1, source_target_pairs={{0,1},{1,0},{2,3},{3,2},{4,5},{5,4},{6,7},{7,6},{8,9},{9,8},{10,11... | collective-permute-start | bytes 589832 | tf_op jit(solution)/shard_map/ppermute | solution.py:324
  60.9 15.1 %collective-permute-start.27 = (bf16[192,1536]{1,0:T(8,128)(2,1)S(1)}, bf16[192,1536]{1,0:T(8,128)(2,1)S(1)}, u32[]{:S(2)}, u32[]{:S(2)}) collective-permute-start(bf16[192,1536]{1,0:T(8,128)(2,1)S(1)} %pad_maximum_fusion.2), channel_id=1, source_target_pairs={{0,8},{4,12},{8,0},{12,4},{16,24},{20,28},{24,16},{28,20},{1,9},{5... | collective-permute-start | bytes 1769480 | tf_op jit(solution)/shard_map/ppermute | solution.py:324
  61.5 14.5 %collective-permute-start.26 = (bf16[192,1536]{1,0:T(8,128)(2,1)S(1)}, bf16[192,1536]{1,0:T(8,128)(2,1)S(1)}, u32[]{:S(2)}, u32[]{:S(2)}) collective-permute-start(bf16[192,1536]{1,0:T(8,128)(2,1)S(1)} %pad_maximum_fusion), channel_id=1, source_target_pairs={{0,16},{4,20},{8,24},{12,28},{16,0},{20,4},{24,8},{28,12},{1,17},{... | collective-permute-start | bytes 1769480 | tf_op jit(solution)/shard_map/ppermute | solution.py:324
  66.4 9.6 %collective-permute-start.23 = (bf16[256,768]{1,0:T(8,128)(2,1)S(1)}, bf16[256,768]{1,0:T(8,128)(2,1)S(1)}, u32[]{:S(2)}, u32[]{:S(2)}) collective-permute-start(bf16[256,768]{1,0:T(8,128)(2,1)S(1)} %pad_maximum_fusion.4), channel_id=1, source_target_pairs={{0,4},{4,0},{8,12},{12,8},{16,20},{20,16},{24,28},{28,24},{1,5},{5... | collective-permute-start | bytes 1179656 | tf_op jit(solution)/shard_map/ppermute | solution.py:324
  69.9 6.0 %collective-permute-start.19 = (bf16[128,768]{1,0:T(8,128)(2,1)S(1)}, bf16[128,768]{1,0:T(8,128)(2,1)S(1)}, u32[]{:S(2)}, u32[]{:S(2)}) collective-permute-start(bf16[128,768]{1,0:T(8,128)(2,1)S(1)} %get-tuple-element.141.refs_0_), channel_id=1, source_target_pairs={{0,1},{1,0},{2,3},{3,2},{4,5},{5,4},{6,7},{7,6},{8,9},{9,8},{10,11... | collective-permute-start | bytes 589832 | tf_op jit(solution)/shard_map/ppermute | solution.py:324
  70.3 5.7 %collective-permute-start.20 = (bf16[128,768]{1,0:T(8,128)(2,1)S(1)}, bf16[128,768]{1,0:T(8,128)(2,1)S(1)}, u32[]{:S(2)}, u32[]{:S(2)}) collective-permute-start(bf16[128,768]{1,0:T(8,128)(2,1)S(1)} %get-tuple-element.141.refs_0_), channel_id=1, source_target_pairs={{0,4},{4,0},{8,12},{12,8},{16,20},{20,16},{24,28},{28,24},{1,5},{5... | collective-permute-start | bytes 589832 | tf_op jit(solution)/shard_map/ppermute | solution.py:324
  82.7 15.4 %collective-permute-start.36 = (bf16[192,1536]{1,0:T(8,128)(2,1)S(1)}, bf16[192,1536]{1,0:T(8,128)(2,1)S(1)}, u32[]{:S(2)}, u32[]{:S(2)}) collective-permute-start(bf16[192,1536]{1,0:T(8,128)(2,1)S(1)} %get-tuple-element.162), channel_id=1, source_target_pairs={{0,8},{4,12},{8,0},{12,4},{16,24},{20,28},{24,16},{28,20},{1,9},{5... | collective-permute-start | bytes 1769480 | tf_op jit(solution)/shard_map/ppermute | solution.py:324
  83.3 15.1 %collective-permute-start.37 = (bf16[192,1536]{1,0:T(8,128)(2,1)S(1)}, bf16[192,1536]{1,0:T(8,128)(2,1)S(1)}, u32[]{:S(2)}, u32[]{:S(2)}) collective-permute-start(bf16[192,1536]{1,0:T(8,128)(2,1)S(1)} %get-tuple-element.163), channel_id=1, source_target_pairs={{0,16},{4,20},{8,24},{12,28},{16,0},{20,4},{24,8},{28,12},{1,17},{... | collective-permute-start | bytes 1769480 | tf_op jit(solution)/shard_map/ppermute | solution.py:324
  84.4 7.9 %collective-permute-start.32 = (bf16[128,768]{1,0:T(8,128)(2,1)S(1)}, bf16[128,768]{1,0:T(8,128)(2,1)S(1)}, u32[]{:S(2)}, u32[]{:S(2)}) collective-permute-start(bf16[128,768]{1,0:T(8,128)(2,1)S(1)} %get-tuple-element.156), channel_id=1, source_target_pairs={{0,1},{1,0},{2,3},{3,2},{4,5},{5,4},{6,7},{7,6},{8,9},{9,8},{10,11... | collective-permute-start | bytes 589832 | tf_op jit(solution)/shard_map/ppermute | solution.py:324
  85.7 10.8 %collective-permute-start.29 = (bf16[128,768]{1,0:T(8,128)(2,1)S(1)}, bf16[128,768]{1,0:T(8,128)(2,1)S(1)}, u32[]{:S(2)}, u32[]{:S(2)}) collective-permute-start(bf16[128,768]{1,0:T(8,128)(2,1)S(1)} %get-tuple-element.150), channel_id=1, source_target_pairs={{0,1},{1,0},{2,3},{3,2},{4,5},{5,4},{6,7},{7,6},{8,9},{9,8},{10,11... | collective-permute-start | bytes 589832 | tf_op jit(solution)/shard_map/ppermute | solution.py:324
  92.9 6.5 %collective-permute-start.33 = (bf16[128,768]{1,0:T(8,128)(2,1)S(1)}, bf16[128,768]{1,0:T(8,128)(2,1)S(1)}, u32[]{:S(2)}, u32[]{:S(2)}) collective-permute-start(bf16[128,768]{1,0:T(8,128)(2,1)S(1)} %get-tuple-element.167.refs_0_), channel_id=1, source_target_pairs={{0,1},{1,0},{2,3},{3,2},{4,5},{5,4},{6,7},{7,6},{8,9},{9,8},{10,11... | collective-permute-start | bytes 589832 | tf_op jit(solution)/shard_map/ppermute | solution.py:324
  99.6 9.6 %collective-permute-start.41 = (bf16[96,1536]{1,0:T(8,128)(2,1)S(1)}, bf16[96,1536]{1,0:T(8,128)(2,1)S(1)}, u32[]{:S(2)}, u32[]{:S(2)}) collective-permute-start(bf16[96,1536]{1,0:T(8,128)(2,1)S(1)} %get-tuple-element.166), channel_id=1, source_target_pairs={{0,16},{4,20},{8,24},{12,28},{16,0},{20,4},{24,8},{28,12},{1,17},{... | collective-permute-start | bytes 884744 | tf_op jit(solution)/shard_map/ppermute | solution.py:324
  100.5 8.7 %collective-permute-start.42 = (bf16[96,1536]{1,0:T(8,128)(2,1)S(1)}, bf16[96,1536]{1,0:T(8,128)(2,1)S(1)}, u32[]{:S(2)}, u32[]{:S(2)}) collective-permute-start(bf16[96,1536]{1,0:T(8,128)(2,1)S(1)} %get-tuple-element.185), channel_id=1, source_target_pairs={{0,8},{4,12},{8,0},{12,4},{16,24},{20,28},{24,16},{28,20},{1,9},{5... | collective-permute-start | bytes 884744 | tf_op jit(solution)/shard_map/ppermute | solution.py:324
  109.7 22.1 %collective-permute-start.38 = (f32[256,768]{1,0:T(8,128)S(1)}, f32[256,768]{1,0:T(8,128)S(1)}, u32[]{:S(2)}, u32[]{:S(2)}) collective-permute-start(f32[256,768]{1,0:T(8,128)S(1)} %get-tuple-element.177), channel_id=1, source_target_pairs={{0,4},{4,0},{8,12},{12,8},{16,20},{20,16},{24,28},{28,24},{1,5},{5... | collective-permute-start | bytes 2359304 | tf_op jit(solution)/shard_map/ppermute | solution.py:324
  114.1 5.3 %collective-permute-start.45 = (f32[8,1152]{1,0:T(8,128)S(1)}, f32[8,1152]{1,0:T(8,128)S(1)}, u32[]{:S(2)}, u32[]{:S(2)}) collective-permute-start(f32[8,1152]{1,0:T(8,128)S(1)} %select_add_fusion.line), channel_id=1, source_target_pairs={{0,2},{1,3},{2,0},{3,1},{4,6},{5,7},{6,4},{7,5},{8,10},{9,11},{10,... | collective-permute-start | bytes 110600 | tf_op jit(solution)/shard_map/ppermute | solution.py:324
  120.0 9.9 %collective-permute-start.53 = (bf16[192,768]{1,0:T(8,128)(2,1)S(1)}, bf16[192,768]{1,0:T(8,128)(2,1)S(1)}, u32[]{:S(2)}, u32[]{:S(2)}) collective-permute-start(bf16[192,768]{1,0:T(8,128)(2,1)S(1)} %get-tuple-element.203), channel_id=1, source_target_pairs={{0,8},{4,12},{8,0},{12,4},{16,24},{20,28},{24,16},{28,20},{1,9},{5... | collective-permute-start | bytes 884744 | tf_op jit(solution)/shard_map/ppermute | solution.py:324
  120.6 9.3 %collective-permute-start.54 = (bf16[192,768]{1,0:T(8,128)(2,1)S(1)}, bf16[192,768]{1,0:T(8,128)(2,1)S(1)}, u32[]{:S(2)}, u32[]{:S(2)}) collective-permute-start(bf16[192,768]{1,0:T(8,128)(2,1)S(1)} %get-tuple-element.217), channel_id=1, source_target_pairs={{0,16},{4,20},{8,24},{12,28},{16,0},{20,4},{24,8},{28,12},{1,17},{... | collective-permute-start | bytes 884744 | tf_op jit(solution)/shard_map/ppermute | solution.py:324
  121.8 10.5 %collective-permute-start.48 = (f32[16,1152]{1,0:T(8,128)S(1)}, f32[16,1152]{1,0:T(8,128)S(1)}, u32[]{:S(2)}, u32[]{:S(2)}) collective-permute-start(f32[16,1152]{1,0:T(8,128)S(1)} %pad_maximum_fusion.13), channel_id=1, source_target_pairs={{0,8},{4,12},{8,0},{12,4},{16,24},{20,28},{24,16},{28,20},{1,9},{5... | collective-permute-start | bytes 221192 | tf_op jit(solution)/shard_map/ppermute | solution.py:324
  122.7 15.6 %collective-permute-start.49 = (bf16[96,1536]{1,0:T(8,128)(2,1)S(1)}, bf16[96,1536]{1,0:T(8,128)(2,1)S(1)}, u32[]{:S(2)}, u32[]{:S(2)}) collective-permute-start(bf16[96,1536]{1,0:T(8,128)(2,1)S(1)} %get-tuple-element.197), channel_id=1, source_target_pairs={{0,2},{1,3},{2,0},{3,1},{4,6},{5,7},{6,4},{7,5},{8,10},{9,11},{10,... | collective-permute-start | bytes 884744 | tf_op jit(solution)/shard_map/ppermute | solution.py:324
  130.0 9.8 %collective-permute-start.55 = (bf16[96,768]{1,0:T(8,128)(2,1)S(1)}, bf16[96,768]{1,0:T(8,128)(2,1)S(1)}, u32[]{:S(2)}, u32[]{:S(2)}) collective-permute-start(bf16[96,768]{1,0:T(8,128)(2,1)S(1)} %get-tuple-element.220), channel_id=1, source_target_pairs={{0,16},{4,20},{8,24},{12,28},{16,0},{20,4},{24,8},{28,12},{1,17},{... | collective-permute-start | bytes 442376 | tf_op jit(solution)/shard_map/ppermute | solution.py:324
  131.1 8.7 %collective-permute-start.56 = (bf16[96,768]{1,0:T(8,128)(2,1)S(1)}, bf16[96,768]{1,0:T(8,128)(2,1)S(1)}, u32[]{:S(2)}, u32[]{:S(2)}) collective-permute-start(bf16[96,768]{1,0:T(8,128)(2,1)S(1)} %get-tuple-element.221), channel_id=1, source_target_pairs={{0,8},{4,12},{8,0},{12,4},{16,24},{20,28},{24,16},{28,20},{1,9},{5... | collective-permute-start | bytes 442376 | tf_op jit(solution)/shard_map/ppermute | solution.py:324
  132.0 10.4 %collective-permute-start.39 = (bf16[128,768]{1,0:T(8,128)(2,1)S(1)}, bf16[128,768]{1,0:T(8,128)(2,1)S(1)}, u32[]{:S(2)}, u32[]{:S(2)}) collective-permute-start(bf16[128,768]{1,0:T(8,128)(2,1)S(1)} %get-tuple-element.179), channel_id=1, source_target_pairs={{0,1},{1,0},{2,3},{3,2},{4,5},{5,4},{6,7},{7,6},{8,9},{9,8},{10,11... | collective-permute-start | bytes 589832 | tf_op jit(solution)/shard_map/ppermute | solution.py:324
  138.3 5.7 %collective-permute-start.50 = (f32[32,1152]{1,0:T(8,128)S(1)}, f32[32,1152]{1,0:T(8,128)S(1)}, u32[]{:S(2)}, u32[]{:S(2)}) collective-permute-start(f32[32,1152]{1,0:T(8,128)S(1)} %pad_maximum_fusion.11), channel_id=1, source_target_pairs={{0,16},{4,20},{8,24},{12,28},{16,0},{20,4},{24,8},{28,12},{1,17},{... | collective-permute-start | bytes 442376 | tf_op jit(solution)/shard_map/ppermute | solution.py:324
  139.9 6.5 %collective-permute-start.57 = (f32[96,768]{1,0:T(8,128)S(1)}, f32[96,768]{1,0:T(8,128)S(1)}, u32[]{:S(2)}, u32[]{:S(2)}) collective-permute-start(f32[96,768]{1,0:T(8,128)S(1)} %get-tuple-element.223), channel_id=1, source_target_pairs={{0,4},{4,0},{8,12},{12,8},{16,20},{20,16},{24,28},{28,24},{1,5},{5... | collective-permute-start | bytes 884744 | tf_op jit(solution)/shard_map/ppermute | solution.py:324
  140.6 15.8 %collective-permute-start.30 = (bf16[64,768]{1,0:T(8,128)(2,1)}, bf16[64,768]{1,0:T(8,128)(2,1)S(1)}, u32[]{:S(2)}, u32[]{:S(2)}) collective-permute-start(bf16[64,768]{1,0:T(8,128)(2,1)} %slice.45), channel_id=1, source_target_pairs={{0,2},{1,3},{2,0},{3,1},{4,6},{5,7},{6,4},{7,5},{8,10},{9,11},{10,... | collective-permute-start | bytes 294920 | tf_op jit(solution)/shard_map/ppermute | solution.py:324
  142.7 12.4 %collective-permute-start.46 = (bf16[64,768]{1,0:T(8,128)(2,1)S(1)}, bf16[64,768]{1,0:T(8,128)(2,1)S(1)}, u32[]{:S(2)}, u32[]{:S(2)}) collective-permute-start(bf16[64,768]{1,0:T(8,128)(2,1)S(1)} %get-tuple-element.205), channel_id=1, source_target_pairs={{0,2},{1,3},{2,0},{3,1},{4,6},{5,7},{6,4},{7,5},{8,10},{9,11},{10,... | collective-permute-start | bytes 294920 | tf_op jit(solution)/shard_map/ppermute | solution.py:324
  145.0 4.5 %collective-permute-start.51 = (f32[16,96]{1,0:T(8,128)S(1)}, f32[16,96]{1,0:T(8,128)S(1)}, u32[]{:S(2)}, u32[]{:S(2)}) collective-permute-start(f32[16,96]{1,0:T(8,128)S(1)} %get-tuple-element.211), channel_id=1, source_target_pairs={{0,1},{1,0},{2,3},{3,2},{4,5},{5,4},{6,7},{7,6},{8,9},{9,8},{10,11... | collective-permute-start | bytes 18440 | tf_op jit(solution)/shard_map/ppermute | solution.py:324
  147.1 13.2 %collective-permute-start.58 = (bf16[96,768]{1,0:T(8,128)(2,1)}, bf16[96,768]{1,0:T(8,128)(2,1)S(1)}, u32[]{:S(2)}, u32[]{:S(2)}) collective-permute-start(bf16[96,768]{1,0:T(8,128)(2,1)} %get-tuple-element.227), channel_id=1, source_target_pairs={{0,2},{1,3},{2,0},{3,1},{4,6},{5,7},{6,4},{7,5},{8,10},{9,11},{10,... | collective-permute-start | bytes 442376 | tf_op jit(solution)/shard_map/ppermute | solution.py:324
  149.5 8.9 %collective-permute-start.52 = (f32[16,96]{1,0:T(8,128)S(1)}, f32[16,96]{1,0:T(8,128)S(1)}, u32[]{:S(2)}, u32[]{:S(2)}) collective-permute-start(f32[16,96]{1,0:T(8,128)S(1)} %add.85.near), channel_id=1, source_target_pairs={{0,2},{1,3},{2,0},{3,1},{4,6},{5,7},{6,4},{7,5},{8,10},{9,11},{10,... | collective-permute-start | bytes 18440 | tf_op jit(solution)/shard_map/ppermute | solution.py:324
  (26 other events, 142.7 us)

commit v5 on v3

--- a/solution.py
+++ b/solution.py
@@ -341,15 +341,13 @@
     ATTN_BLOCKS,
     ATTN_CORE,
     ATTN_FAR,
+    ATTN_FIRST,
     ATTN_HALF,
-    ATTN_OWNER,
     ATTN_PARTS,
+    ATTN_SENT,
     ATTN_SHARD,
     ATTN_SHARE,
-    BACK_SENT,
-    BLOCK_MOVED,
     BLOCK_OUT,
-    FAR,
     FEED,
     FEED_SEND,
     FF_BLOCKS,
@@ -361,6 +359,7 @@
     FF_MOVED,
     FF_OWNER,
     FF_SECOND,
+    FF_SHARD,
     FF_SHARE,
     GRAD_SILU,
     HIDDEN_BACK,
@@ -379,43 +378,43 @@
     PACKED_X,
     PACKED_Y,
     PARTIAL_CORE,
-    RESIDUAL,
     TABLE,
     TOKENS_HALF,
     TOKENS_SENT,
-    UPSTREAM_HALF,
+    UPSTREAM_FAR,
     UPSTREAM_SENT,
-) = range(51)
+) = range(49)
 
 HOLDS = {
     TOKENS_SENT: (ATTN_SHARD,),
-    PARTIAL_CORE: (ATTN_FAR, ATTN_SHARE, TOKENS_HALF,),
+    PARTIAL_CORE: (ATTN_FAR, ATTN_SHARE,),
+    FF_SHARD: (ATTN_FAR, TOKENS_HALF,),
+    MOD_LINE: (ATTN_FIRST,),
     MOD_PLACE: (ATTN_PARTS,),
     FF_FAR: (MOD_LINE,),
     UPSTREAM_SENT: (FF_FAR, FF_SHARE,),
     ATTEND: (FF_SHARE,),
+    UPSTREAM_FAR: (ATTEND_SEND,),
     FF_SECOND: (ATTEND_SEND,),
-    RESIDUAL: (UPSTREAM_HALF,),
     FF_BLOCKS: (FEED_SEND,),
     ACTIVATED: (FEED,),
     HIDDEN_BACK: (OUT_SEND,),
     FF_MIDDLE: (BLOCK_OUT, OUTPUT_NEAR,),
     ATTEND_BACK: (BLOCK_OUT, FF_GOING,),
-    BLOCK_MOVED: (OUTPUT_NEAR,),
     PACK: (FF_CORE,),
-    ATTN_BLOCKS: (PACK,),
+    ATTN_BLOCKS: (FF_HALF, PACK,),
     LINE_NEAR: (FF_CORE,),
     LINE: (FF_HALF,),
     LINE_FAR: (ATTN_BLOCKS, FF_HALF,),
     FF_CORE: (NORM_CROSSED,),
-    BACK_SENT: (FAR,),
     PACKED_X: (FF_CORE, FF_HALF,),
     PACKED_Y: (FF_MOVED,),
     MODULATION_BACK: (ATTN_CORE,),
     ATTN_HALF: (MODULATION_BACK,),
+    ATTN_SENT: (FF_MOVED, MODULATION_BACK,),
     GRAD_SILU: (FF_MOVED,),
+    TABLE: (FF_MOVED,),
     FF_OWNER: (NEAR,),
-    ATTN_OWNER: (TABLE,),
     OUTPUTS: (MODULATION_BACK,),
 }
 
@@ -1076,14 +1075,14 @@
         4,
         0,
     )[0]
-    attn_first = chip_first(attn_share)
+    attn_first = mark(ATTN_FIRST, chip_first(attn_share))
     attn_parts = chip_second(attn_share, *attn_first)
     mark(ATTN_PARTS, attn_parts)
     mod_near = swap(mod_cols, "tensor", 1)
     mod_line = jnp.concatenate([mod_cols, mod_near])
     mark(MOD_LINE, mod_line)
-    mod_far = swap(mod_line, "tensor", 2)
-    ff_far = mark(FF_FAR, swap(ff_shard, "tensor", 2))
+    mod_far = swap(hold(MOD_LINE, mod_line), "tensor", 2)
+    ff_far = mark(FF_FAR, swap(hold(FF_SHARD, ff_shard), "tensor", 2))
     tokens_across = swap(jnp.concatenate([tokens_half, tokens_near]), "dp", 1)
     row = ((1, model_width), jnp.float32)
     mod_full, qkv_bias, expand_row, _, gain_a, gate_a, shift_m, gain_m, gate_m = kernel_call(
@@ -1126,8 +1125,7 @@
     )
     keep, send = halve(own_partial, swap(other_partial, "dp", 1))
     mark(ATTEND_SEND, send)
-    upstream_half = jnp.concatenate([pick(cotangent, half), upstream_far])
-    mark(UPSTREAM_HALF, upstream_half)
+    upstream_half = jnp.concatenate([pick(cotangent, half), hold(UPSTREAM_FAR, upstream_far)])
     ff_first = hold(FF_SECOND, ff_first)
     ff_parts = chip_second(ff_share, *ff_first)
     got = swap(send, "tensor", 1)
@@ -1138,7 +1136,7 @@
         [(keep.shape, jnp.float32), (keep.shape, jnp.float32), (keep.shape, jnp.bfloat16)],
         [
             keep,
-            hold(RESIDUAL, got),
+            got,
             tokens_half,
             output_bias[None],
             gate_a,
@@ -1243,7 +1241,7 @@
         head_count,
         score_scale,
     )
-    block_moved = swap(hold(BLOCK_MOVED, block_own[count:]), "tensor", 2)
+    block_moved = swap(block_own[count:], "tensor", 2)
     norm_crossed = mark(NORM_CROSSED, swap(norm_sums[1:], "dp", 1))
     ff_mine, ff_other = core_step(core, ff_bases, hold(FF_CORE, ff_second))
     mark(FF_CORE, ff_mine)
@@ -1277,7 +1275,7 @@
     summed = lax.broadcasted_iota(jnp.int32, line.shape, 0) < 6
     near = hold(LINE, swap(hold(LINE_NEAR, line), "tensor", 1))
     line = line + jnp.where(summed, near, 0.0)
-    far = mark(FAR, swap(hold(LINE_FAR, line), "tensor", 2))
+    far = swap(hold(LINE_FAR, line), "tensor", 2)
     packed = kernel_call(
         choose_body,
         "choose",
@@ -1297,7 +1295,7 @@
         8,
         0,
     )
-    tokens_moved = swap(hold(BACK_SENT, back_sent), "tensor", 2)
+    tokens_moved = swap(back_sent, "tensor", 2)
     *attn_bases, attn_going, attn_going_second = middle_step(
         attn_blocks[:2], attn_first
     )
@@ -1323,19 +1321,18 @@
     )
     mark(MODULATION_BACK, grad_silu)
     attn_kept, attn_sent = half_step(is_own, attn_mine, hold(ATTN_HALF, swap(attn_other, "dp", 1)))
-    attn_moved = swap(attn_sent, "tensor", 2)
+    attn_moved = swap(hold(ATTN_SENT, attn_sent), "tensor", 2)
     near = grad_silu + swap(hold(GRAD_SILU, grad_silu), "tensor", 1)
     mark(NEAR, near)
     table_grad = kernel_call(
         table_body,
         "table",
         [((row_share, classes_total), jnp.float32)],
-        [labels_rel, cond, near, swap(near, "tensor", 2)],
+        [labels_rel, cond, near, hold(TABLE, swap(near, "tensor", 2))],
         [pltpu.VMEM((latent_total, classes_total), jnp.float32)],
         4,
         0,
     )[0]
-    mark(TABLE, table_grad)
     expand_grad, reduce_grad = owner_sum(
         ff_kept, hold(FF_OWNER, ff_moved), [ff_width, ff_width]
     )
@@ -1343,7 +1340,7 @@
         attend_owner_body,
         "owner_sum",
         [((3, row_share, head_width), jnp.float32), (output_weight.shape, jnp.float32)],
-        [attn_kept, hold(ATTN_OWNER, attn_moved)],
+        [attn_kept, attn_moved],
         [],
         8,
         0,

time: 166 us -> 161 us (0.970)
  starting transfers between devices: 65.9 us -> 49.8 us
  waiting for transfers between devices: 59.8 us -> 69.7 us
    ppermute x59, starting transfers between devices: 65.9 us -> 49.8 us  [swap(): lax.ppermute(values, axis, [(place, place ^ mask) for place in range(coun...]
    ppermute x59, waiting for transfers between devices: 59.8 us -> 69.7 us  [swap(): lax.ppermute(values, axis, [(place, place ^ mask) for place in range(coun...]
  transfers between devices with their start and end apart: 59 -> 59, of which waited for: 24 -> 32; matrix products, arithmetic and copies ran while one was open for 8% -> 8% of each run, Pallas kernels for 9% -> 9%
where the time goes in v5:
time: 161 us; the launch traced here: 160 us
  waiting for transfers between devices  69.7 us (43%)
  starting transfers between devices  49.8 us (31%)
  Pallas kernels  24.1 us (15%)
  other arithmetic  7.32 us (5%)
  local copies, waits for them, and re-layouts  6.05 us (4%)
  matrix products  2.1 us (1%)
    ppermute x59, waiting for transfers between devices, swap(): lax.ppermute(values, axis, [(place, place ^ mask) for place in range(coun...  69.7 us
    ppermute x59, starting transfers between devices, swap(): lax.ppermute(values, axis, [(place, place ^ mask) for place in range(coun...  49.8 us
    pallas_call x28, Pallas kernels, kernel_call(): pl.pallas_call(body, out_shape=shapes, in_specs=specs, out_specs=[pl.Bloc...  24.1 us
  transfers between devices with their start and end apart: 59, of which 32 were waited for; matrix products, arithmetic and copies ran while one was open for 8% of the time, Pallas kernels for 9%

profile of v5, /device:TPU:0, one launch (start us, length us, event | category | flops | bytes accessed | tf_op | source)
XLA Modules:
  0.0 160.3 jit_solution(13998660422757464303)
XLA Ops:
  2.6 4.1 %collective-permute-start.3 = (bf16[96,768]{1,0:T(8,128)(2,1)S(1)}, bf16[96,768]{1,0:T(8,128)(2,1)S(1)}, u32[]{:S(2)}, u32[]{:S(2)}) collective-permute-start(bf16[96,768]{1,0:T(8,128)(2,1)S(1)} %join_weights.1), channel_id=1, source_target_pairs={{0,2},{1,3},{2,0},{3,1},{4,6},{5,7},{6,4},{7,5},{8,10},{9,11},{10,... | collective-permute-start | bytes 442376 | tf_op jit(solution)/shard_map/ppermute | solution.py:324
  9.5 1.6 collective-permute-start.5
  11.0 1.5 dynamic-slice_bitcast_fusion.2
  13.9 1.6 %collective-permute-start.6 = (f32[4,1152]{1,0:T(4,128)S(1)}, f32[4,1152]{1,0:T(4,128)S(1)}, u32[]{:S(2)}, u32[]{:S(2)}) collective-permute-start(f32[4,1152]{1,0:T(4,128)S(1)} %slice.57), channel_id=1, source_target_pairs={{0,8},{4,12},{8,0},{12,4},{16,24},{20,28},{24,16},{28,20},{1,9},{5... | collective-permute-start | bytes 55304 | tf_op jit(solution)/shard_map/ppermute | solution.py:324
  15.5 1.3 collective-permute-start.11
  16.8 1.5 collective-permute-start.12
  18.3 1.4 collective-permute-done
  19.9 1.7 %collective-permute-done.11.refs_6_ = bf16[96,768]{1,0:T(8,128)(2,1)S(1)} collective-permute-done((bf16[96,768]{1,0:T(8,128)(2,1)S(1)}, bf16[96,768]{1,0:T(8,128)(2,1)S(1)}, u32[]{:S(2)}, u32[]{:S(2)}) %collective-permute-start.11) | collective-permute-done | bytes 147488 | tf_op jit(solution)/shard_map/ppermute | solution.py:324
  23.3 1.2 collective-permute-done.8.crossed
  24.6 2.7 %collective-permute-start.9 = (f32[8,1152]{1,0:T(8,128)S(1)}, f32[8,1152]{1,0:T(8,128)S(1)}, u32[]{:S(2)}, u32[]{:S(2)}) collective-permute-start(f32[8,1152]{1,0:T(8,128)S(1)} %mod_sum.1.own), channel_id=1, source_target_pairs={{0,1},{1,0},{2,3},{3,2},{4,5},{5,4},{6,7},{7,6},{8,9},{9,8},{10,11... | collective-permute-start | bytes 110600 | tf_op jit(solution)/shard_map/ppermute | solution.py:324
  27.3 1.7 %collective-permute-start.14 = (bf16[192,768]{1,0:T(8,128)(2,1)}, bf16[192,768]{1,0:T(8,128)(2,1)S(1)}, u32[]{:S(2)}, u32[]{:S(2)}) collective-permute-start(bf16[192,768]{1,0:T(8,128)(2,1)} %get-tuple-element.262), channel_id=1, source_target_pairs={{0,16},{4,20},{8,24},{12,28},{16,0},{20,4},{24,8},{28,12},{1,17},{... | collective-permute-start | bytes 884744 | tf_op jit(solution)/shard_map/ppermute | solution.py:324
  29.9 4.5 %collective-permute-done.4 = bf16[96,1536]{1,0:T(8,128)(2,1)} collective-permute-done((bf16[96,1536]{1,0:T(8,128)(2,1)S(1)}, bf16[96,1536]{1,0:T(8,128)(2,1)}, u32[]{:S(2)}, u32[]{:S(2)}) %collective-permute-start.4) | collective-permute-done | bytes 294944 | tf_op jit(solution)/shard_map/ppermute | solution.py:324
  34.4 1.7 %broadcast_select_fusion = bf16[96,1536]{1,0:T(8,128)(2,1)} fusion(bf16[96,1536]{1,0:T(8,128)(2,1)} %collective-permute-done.4, bf16[96,1536]{1,0:T(8,128)(2,1)S(1)} %constant_dynamic-update-slice_fusion, pred[]{:T(512)S(6)} %eq.21), kind=kLoop, calls=%fused_computation.14 | loop fusion | flops 147456 | bytes 884737 | tf_op jit(solution)/shard_map/jit(_where)/select_n | solution.py:437
  38.1 4.7 %collective-permute-done.13.far = f32[16,1152]{1,0:T(8,128)S(1)} collective-permute-done((f32[16,1152]{1,0:T(8,128)S(1)}, f32[16,1152]{1,0:T(8,128)S(1)}, u32[]{:S(2)}, u32[]{:S(2)}) %collective-permute-start.13) | collective-permute-done | bytes 73760 | tf_op jit(solution)/shard_map/ppermute | solution.py:324
  42.8 1.1 mod_place.1
  43.9 1.1 broadcast_select_fusion.2
  45.1 4.0 %attend_forward.1 = (bf16[512,768]{1,0:T(8,128)(2,1)S(1)}, f32[512,768]{1,0:T(8,128)S(1)}, bf16[512,576]{1,0:T(8,128)(2,1)S(1)}, bf16[512,192]{1,0:T(8,128)(2,1)...) custom-call(s32[1]{0:T(128)} %bitcast.1.chip_ref, ...), custom_call_target="tpu_custom_call" | custom-call | flops 704643072 | bytes 7903492 | tf_op jit(solution)/shard_map/attend_forward/pallas_call | solution.py:536
  49.3 1.4 collective-permute-start.24
  51.8 2.5 %collective-permute-start.17 = (bf16[128,768]{1,0:T(8,128)(2,1)S(1)}, bf16[128,768]{1,0:T(8,128)(2,1)S(1)}, u32[]{:S(2)}, u32[]{:S(2)}) collective-permute-start(bf16[128,768]{1,0:T(8,128)(2,1)S(1)} %get-tuple-element.141), channel_id=1, source_target_pairs={{0,1},{1,0},{2,3},{3,2},{4,5},{5,4},{6,7},{7,6},{8,9},{9,8},{10,11... | collective-permute-start | bytes 589832 | tf_op jit(solution)/shard_map/ppermute | solution.py:324
  54.4 4.3 %collective-permute-done.24.refs_10_ = bf16[96,1536]{1,0:T(8,128)(2,1)S(1)} collective-permute-done((bf16[96,1536]{1,0:T(8,128)(2,1)S(1)}, bf16[96,1536]{1,0:T(8,128)(2,1)S(1)}, u32[]{:S(2)}, u32[]{:S(2)}) %collective-permute-start.24) | collective-permute-done | bytes 294944 | tf_op jit(solution)/shard_map/ppermute | solution.py:324
  58.6 1.2 collective-permute-done.25.refs_11_
  60.6 1.5 collective-permute-start.26
  62.2 4.3 %collective-permute-done.22.refs_5_ = bf16[128,768]{1,0:T(8,128)(2,1)S(1)} collective-permute-done((bf16[128,768]{1,0:T(8,128)(2,1)S(1)}, bf16[128,768]{1,0:T(8,128)(2,1)S(1)}, u32[]{:S(2)}, u32[]{:S(2)}) %collective-permute-start.22) | collective-permute-done | bytes 196640 | tf_op jit(solution)/shard_map/ppermute | solution.py:324
  67.5 6.7 %collective-permute-done.18.refs_1_ = bf16[128,768]{1,0:T(8,128)(2,1)S(1)} collective-permute-done((bf16[128,768]{1,0:T(8,128)(2,1)S(1)}, bf16[128,768]{1,0:T(8,128)(2,1)S(1)}, u32[]{:S(2)}, u32[]{:S(2)}) %collective-permute-start.18) | collective-permute-done | bytes 196640 | tf_op jit(solution)/shard_map/ppermute | solution.py:324
  75.6 4.2 %feed_forward.1 = (bf16[512,768]{1,0:T(8,128)(2,1)S(1)}, f32[1,768]{1,0:T(1,128)S(1)}, bf16[768,768]{1,0:T(8,128)(2,1)S(1)}, f32[256,768]{1,0:T(8,128)S(1)}, f32...) custom-call(s32[1]{0:T(128)} %bitcast.1.chip_ref, ...), custom_call_target="tpu_custom_call" | custom-call | flops 3019898880 | bytes 11053060 | tf_op jit(solution)/shard_map/feed_forward/pallas_call | solution.py:536
  81.0 1.2 collective-permute-done.31.got
  82.2 1.5 collective-permute-start.36
  87.3 5.1 %collective-permute-done.32.got = bf16[128,768]{1,0:T(8,128)(2,1)S(1)} collective-permute-done((bf16[128,768]{1,0:T(8,128)(2,1)S(1)}, bf16[128,768]{1,0:T(8,128)(2,1)S(1)}, u32[]{:S(2)}, u32[]{:S(2)}) %collective-permute-start.32) | collective-permute-done | bytes 196640 | tf_op jit(solution)/shard_map/ppermute | solution.py:324
  93.1 1.2 collective-permute-start.33
  94.3 2.4 %collective-permute-done.29.got = bf16[128,768]{1,0:T(8,128)(2,1)S(1)} collective-permute-done((bf16[128,768]{1,0:T(8,128)(2,1)S(1)}, bf16[128,768]{1,0:T(8,128)(2,1)S(1)}, u32[]{:S(2)}, u32[]{:S(2)}) %collective-permute-start.29) | collective-permute-done | bytes 196640 | tf_op jit(solution)/shard_map/ppermute | solution.py:324
  96.8 2.6 %collective-permute-done.33.refs_1_ = bf16[128,768]{1,0:T(8,128)(2,1)S(1)} collective-permute-done((bf16[128,768]{1,0:T(8,128)(2,1)S(1)}, bf16[128,768]{1,0:T(8,128)(2,1)S(1)}, u32[]{:S(2)}, u32[]{:S(2)}) %collective-permute-start.33) | collective-permute-done | bytes 196640 | tf_op jit(solution)/shard_map/ppermute | solution.py:324
  99.6 1.2 collective-permute-start.42
  103.2 4.3 %attend_back.1 = (bf16[512,768]{1,0:T(8,128)(2,1)S(1)}, bf16[512,576]{1,0:T(8,128)(2,1)S(1)}, f32[1,576]{1,0:T(1,128)S(1)}, f32[2,1536]{1,0:T(2,128)S(1)}, f32[2...) custom-call(bf16[128,768]{1,0:T(8,128)(2,1)S(1)} %get-tuple-element.175.refs_0_, ...), custom_call_target="tpu_custom_call" | custom-call | flops 855638016 | bytes 7289088 | tf_op jit(solution)/shard_map/attend_back/pallas_call | solution.py:536
  109.2 1.1 collective-permute-start.44
  111.1 2.1 %collective-permute-done.44 = f32[8,1152]{1,0:T(8,128)S(1)} collective-permute-done((f32[8,1152]{1,0:T(8,128)S(1)}, f32[8,1152]{1,0:T(8,128)S(1)}, u32[]{:S(2)}, u32[]{:S(2)}) %collective-permute-start.44) | collective-permute-done | bytes 36896 | tf_op jit(solution)/shard_map/ppermute | solution.py:324
  113.2 1.2 grad_blocks.1
  114.5 1.4 collective-permute-start.46
  115.9 3.5 %collective-permute-done.46.far = f32[8,1152]{1,0:T(8,128)S(1)} collective-permute-done((f32[8,1152]{1,0:T(8,128)S(1)}, f32[8,1152]{1,0:T(8,128)S(1)}, u32[]{:S(2)}, u32[]{:S(2)}) %collective-permute-start.46) | collective-permute-done | bytes 36896 | tf_op jit(solution)/shard_map/ppermute | solution.py:324
  120.0 1.5 collective-permute-start.51
  122.4 1.2 collective-permute-start.48
  123.6 1.2 collective-permute-start.49
  125.9 4.0 %collective-permute-done.51.got_first = bf16[192,768]{1,0:T(8,128)(2,1)S(1)} collective-permute-done((bf16[192,768]{1,0:T(8,128)(2,1)S(1)}, bf16[192,768]{1,0:T(8,128)(2,1)S(1)}, u32[]{:S(2)}, u32[]{:S(2)}) %collective-permute-start.51) | collective-permute-done | bytes 294944 | tf_op jit(solution)/shard_map/ppermute | solution.py:324
  131.6 1.2 collective-permute-start.54
  132.8 6.5 %collective-permute-done.49.moved = bf16[96,1536]{1,0:T(8,128)(2,1)S(1)} collective-permute-done((bf16[96,1536]{1,0:T(8,128)(2,1)S(1)}, bf16[96,1536]{1,0:T(8,128)(2,1)S(1)}, u32[]{:S(2)}, u32[]{:S(2)}) %collective-permute-start.49) | collective-permute-done | bytes 294944 | tf_op jit(solution)/shard_map/ppermute | solution.py:324
  140.9 3.0 %collective-permute-start.40 = (bf16[64,768]{1,0:T(8,128)(2,1)S(1)}, bf16[64,768]{1,0:T(8,128)(2,1)S(1)}, u32[]{:S(2)}, u32[]{:S(2)}) collective-permute-start(bf16[64,768]{1,0:T(8,128)(2,1)S(1)} %get-tuple-element.191), channel_id=1, source_target_pairs={{0,2},{1,3},{2,0},{3,1},{4,6},{5,7},{6,4},{7,5},{8,10},{9,11},{10,... | collective-permute-start | bytes 294920 | tf_op jit(solution)/shard_map/ppermute | solution.py:324
  146.9 2.1 %collective-permute-start.58 = (bf16[96,768]{1,0:T(8,128)(2,1)}, bf16[96,768]{1,0:T(8,128)(2,1)S(1)}, u32[]{:S(2)}, u32[]{:S(2)}) collective-permute-start(bf16[96,768]{1,0:T(8,128)(2,1)} %get-tuple-element.237), channel_id=1, source_target_pairs={{0,2},{1,3},{2,0},{3,1},{4,6},{5,7},{6,4},{7,5},{8,10},{9,11},{10,... | collective-permute-start | bytes 442376 | tf_op jit(solution)/shard_map/ppermute | solution.py:324
  154.3 3.4 %collective-permute-done.56.far = f32[16,96]{1,0:T(8,128)S(1)} collective-permute-done((f32[16,96]{1,0:T(8,128)S(1)}, f32[16,96]{1,0:T(8,128)S(1)}, u32[]{:S(2)}, u32[]{:S(2)}) %collective-permute-start.56) | collective-permute-done | bytes 6176 | tf_op jit(solution)/shard_map/ppermute | solution.py:324
  157.7 1.8 %table.1 = f32[96,1000]{1,0:T(8,128)} custom-call(s32[16]{0:T(128)S(1)} %get-tuple-element.251.labels, f32[16,96]{1,0:T(8,128)S(1)} %get-tuple-element.253.cond, f32[16,96]{1,0:T(8,128)S(1)} %add.85.near, f32[16,96]{1,0:T(8,128)S(1)} %collective-permute-done.56.far), custom_call_target="tpu_custom_call" | custom-call | bytes 402496 | tf_op jit(solution)/shard_map/table/pallas_call | solution.py:536
  (181 shorter events, 41.0 us)
Async XLA Ops:
  2.6 11.1 %collective-permute-start.3 = (bf16[96,768]{1,0:T(8,128)(2,1)S(1)}, bf16[96,768]{1,0:T(8,128)(2,1)S(1)}, u32[]{:S(2)}, u32[]{:S(2)}) collective-permute-start(bf16[96,768]{1,0:T(8,128)(2,1)S(1)} %join_weights.1), channel_id=1, source_target_pairs={{0,2},{1,3},{2,0},{3,1},{4,6},{5,7},{6,4},{7,5},{8,10},{9,11},{10,... | collective-permute-start | bytes 442376 | tf_op jit(solution)/shard_map/ppermute | solution.py:324
  9.5 4.4 %collective-permute-start.5 = (f32[8,1152]{1,0:T(8,128)S(1)}, f32[8,1152]{1,0:T(8,128)S(1)}, u32[]{:S(2)}, u32[]{:S(2)}) collective-permute-start(f32[8,1152]{1,0:T(8,128)S(1)} %slice.55), channel_id=1, source_target_pairs={{0,16},{4,20},{8,24},{12,28},{16,0},{20,4},{24,8},{28,12},{1,17},{... | collective-permute-start | bytes 110600 | tf_op jit(solution)/shard_map/ppermute | solution.py:324
  12.6 7.2 %collective-permute-start = (bf16[64,768]{1,0:T(8,128)(2,1)}, bf16[64,768]{1,0:T(8,128)(2,1)S(1)}, u32[]{:S(2)}, u32[]{:S(2)}) collective-permute-start(bf16[64,768]{1,0:T(8,128)(2,1)} %dynamic-slice_bitcast_fusion.2), channel_id=1, source_target_pairs={{0,2},{1,3},{2,0},{3,1},{4,6},{5,7},{6,4},{7,5},{8,10},{9,11},{10,... | collective-permute-start | bytes 294920 | tf_op jit(solution)/shard_map/ppermute | solution.py:324
  13.9 4.4 %collective-permute-start.6 = (f32[4,1152]{1,0:T(4,128)S(1)}, f32[4,1152]{1,0:T(4,128)S(1)}, u32[]{:S(2)}, u32[]{:S(2)}) collective-permute-start(f32[4,1152]{1,0:T(4,128)S(1)} %slice.57), channel_id=1, source_target_pairs={{0,8},{4,12},{8,0},{12,4},{16,24},{20,28},{24,16},{28,20},{1,9},{5... | collective-permute-start | bytes 55304 | tf_op jit(solution)/shard_map/ppermute | solution.py:324
  15.5 6.0 %collective-permute-start.11 = (bf16[96,768]{1,0:T(8,128)(2,1)S(1)}, bf16[96,768]{1,0:T(8,128)(2,1)S(1)}, u32[]{:S(2)}, u32[]{:S(2)}) collective-permute-start(bf16[96,768]{1,0:T(8,128)(2,1)S(1)} %get-tuple-element.257), channel_id=1, source_target_pairs={{0,8},{4,12},{8,0},{12,4},{16,24},{20,28},{24,16},{28,20},{1,9},{5... | collective-permute-start | bytes 442376 | tf_op jit(solution)/shard_map/ppermute | solution.py:324
  16.8 5.6 %collective-permute-start.12 = (bf16[96,768]{1,0:T(8,128)(2,1)S(1)}, bf16[96,768]{1,0:T(8,128)(2,1)S(1)}, u32[]{:S(2)}, u32[]{:S(2)}) collective-permute-start(bf16[96,768]{1,0:T(8,128)(2,1)S(1)} %get-tuple-element.256), channel_id=1, source_target_pairs={{0,16},{4,20},{8,24},{12,28},{16,0},{20,4},{24,8},{28,12},{1,17},{... | collective-permute-start | bytes 442376 | tf_op jit(solution)/shard_map/ppermute | solution.py:324
  19.8 14.6 %collective-permute-start.4 = (bf16[96,1536]{1,0:T(8,128)(2,1)S(1)}, bf16[96,1536]{1,0:T(8,128)(2,1)}, u32[]{:S(2)}, u32[]{:S(2)}) collective-permute-start(bf16[96,1536]{1,0:T(8,128)(2,1)S(1)} %constant_dynamic-update-slice_fusion), channel_id=1, source_target_pairs={{0,2},{1,3},{2,0},{3,1},{4,6},{5,7},{6,4},{7,5},{8,10},{9,11},{10,... | collective-permute-start | bytes 884744 | tf_op jit(solution)/shard_map/ppermute | solution.py:324
  24.6 5.4 %collective-permute-start.9 = (f32[8,1152]{1,0:T(8,128)S(1)}, f32[8,1152]{1,0:T(8,128)S(1)}, u32[]{:S(2)}, u32[]{:S(2)}) collective-permute-start(f32[8,1152]{1,0:T(8,128)S(1)} %mod_sum.1.own), channel_id=1, source_target_pairs={{0,1},{1,0},{2,3},{3,2},{4,5},{5,4},{6,7},{7,6},{8,9},{9,8},{10,11... | collective-permute-start | bytes 110600 | tf_op jit(solution)/shard_map/ppermute | solution.py:324
  27.2 9.9 %collective-permute-start.1 = (bf16[128,768]{1,0:T(8,128)(2,1)S(1)}, bf16[128,768]{1,0:T(8,128)(2,1)S(1)}, u32[]{:S(2)}, u32[]{:S(2)}) collective-permute-start(bf16[128,768]{1,0:T(8,128)(2,1)S(1)} %pad_maximum_fusion.9.refs_0_.tokens), channel_id=1, source_target_pairs={{0,1},{1,0},{2,3},{3,2},{4,5},{5,4},{6,7},{7,6},{8,9},{9,8},{10,11... | collective-permute-start | bytes 589832 | tf_op jit(solution)/shard_map/ppermute | solution.py:324
  27.3 15.5 %collective-permute-start.14 = (bf16[192,768]{1,0:T(8,128)(2,1)}, bf16[192,768]{1,0:T(8,128)(2,1)S(1)}, u32[]{:S(2)}, u32[]{:S(2)}) collective-permute-start(bf16[192,768]{1,0:T(8,128)(2,1)} %get-tuple-element.262), channel_id=1, source_target_pairs={{0,16},{4,20},{8,24},{12,28},{16,0},{20,4},{24,8},{28,12},{1,17},{... | collective-permute-start | bytes 884744 | tf_op jit(solution)/shard_map/ppermute | solution.py:324
  29.0 13.7 %collective-permute-start.15 = (bf16[192,768]{1,0:T(8,128)(2,1)}, bf16[192,768]{1,0:T(8,128)(2,1)}, u32[]{:S(2)}, u32[]{:S(2)}) collective-permute-start(bf16[192,768]{1,0:T(8,128)(2,1)} %get-tuple-element.260), channel_id=1, source_target_pairs={{0,8},{4,12},{8,0},{12,4},{16,24},{20,28},{24,16},{28,20},{1,9},{5... | collective-permute-start | bytes 884744 | tf_op jit(solution)/shard_map/ppermute | solution.py:324
  36.1 7.8 %collective-permute-start.10 = (bf16[96,1536]{1,0:T(8,128)(2,1)}, bf16[96,1536]{1,0:T(8,128)(2,1)}, u32[]{:S(2)}, u32[]{:S(2)}) collective-permute-start(bf16[96,1536]{1,0:T(8,128)(2,1)} %broadcast_select_fusion), channel_id=1, source_target_pairs={{0,4},{4,0},{8,12},{12,8},{16,20},{20,16},{24,28},{28,24},{1,5},{5... | collective-permute-start | bytes 884744 | tf_op jit(solution)/shard_map/ppermute | solution.py:324
  36.2 6.6 %collective-permute-start.13 = (f32[16,1152]{1,0:T(8,128)S(1)}, f32[16,1152]{1,0:T(8,128)S(1)}, u32[]{:S(2)}, u32[]{:S(2)}) collective-permute-start(f32[16,1152]{1,0:T(8,128)S(1)} %pad_maximum_fusion.12), channel_id=1, source_target_pairs={{0,2},{1,3},{2,0},{3,1},{4,6},{5,7},{6,4},{7,5},{8,10},{9,11},{10,... | collective-permute-start | bytes 221192 | tf_op jit(solution)/shard_map/ppermute | solution.py:324
  38.0 7.1 %collective-permute-start.2 = (bf16[256,768]{1,0:T(8,128)(2,1)S(1)}, bf16[256,768]{1,0:T(8,128)(2,1)S(1)}, u32[]{:S(2)}, u32[]{:S(2)}) collective-permute-start(bf16[256,768]{1,0:T(8,128)(2,1)S(1)} %pad_maximum_fusion.3), channel_id=1, source_target_pairs={{0,4},{4,0},{8,12},{12,8},{16,20},{20,16},{24,28},{28,24},{1,5},{5... | collective-permute-start | bytes 1179656 | tf_op jit(solution)/shard_map/ppermute | solution.py:324
  49.3 9.4 %collective-permute-start.24 = (bf16[96,1536]{1,0:T(8,128)(2,1)S(1)}, bf16[96,1536]{1,0:T(8,128)(2,1)S(1)}, u32[]{:S(2)}, u32[]{:S(2)}) collective-permute-start(bf16[96,1536]{1,0:T(8,128)(2,1)S(1)} %get-tuple-element.255), channel_id=1, source_target_pairs={{0,8},{4,12},{8,0},{12,4},{16,24},{20,28},{24,16},{28,20},{1,9},{5... | collective-permute-start | bytes 884744 | tf_op jit(solution)/shard_map/ppermute | solution.py:324
  50.7 9.1 %collective-permute-start.25 = (bf16[96,1536]{1,0:T(8,128)(2,1)S(1)}, bf16[96,1536]{1,0:T(8,128)(2,1)S(1)}, u32[]{:S(2)}, u32[]{:S(2)}) collective-permute-start(bf16[96,1536]{1,0:T(8,128)(2,1)S(1)} %get-tuple-element.254), channel_id=1, source_target_pairs={{0,16},{4,20},{8,24},{12,28},{16,0},{20,4},{24,8},{28,12},{1,17},{... | collective-permute-start | bytes 884744 | tf_op jit(solution)/shard_map/ppermute | solution.py:324
  51.6 8.9 %collective-permute-start.21 = (bf16[64,768]{1,0:T(8,128)(2,1)S(1)}, bf16[64,768]{1,0:T(8,128)(2,1)S(1)}, u32[]{:S(2)}, u32[]{:S(2)}) collective-permute-start(bf16[64,768]{1,0:T(8,128)(2,1)S(1)} %get-tuple-element.146), channel_id=1, source_target_pairs={{0,2},{1,3},{2,0},{3,1},{4,6},{5,7},{6,4},{7,5},{8,10},{9,11},{10,... | collective-permute-start | bytes 294920 | tf_op jit(solution)/shard_map/ppermute | solution.py:324
  51.8 14.7 %collective-permute-start.17 = (bf16[128,768]{1,0:T(8,128)(2,1)S(1)}, bf16[128,768]{1,0:T(8,128)(2,1)S(1)}, u32[]{:S(2)}, u32[]{:S(2)}) collective-permute-start(bf16[128,768]{1,0:T(8,128)(2,1)S(1)} %get-tuple-element.141), channel_id=1, source_target_pairs={{0,1},{1,0},{2,3},{3,2},{4,5},{5,4},{6,7},{7,6},{8,9},{9,8},{10,11... | collective-permute-start | bytes 589832 | tf_op jit(solution)/shard_map/ppermute | solution.py:324
  59.8 14.6 %collective-permute-start.27 = (bf16[192,1536]{1,0:T(8,128)(2,1)S(1)}, bf16[192,1536]{1,0:T(8,128)(2,1)S(1)}, u32[]{:S(2)}, u32[]{:S(2)}) collective-permute-start(bf16[192,1536]{1,0:T(8,128)(2,1)S(1)} %pad_maximum_fusion.2), channel_id=1, source_target_pairs={{0,8},{4,12},{8,0},{12,4},{16,24},{20,28},{24,16},{28,20},{1,9},{5... | collective-permute-start | bytes 1769480 | tf_op jit(solution)/shard_map/ppermute | solution.py:324
  60.5 5.9 %collective-permute-start.22 = (bf16[128,768]{1,0:T(8,128)(2,1)S(1)}, bf16[128,768]{1,0:T(8,128)(2,1)S(1)}, u32[]{:S(2)}, u32[]{:S(2)}) collective-permute-start(bf16[128,768]{1,0:T(8,128)(2,1)S(1)} %pad_maximum_fusion.10.refs_4_.upstream), channel_id=1, source_target_pairs={{0,1},{1,0},{2,3},{3,2},{4,5},{5,4},{6,7},{7,6},{8,9},{9,8},{10,11... | collective-permute-start | bytes 589832 | tf_op jit(solution)/shard_map/ppermute | solution.py:324
  60.6 14.4 %collective-permute-start.26 = (bf16[192,1536]{1,0:T(8,128)(2,1)S(1)}, bf16[192,1536]{1,0:T(8,128)(2,1)S(1)}, u32[]{:S(2)}, u32[]{:S(2)}) collective-permute-start(bf16[192,1536]{1,0:T(8,128)(2,1)S(1)} %pad_maximum_fusion), channel_id=1, source_target_pairs={{0,16},{4,20},{8,24},{12,28},{16,0},{20,4},{24,8},{28,12},{1,17},{... | collective-permute-start | bytes 1769480 | tf_op jit(solution)/shard_map/ppermute | solution.py:324
  66.5 8.5 %collective-permute-start.23 = (bf16[256,768]{1,0:T(8,128)(2,1)S(1)}, bf16[256,768]{1,0:T(8,128)(2,1)S(1)}, u32[]{:S(2)}, u32[]{:S(2)}) collective-permute-start(bf16[256,768]{1,0:T(8,128)(2,1)S(1)} %pad_maximum_fusion.4), channel_id=1, source_target_pairs={{0,4},{4,0},{8,12},{12,8},{16,20},{20,16},{24,28},{28,24},{1,5},{5... | collective-permute-start | bytes 1179656 | tf_op jit(solution)/shard_map/ppermute | solution.py:324
  66.8 7.4 %collective-permute-start.18 = (bf16[128,768]{1,0:T(8,128)(2,1)S(1)}, bf16[128,768]{1,0:T(8,128)(2,1)S(1)}, u32[]{:S(2)}, u32[]{:S(2)}) collective-permute-start(bf16[128,768]{1,0:T(8,128)(2,1)S(1)} %get-tuple-element.145.refs_0_), channel_id=1, source_target_pairs={{0,1},{1,0},{2,3},{3,2},{4,5},{5,4},{6,7},{7,6},{8,9},{9,8},{10,11... | collective-permute-start | bytes 589832 | tf_op jit(solution)/shard_map/ppermute | solution.py:324
  67.2 7.0 %collective-permute-start.19 = (bf16[128,768]{1,0:T(8,128)(2,1)S(1)}, bf16[128,768]{1,0:T(8,128)(2,1)S(1)}, u32[]{:S(2)}, u32[]{:S(2)}) collective-permute-start(bf16[128,768]{1,0:T(8,128)(2,1)S(1)} %get-tuple-element.145.refs_0_), channel_id=1, source_target_pairs={{0,4},{4,0},{8,12},{12,8},{16,20},{20,16},{24,28},{28,24},{1,5},{5... | collective-permute-start | bytes 589832 | tf_op jit(solution)/shard_map/ppermute | solution.py:324
  80.5 5.7 %collective-permute-start.28 = (f32[256,768]{1,0:T(8,128)S(1)}, f32[256,768]{1,0:T(8,128)S(1)}, u32[]{:S(2)}, u32[]{:S(2)}) collective-permute-start(f32[256,768]{1,0:T(8,128)S(1)} %fusion), channel_id=1, source_target_pairs={{0,4},{4,0},{8,12},{12,8},{16,20},{20,16},{24,28},{28,24},{1,5},{5... | collective-permute-start | bytes 2359304 | tf_op jit(solution)/shard_map/ppermute | solution.py:324
  82.2 17.2 %collective-permute-start.36 = (bf16[192,1536]{1,0:T(8,128)(2,1)S(1)}, bf16[192,1536]{1,0:T(8,128)(2,1)S(1)}, u32[]{:S(2)}, u32[]{:S(2)}) collective-permute-start(bf16[192,1536]{1,0:T(8,128)(2,1)S(1)} %get-tuple-element.170), channel_id=1, source_target_pairs={{0,8},{4,12},{8,0},{12,4},{16,24},{20,28},{24,16},{28,20},{1,9},{5... | collective-permute-start | bytes 1769480 | tf_op jit(solution)/shard_map/ppermute | solution.py:324
  83.7 15.7 %collective-permute-start.37 = (bf16[192,1536]{1,0:T(8,128)(2,1)S(1)}, bf16[192,1536]{1,0:T(8,128)(2,1)S(1)}, u32[]{:S(2)}, u32[]{:S(2)}) collective-permute-start(bf16[192,1536]{1,0:T(8,128)(2,1)S(1)} %get-tuple-element.171), channel_id=1, source_target_pairs={{0,16},{4,20},{8,24},{12,28},{16,0},{20,4},{24,8},{28,12},{1,17},{... | collective-permute-start | bytes 1769480 | tf_op jit(solution)/shard_map/ppermute | solution.py:324
  84.6 7.8 %collective-permute-start.32 = (bf16[128,768]{1,0:T(8,128)(2,1)S(1)}, bf16[128,768]{1,0:T(8,128)(2,1)S(1)}, u32[]{:S(2)}, u32[]{:S(2)}) collective-permute-start(bf16[128,768]{1,0:T(8,128)(2,1)S(1)} %get-tuple-element.162), channel_id=1, source_target_pairs={{0,1},{1,0},{2,3},{3,2},{4,5},{5,4},{6,7},{7,6},{8,9},{9,8},{10,11... | collective-permute-start | bytes 589832 | tf_op jit(solution)/shard_map/ppermute | solution.py:324
  86.3 10.3 %collective-permute-start.29 = (bf16[128,768]{1,0:T(8,128)(2,1)S(1)}, bf16[128,768]{1,0:T(8,128)(2,1)S(1)}, u32[]{:S(2)}, u32[]{:S(2)}) collective-permute-start(bf16[128,768]{1,0:T(8,128)(2,1)S(1)} %get-tuple-element.156), channel_id=1, source_target_pairs={{0,1},{1,0},{2,3},{3,2},{4,5},{5,4},{6,7},{7,6},{8,9},{9,8},{10,11... | collective-permute-start | bytes 589832 | tf_op jit(solution)/shard_map/ppermute | solution.py:324
  93.1 6.3 %collective-permute-start.33 = (bf16[128,768]{1,0:T(8,128)(2,1)S(1)}, bf16[128,768]{1,0:T(8,128)(2,1)S(1)}, u32[]{:S(2)}, u32[]{:S(2)}) collective-permute-start(bf16[128,768]{1,0:T(8,128)(2,1)S(1)} %get-tuple-element.175.refs_0_), channel_id=1, source_target_pairs={{0,1},{1,0},{2,3},{3,2},{4,5},{5,4},{6,7},{7,6},{8,9},{9,8},{10,11... | collective-permute-start | bytes 589832 | tf_op jit(solution)/shard_map/ppermute | solution.py:324
  99.6 9.1 %collective-permute-start.42 = (bf16[96,1536]{1,0:T(8,128)(2,1)S(1)}, bf16[96,1536]{1,0:T(8,128)(2,1)S(1)}, u32[]{:S(2)}, u32[]{:S(2)}) collective-permute-start(bf16[96,1536]{1,0:T(8,128)(2,1)S(1)} %get-tuple-element.174), channel_id=1, source_target_pairs={{0,16},{4,20},{8,24},{12,28},{16,0},{20,4},{24,8},{28,12},{1,17},{... | collective-permute-start | bytes 884744 | tf_op jit(solution)/shard_map/ppermute | solution.py:324
  100.8 7.8 %collective-permute-start.43 = (bf16[96,1536]{1,0:T(8,128)(2,1)S(1)}, bf16[96,1536]{1,0:T(8,128)(2,1)S(1)}, u32[]{:S(2)}, u32[]{:S(2)}) collective-permute-start(bf16[96,1536]{1,0:T(8,128)(2,1)S(1)} %get-tuple-element.195), channel_id=1, source_target_pairs={{0,8},{4,12},{8,0},{12,4},{16,24},{20,28},{24,16},{28,20},{1,9},{5... | collective-permute-start | bytes 884744 | tf_op jit(solution)/shard_map/ppermute | solution.py:324
  109.2 4.0 %collective-permute-start.44 = (f32[8,1152]{1,0:T(8,128)S(1)}, f32[8,1152]{1,0:T(8,128)S(1)}, u32[]{:S(2)}, u32[]{:S(2)}) collective-permute-start(f32[8,1152]{1,0:T(8,128)S(1)} %pack.1), channel_id=1, source_target_pairs={{0,1},{1,0},{2,3},{3,2},{4,5},{5,4},{6,7},{7,6},{8,9},{9,8},{10,11... | collective-permute-start | bytes 110600 | tf_op jit(solution)/shard_map/ppermute | solution.py:324
  110.3 14.4 %collective-permute-start.38 = (f32[256,768]{1,0:T(8,128)S(1)}, f32[256,768]{1,0:T(8,128)S(1)}, u32[]{:S(2)}, u32[]{:S(2)}) collective-permute-start(f32[256,768]{1,0:T(8,128)S(1)} %get-tuple-element.185), channel_id=1, source_target_pairs={{0,4},{4,0},{8,12},{12,8},{16,20},{20,16},{24,28},{28,24},{1,5},{5... | collective-permute-start | bytes 2359304 | tf_op jit(solution)/shard_map/ppermute | solution.py:324
  114.5 4.9 %collective-permute-start.46 = (f32[8,1152]{1,0:T(8,128)S(1)}, f32[8,1152]{1,0:T(8,128)S(1)}, u32[]{:S(2)}, u32[]{:S(2)}) collective-permute-start(f32[8,1152]{1,0:T(8,128)S(1)} %select_add_fusion.line), channel_id=1, source_target_pairs={{0,2},{1,3},{2,0},{3,1},{4,6},{5,7},{6,4},{7,5},{8,10},{9,11},{10,... | collective-permute-start | bytes 110600 | tf_op jit(solution)/shard_map/ppermute | solution.py:324
  120.0 9.9 %collective-permute-start.51 = (bf16[192,768]{1,0:T(8,128)(2,1)S(1)}, bf16[192,768]{1,0:T(8,128)(2,1)S(1)}, u32[]{:S(2)}, u32[]{:S(2)}) collective-permute-start(bf16[192,768]{1,0:T(8,128)(2,1)S(1)} %get-tuple-element.212), channel_id=1, source_target_pairs={{0,8},{4,12},{8,0},{12,4},{16,24},{20,28},{24,16},{28,20},{1,9},{5... | collective-permute-start | bytes 884744 | tf_op jit(solution)/shard_map/ppermute | solution.py:324
  121.5 9.1 %collective-permute-start.52 = (bf16[192,768]{1,0:T(8,128)(2,1)S(1)}, bf16[192,768]{1,0:T(8,128)(2,1)S(1)}, u32[]{:S(2)}, u32[]{:S(2)}) collective-permute-start(bf16[192,768]{1,0:T(8,128)(2,1)S(1)} %get-tuple-element.218), channel_id=1, source_target_pairs={{0,16},{4,20},{8,24},{12,28},{16,0},{20,4},{24,8},{28,12},{1,17},{... | collective-permute-start | bytes 884744 | tf_op jit(solution)/shard_map/ppermute | solution.py:324
  122.4 10.4 %collective-permute-start.48 = (f32[16,1152]{1,0:T(8,128)S(1)}, f32[16,1152]{1,0:T(8,128)S(1)}, u32[]{:S(2)}, u32[]{:S(2)}) collective-permute-start(f32[16,1152]{1,0:T(8,128)S(1)} %pad_maximum_fusion.13), channel_id=1, source_target_pairs={{0,8},{4,12},{8,0},{12,4},{16,24},{20,28},{24,16},{28,20},{1,9},{5... | collective-permute-start | bytes 221192 | tf_op jit(solution)/shard_map/ppermute | solution.py:324
  123.6 15.7 %collective-permute-start.49 = (bf16[96,1536]{1,0:T(8,128)(2,1)S(1)}, bf16[96,1536]{1,0:T(8,128)(2,1)S(1)}, u32[]{:S(2)}, u32[]{:S(2)}) collective-permute-start(bf16[96,1536]{1,0:T(8,128)(2,1)S(1)} %get-tuple-element.206), channel_id=1, source_target_pairs={{0,2},{1,3},{2,0},{3,1},{4,6},{5,7},{6,4},{7,5},{8,10},{9,11},{10,... | collective-permute-start | bytes 884744 | tf_op jit(solution)/shard_map/ppermute | solution.py:324
  124.9 15.7 %collective-permute-start.39 = (bf16[128,768]{1,0:T(8,128)(2,1)S(1)}, bf16[128,768]{1,0:T(8,128)(2,1)S(1)}, u32[]{:S(2)}, u32[]{:S(2)}) collective-permute-start(bf16[128,768]{1,0:T(8,128)(2,1)S(1)} %get-tuple-element.187), channel_id=1, source_target_pairs={{0,1},{1,0},{2,3},{3,2},{4,5},{5,4},{6,7},{7,6},{8,9},{9,8},{10,11... | collective-permute-start | bytes 589832 | tf_op jit(solution)/shard_map/ppermute | solution.py:324
  130.7 13.2 %collective-permute-start.53 = (bf16[96,768]{1,0:T(8,128)(2,1)S(1)}, bf16[96,768]{1,0:T(8,128)(2,1)S(1)}, u32[]{:S(2)}, u32[]{:S(2)}) collective-permute-start(bf16[96,768]{1,0:T(8,128)(2,1)S(1)} %get-tuple-element.221), channel_id=1, source_target_pairs={{0,16},{4,20},{8,24},{12,28},{16,0},{20,4},{24,8},{28,12},{1,17},{... | collective-permute-start | bytes 442376 | tf_op jit(solution)/shard_map/ppermute | solution.py:324
  131.6 12.3 %collective-permute-start.54 = (bf16[96,768]{1,0:T(8,128)(2,1)S(1)}, bf16[96,768]{1,0:T(8,128)(2,1)S(1)}, u32[]{:S(2)}, u32[]{:S(2)}) collective-permute-start(bf16[96,768]{1,0:T(8,128)(2,1)S(1)} %get-tuple-element.222), channel_id=1, source_target_pairs={{0,8},{4,12},{8,0},{12,4},{16,24},{20,28},{24,16},{28,20},{1,9},{5... | collective-permute-start | bytes 442376 | tf_op jit(solution)/shard_map/ppermute | solution.py:324
  139.3 5.2 %collective-permute-start.50 = (f32[32,1152]{1,0:T(8,128)S(1)}, f32[32,1152]{1,0:T(8,128)S(1)}, u32[]{:S(2)}, u32[]{:S(2)}) collective-permute-start(f32[32,1152]{1,0:T(8,128)S(1)} %pad_maximum_fusion.11), channel_id=1, source_target_pairs={{0,16},{4,20},{8,24},{12,28},{16,0},{20,4},{24,8},{28,12},{1,17},{... | collective-permute-start | bytes 442376 | tf_op jit(solution)/shard_map/ppermute | solution.py:324
  140.6 12.0 %collective-permute-start.30 = (bf16[64,768]{1,0:T(8,128)(2,1)}, bf16[64,768]{1,0:T(8,128)(2,1)S(1)}, u32[]{:S(2)}, u32[]{:S(2)}) collective-permute-start(bf16[64,768]{1,0:T(8,128)(2,1)} %slice.45), channel_id=1, source_target_pairs={{0,2},{1,3},{2,0},{3,1},{4,6},{5,7},{6,4},{7,5},{8,10},{9,11},{10,... | collective-permute-start | bytes 294920 | tf_op jit(solution)/shard_map/ppermute | solution.py:324
  140.9 10.3 %collective-permute-start.40 = (bf16[64,768]{1,0:T(8,128)(2,1)S(1)}, bf16[64,768]{1,0:T(8,128)(2,1)S(1)}, u32[]{:S(2)}, u32[]{:S(2)}) collective-permute-start(bf16[64,768]{1,0:T(8,128)(2,1)S(1)} %get-tuple-element.191), channel_id=1, source_target_pairs={{0,2},{1,3},{2,0},{3,1},{4,6},{5,7},{6,4},{7,5},{8,10},{9,11},{10,... | collective-permute-start | bytes 294920 | tf_op jit(solution)/shard_map/ppermute | solution.py:324
  145.6 4.4 %collective-permute-start.55 = (f32[16,96]{1,0:T(8,128)S(1)}, f32[16,96]{1,0:T(8,128)S(1)}, u32[]{:S(2)}, u32[]{:S(2)}) collective-permute-start(f32[16,96]{1,0:T(8,128)S(1)} %get-tuple-element.229), channel_id=1, source_target_pairs={{0,1},{1,0},{2,3},{3,2},{4,5},{5,4},{6,7},{7,6},{8,9},{9,8},{10,11... | collective-permute-start | bytes 18440 | tf_op jit(solution)/shard_map/ppermute | solution.py:324
  146.9 12.6 %collective-permute-start.58 = (bf16[96,768]{1,0:T(8,128)(2,1)}, bf16[96,768]{1,0:T(8,128)(2,1)S(1)}, u32[]{:S(2)}, u32[]{:S(2)}) collective-permute-start(bf16[96,768]{1,0:T(8,128)(2,1)} %get-tuple-element.237), channel_id=1, source_target_pairs={{0,2},{1,3},{2,0},{3,1},{4,6},{5,7},{6,4},{7,5},{8,10},{9,11},{10,... | collective-permute-start | bytes 442376 | tf_op jit(solution)/shard_map/ppermute | solution.py:324
  150.0 7.6 %collective-permute-start.56 = (f32[16,96]{1,0:T(8,128)S(1)}, f32[16,96]{1,0:T(8,128)S(1)}, u32[]{:S(2)}, u32[]{:S(2)}) collective-permute-start(f32[16,96]{1,0:T(8,128)S(1)} %add.85.near), channel_id=1, source_target_pairs={{0,2},{1,3},{2,0},{3,1},{4,6},{5,7},{6,4},{7,5},{8,10},{9,11},{10,... | collective-permute-start | bytes 18440 | tf_op jit(solution)/shard_map/ppermute | solution.py:324
  (26 other events, 143.7 us)
